TPU v7x, 256 devices: a whole 4x4x8 slice. The times are simulated.
256 devices in a mesh: row: 32 (over x, z_lo, y), col: 8 (over z_hi, core).
Axes of the slice: x: 4, y: 4, z: 8 (z_hi: 4, z_lo: 2; z = z_hi * 2 + z_lo), core: 2. Of those that a mesh axis runs over, the one named last changes fastest.
Arguments:
- root_cov: float32 [6144, 6144], P('row', 'col'), as said below
- structure: int32 [16], replicated, may hold values from 0 to 47
- child_factor: float32 [2048, 4096], P('row', 'col'), may hold values from -0.9 to 0.9
- child_diag: float32 [4096, 4096], P('row', 'col'), may hold values from -6 to 6
Outputs:
- cross_cov: float32 [2048, 4096], P('row', 'col')
- child_cov: float32 [4096, 4096], P('row', 'col')
Inputs may be any that keep to these rules, and one draw needn't show every extreme that they name: root_cov is exactly symmetric and positive definite; its off-diagonal entries are small against its diagonal, which is about 1.5 times the product of a row scale and a column scale.
All inputs are finite; a program needn't handle non-finite values.
Results may differ from a plain program's by a relative error of at most 0.000078.
Values sent between devices are 32-bit elements; how exact they have to be, the bound alone decides.
No kernel may reach another device: no remote copies, remote signals or barrier semaphores. Data moves between devices by JAX's collectives and lax.ppermute only.
A program may use at most 64 MiB of HBM per device.

v0:
```python
import jax
import jax.numpy as jnp
from jax import lax
from jax.sharding import PartitionSpec as P

BLK = 128


def contract_rows(first_mat, second_mat):
    return lax.dot_general(
        first_mat,
        second_mat,
        (((0,), (0,)), ((), ())),
        precision=lax.Precision.HIGHEST,
        preferred_element_type=jnp.float32,
    )


def per_device(root_cov, structure, child_factor, child_diag):
    rows_dev = root_cov.shape[0]
    offsets = lax.iota(jnp.int32, BLK)
    struct_rows = (structure[:, None] * BLK + offsets[None, :]).reshape(-1)
    row_index = lax.axis_index("row")
    global_rows = row_index * rows_dev + lax.iota(jnp.int32, rows_dev)
    tile_index = global_rows // BLK
    rank_count = jnp.sum((structure[None, :] < tile_index[:, None]).astype(jnp.int32), axis=1)
    member = jnp.any(structure[None, :] == tile_index[:, None], axis=1)
    position = rank_count * BLK + global_rows % BLK
    shard_piece = lax.all_gather(root_cov, "col", axis=1, tiled=True)
    local_index = struct_rows
    inside = (local_index >= 0) & (local_index < shard_piece.shape[1])
    taken_rows = jnp.take(shard_piece, jnp.clip(local_index, 0, shard_piece.shape[1] - 1), axis=1)
    picked = jnp.where(inside[None, :], taken_rows, 0.0)
    shard_piece = lax.all_gather(child_factor, "row", axis=0, tiled=True)
    local_index = position
    inside = member & (local_index >= 0) & (local_index < shard_piece.shape[0])
    taken_rows = jnp.take(shard_piece, jnp.clip(local_index, 0, shard_piece.shape[0] - 1), axis=0)
    spread = jnp.where(inside[:, None], taken_rows, 0.0)
    cross_cov = lax.psum_scatter(
        -contract_rows(picked, spread), "row", scatter_dimension=0, tiled=True
    )
    factor_rows = lax.all_gather(child_factor, "col", axis=1, tiled=True)
    child_cov = child_diag + lax.psum_scatter(
        -contract_rows(factor_rows, cross_cov), "row", scatter_dimension=0, tiled=True
    )
    return (cross_cov, child_cov)


def solution(mesh):
    return jax.shard_map(
        per_device,
        mesh=mesh,
        in_specs=(P("row", "col"), P(), P("row", "col"), P("row", "col")),
        out_specs=(P("row", "col"), P("row", "col")),
        check_vma=False,
    )
```

profile of v0, /device:TPU:64, one launch (start us, length us, event | category | flops | bytes accessed | tf_op | source)
XLA Modules:
  0.0 641.2 jit_solution(759094218836384815)
XLA Ops:
  7.2 0.0 copy-start.1
  7.2 0.0 all-gather.6.cloned.1.call-start
  7.2 0.7 all-gather.6.cloned.1.call-update
  7.9 0.0 all-gather.4.cloned.1.call-start
  8.0 2.2 copy.12
  10.2 0.0 all-gather.4.cloned.1.call-update
  10.2 0.0 all-gather.8.cloned.1.call-start
  10.2 0.7 all-gather.8.cloned.1.call-update
  10.9 0.0 reduce-scatter.3.cloned.1.call-start
  11.0 0.0 copy-done.1
  11.0 0.1 convert_reduce_fusion
  11.1 0.1 compare_reduce_fusion
  11.3 0.1 compare_and_fusion
  11.4 0.1 fusion.16
  11.4 0.1 fusion.12
  11.5 160.5 %all-gather.6.cloned.1.call-done = f32[2048,512]{1,0:T(8,128)} async-done(((f32[64,512]{1,0:T(8,128)}), f32[2048,512]{1,0:T(8,128)}) %all-gather.6.cloned.1.call-update) | async-done | bytes 4194320 | tf_op jit(solution)/shard_map/all_gather | solution.py:34
  172.1 3.2 gather_fusion.1
  175.3 67.9 %all-gather.4.cloned.1.call-done = f32[192,6144]{0,1:T(8,128)} async-done(((f32[192,768]{0,1:T(8,128)}), f32[192,6144]{0,1:T(8,128)}) %all-gather.4.cloned.1.call-update) | async-done | bytes 4718608 | tf_op jit(solution)/shard_map/all_gather | solution.py:29
  243.2 9.4 %gather_fusion = f32[2048,192]{1,0:T(8,128)S(1)} fusion(f32[192,6144]{0,1:T(8,128)} %all-gather.4.cloned.1.call-done, s32[2048]{0:T(1024)S(1)} %broadcast_clamp_fusion), kind=kCustom, calls=%fused_computation | custom fusion | bytes 3153920 | tf_op jit(solution)/shard_map/jit(_take)/gather | solution.py:32
  252.7 5.3 convolution_negate_fusion
  257.9 0.0 reduce-scatter.3.cloned.1.call-update
  258.0 0.0 reduce-scatter.5.cloned.1.call-start
  258.0 14.9 %all-gather.8.cloned.1.call-done = f32[64,4096]{1,0:T(8,128)} async-done(((f32[64,512]{1,0:T(8,128)}), f32[64,4096]{1,0:T(8,128)}) %all-gather.8.cloned.1.call-update) | async-done | bytes 1048592 | tf_op jit(solution)/shard_map/all_gather | solution.py:42
  272.9 173.4 %reduce-scatter.3.cloned.1.call-done = f32[64,512]{1,0:T(8,128)} async-done(((f32[2048,512]{1,0:T(8,128)}), f32[64,512]{1,0:T(8,128)}) %reduce-scatter.3.cloned.1.call-update) | async-done | bytes 131088 | tf_op jit(solution)/shard_map/reduce_scatter | solution.py:39
  446.4 10.0 %negate_bitcast_fusion = f32[4096,512]{0,1:T(8,128)} fusion(f32[64,512]{1,0:T(8,128)} %reduce-scatter.3.cloned.1.call-done, f32[64,4096]{1,0:T(8,128)} %all-gather.8.cloned.1.call-done), kind=kOutput, calls=%fused_computation.2 | convolution fusion | flops 1612709888 | bytes 9568256 | tf_op jit(solution)/shard_map/dot_general | solution.py:10
  456.4 0.0 copy-start
  456.4 0.0 reduce-scatter.5.cloned.1.call-update
  456.5 0.9 copy-done
  457.4 0.1 copy.13
  457.5 175.3 %reduce-scatter.5.cloned.1.call-done = f32[128,512]{0,1:T(8,128)} async-done(((f32[4096,512]{0,1:T(8,128)}), f32[128,512]{0,1:T(8,128)}) %reduce-scatter.5.cloned.1.call-update) | async-done | bytes 262160 | tf_op jit(solution)/shard_map/reduce_scatter | solution.py:43
  632.9 1.0 add.152
  633.8 0.8 copy.14
  (9 shorter events, 0.1 us)
Async XLA Ops:
  7.2 3.8 copy-start.1
  7.2 164.9 %all-gather.6.cloned.1.call-start = ((), (), s32[]{:S(2)}) async-start(), calls=%async_computation.3 | async-start | bytes 4325376 | tf_op jit(solution)/shard_map/all_gather | solution.py:34
  7.9 235.3 %all-gather.4.cloned.1.call-start = ((), (), s32[]{:S(2)}) async-start(), calls=%async_computation.2 | async-start | bytes 7077888 | tf_op jit(solution)/shard_map/all_gather | solution.py:29
  10.2 262.8 %all-gather.8.cloned.1.call-start = ((), (), s32[]{:S(2)}) async-start(), calls=%async_computation.5 | async-start | bytes 1179648 | tf_op jit(solution)/shard_map/all_gather | solution.py:42
  10.9 435.5 %reduce-scatter.3.cloned.1.call-start = ((), (), s32[]{:S(2)}) async-start(), calls=%async_computation.4 | async-start | bytes 4325376 | tf_op jit(solution)/shard_map/reduce_scatter | solution.py:39
  258.0 374.9 %reduce-scatter.5.cloned.1.call-start = ((), (), s32[]{:S(2)}) async-start(), calls=%async_computation.6 | async-start | bytes 8650752 | tf_op jit(solution)/shard_map/reduce_scatter | solution.py:43
  456.4 0.9 copy-start
Sparse Core Ops, SparseCore 0:
  9.8 162.2 all-gather.5
  173.9 69.2 all-gather.3
  245.1 27.8 all-gather.7
  275.9 170.4 reduce-scatter.2
  456.6 176.2 reduce-scatter.4
where the time goes:
time: 641 us
  waiting for transfers between devices  594 us (93%)
  local copies, waits for them, and re-layouts  16.8 us (3%)
  matrix products  15.3 us (2%)
  between operations  13.9 us (2%)
    reduce_scatter x1, waiting for transfers between devices, per_device(): lax.psum_scatter(-contract_rows(factor_rows, cross_cov), 'row', scatter_d...  175 us
    reduce_scatter x1, waiting for transfers between devices, per_device(): lax.psum_scatter(-contract_rows(picked, spread), 'row', scatter_dimension...  173 us
    all_gather x1, waiting for transfers between devices, per_device(): shard_piece = lax.all_gather(child_factor, 'row', axis=0, tiled=True)  161 us
    all_gather x1, waiting for transfers between devices, per_device(): shard_piece = lax.all_gather(root_cov, 'col', axis=1, tiled=True)  67.9 us
    dot_general x2, matrix products, contract_rows(): lax.dot_general(first_mat, second_mat, (((0,), (0,)), ((), ())), precisio...  15.3 us
    all_gather x1, waiting for transfers between devices, per_device(): factor_rows = lax.all_gather(child_factor, 'col', axis=1, tiled=True)  14.9 us
  transfers between devices with their start and end apart: 5, of which 5 were waited for; matrix products, arithmetic and copies ran while one was open for 3% of the time, Pallas kernels for 0%

commit v1 on v0

v1 whole, which is shorter than its diff:
```python
import jax
import jax.numpy as jnp
from jax import lax
from jax.experimental import pallas as pl
from jax.experimental.pallas import tpu as pltpu
from jax.sharding import Mesh, PartitionSpec as P

BLK = 128
AXES = ("x", "zl", "y", "zh", "core")
SIZES = (4, 2, 4, 4, 2)
ROWS = ("x", "zl", "y")
COLS = ("zh", "core")
GROUP = ("x", "zl")
HI = lax.Precision.HIGHEST


def spread_kernel(table, wide, out):
    for p in range(16):
        owner = table[p]
        column = pl.multiple_of(table[16 + p], BLK)
        for y in range(4):
            row = pl.multiple_of(table[32 + y], 8)
            out[(p // 2) * 4 + y, :, (p % 2) * BLK:(p % 2 + 1) * BLK] = wide[
                owner, pl.ds(row, 8), pl.ds(column, BLK)
            ]


def pick_kernel(table, pieces, out):
    for j in range(8):
        out[j] = pieces[table[j]]


def contract(first, second):
    return lax.dot_general(
        first, second, (((0,), (0,)), ((), ())), precision=HI, preferred_element_type=jnp.float32
    )


def vmem():
    return pl.BlockSpec(memory_space=pltpu.VMEM)


def smem():
    return pl.BlockSpec(memory_space=pltpu.SMEM)


def gather_group(block):
    copies = jnp.broadcast_to(block[None], (8,) + block.shape)
    return lax.all_to_all(copies, GROUP, 0, 0).reshape(-1, block.shape[1])


def per_device(root_cov, structure, child_factor, child_diag):
    y = lax.axis_index("y")
    row_dev = (lax.axis_index("x") * 2 + lax.axis_index("zl")) * 4 + y

    factor_mine = lax.all_gather(child_factor, GROUP, axis=0, tiled=True)
    turn = []
    for a in range(8):
        for b in range(4):
            for c in range(8):
                turn.append(((a * 4 + b) * 8 + c, (c * 4 + b) * 8 + a))
    turned = lax.ppermute(child_factor, AXES, turn)

    halves = row_dev * 3 + lax.iota(jnp.int32, 3)
    tiles = halves // 2
    position = jnp.sum((structure[None, :] < tiles[:, None]).astype(jnp.int32), axis=1)
    member = jnp.any(structure[None, :] == tiles[:, None], axis=1)
    kind = jnp.where(member, (2 * position + halves % 2) % 4, -1)
    classes = lax.iota(jnp.int32, 4)
    slot = jnp.sum(
        jnp.where(kind[None, :] == classes[:, None], lax.iota(jnp.int32, 3)[None, :], 0), axis=1
    )
    table = jnp.concatenate([structure // 6, structure % 6 * BLK, slot * 8])

    shares = root_cov.reshape(3, 8, 8, 768).transpose(1, 0, 2, 3).reshape(8, 24, 768)
    wide = lax.all_to_all(shares, COLS, 0, 0)
    wide, turned = lax.optimization_barrier((wide, turned))
    factor_turned = lax.all_gather(turned, COLS, axis=0, tiled=True)
    sends = pl.pallas_call(
        spread_kernel,
        out_shape=jax.ShapeDtypeStruct((32, 8, 256), jnp.float32),
        in_specs=[smem(), vmem()],
        out_specs=vmem(),
    )(table, wide)
    pieces = lax.all_to_all(sends, ROWS, 0, 0)
    steps = 2 * lax.iota(jnp.int32, 8) + y // 2
    sources = (2 * jnp.take(structure, steps) + y % 2) // 3
    piece = pl.pallas_call(
        pick_kernel,
        out_shape=jax.ShapeDtypeStruct((8, 8, 256), jnp.float32),
        in_specs=[smem(), vmem()],
        out_specs=vmem(),
    )(sources, pieces)
    parts = [piece]
    zh = lax.axis_index("zh")
    for k in range(1, 4):
        parts.append(lax.ppermute(piece, "zh", [(i, (i + k) % 4) for i in range(4)]))
    near = jnp.stack(parts)
    far = lax.ppermute(near, "core", [(0, 1), (1, 0)])
    core = lax.axis_index("core")
    first = jnp.where(core == 0, near, far)
    second = jnp.where(core == 0, far, near)
    both = jnp.stack([first, second], axis=1)
    order = (zh - lax.iota(jnp.int32, 4)) % 4
    both = jnp.take(both, order, axis=0)
    brick = both.reshape(8, 8, 8, 256).transpose(1, 0, 2, 3).reshape(512, 256)

    share = contract(brick, factor_mine)
    got = lax.all_to_all(share.reshape(4, 64, 512), "y", 0, 0)
    cross = -(got[0] + got[1] + got[2] + got[3])
    cross_group = gather_group(cross)
    share = contract(factor_turned, cross_group)
    got = lax.all_to_all(share.reshape(4, 128, 512), "y", 0, 0)
    child = child_diag - (got[0] + got[1] + got[2] + got[3])
    return cross, child


def solution(mesh):
    fine = Mesh(mesh.devices.reshape(SIZES), AXES)
    spec = P(ROWS, COLS)
    return jax.shard_map(
        per_device,
        mesh=fine,
        in_specs=(spec, P(), spec, spec),
        out_specs=(spec, spec),
        check_vma=False,
    )
```

time: 641 us -> 157 us (0.24)
  the two profiles are of different devices: /device:TPU:64 before, /device:TPU:1 now
where the time goes in v1:
time: 157 us; the launch traced here: 156 us
  waiting for transfers between devices  65.3 us (42%)
  starting transfers between devices  35.7 us (23%)
  blocking collectives  18.7 us (12%)
  between operations  15.7 us (10%)
  local copies, waits for them, and re-layouts  8.4 us (5%)
  matrix products  4.94 us (3%)
  other arithmetic  3.7 us (2%)
  Pallas kernels  3.48 us (2%)
    all_to_all x1, waiting for transfers between devices, per_device(): wide = lax.all_to_all(shares, COLS, 0, 0)  21.5 us
    all_to_all x1, blocking collectives, per_device(): got = lax.all_to_all(share.reshape(4, 128, 512), 'y', 0, 0)  18.7 us
    all_gather x1, waiting for transfers between devices, per_device(): factor_turned = lax.all_gather(turned, COLS, axis=0, tiled=True)  18.2 us
    all_to_all x1, waiting for transfers between devices, per_device(): got = lax.all_to_all(share.reshape(4, 64, 512), 'y', 0, 0)  8.62 us
    all_to_all x1, waiting for transfers between devices, per_device(): pieces = lax.all_to_all(sends, ROWS, 0, 0)  8.52 us
    all_to_all x1, starting transfers between devices, per_device(): wide = lax.all_to_all(shares, COLS, 0, 0)  8.32 us
    all_to_all x1, starting transfers between devices, per_device(): pieces = lax.all_to_all(sends, ROWS, 0, 0)  7.68 us
    ppermute x3, waiting for transfers between devices, per_device(): lax.ppermute(piece, 'zh', [(i, (i + k) % 4) for i in range(4)])  5.28 us
  transfers between devices with their start and end apart: 11, of which 9 were waited for; matrix products, arithmetic and copies ran while one was open for 6% of the time, Pallas kernels for 2%

profile of v1, /device:TPU:1, one launch (start us, length us, event | category | flops | bytes accessed | tf_op | source)
XLA Modules:
  0.0 156.0 jit_solution(8455088100191387907)
XLA Ops:
  8.0 0.0 all-gather.3.cloned.1.call-start
  8.0 4.9 %collective-permute-start = (f32[64,512]{1,0:T(8,128)}, f32[64,512]{1,0:T(8,128)S(1)}, u32[]{:S(2)}, u32[]{:S(2)}) collective-permute-start(f32[64,512]{1,0:T(8,128)} %param.6), channel_id=1, source_target_pairs={{0,0},{1,32},{2,64},{3,96},{4,128},{5,160},{6,192},{7,224},{8,8},{... | collective-permute-start | bytes 393224 | tf_op jit(solution)/shard_map/ppermute | solution.py:62
  13.0 0.0 all-gather.3.cloned.1.call-update
  13.0 1.9 %copy.22 = f32[3,8,8,768]{3,2,0,1:T(8,128)} copy(f32[3,8,8,768]{3,2,1,0:T(8,128)} %bitcast.49) | data formatting | bytes 1179648 | tf_op jit(solution)/shard_map/reshape | solution.py:75
  15.0 8.3 %all-to-all-start = ((f32[8,24,768]{2,1,0:T(8,128)}), f32[8,24,768]{2,1,0:T(8,128)S(1)}, u32[]{:S(2)}, u32[]{:S(2)}) async-start(f32[8,24,768]{2,1,0:T(8,128)} %bitcast.43), calls=%async_computation | async-start | bytes 1179648 | tf_op jit(solution)/shard_map/all_to_all | solution.py:76
  23.3 0.6 copy-done
  23.9 0.2 compare_reduce_fusion
  24.1 0.2 convert_reduce_fusion
  24.3 0.1 select_reduce_fusion
  24.5 0.6 pad_add_fusion.table
  25.1 21.5 %all-to-all-done.wide = f32[8,24,768]{2,1,0:T(8,128)S(1)} async-done(((f32[8,24,768]{2,1,0:T(8,128)}), f32[8,24,768]{2,1,0:T(8,128)S(1)}, u32[]{:S(2)}, u32[]{:S(2)}) %all-to-all-start) | async-done | bytes 589856 | tf_op jit(solution)/shard_map/all_to_all | solution.py:76
  46.6 0.8 copy-done.1
  47.4 1.9 %shard_map.59 = f32[32,8,256]{2,1,0:T(8,128)} custom-call(s32[36]{0:T(128)} %pad_add_fusion.table, f32[8,24,768]{2,1,0:T(8,128)} %copy-done.1), custom_call_target="tpu_custom_call" | custom-call | tf_op jit(solution)/shard_map/pallas_call | solution.py:79
  49.3 7.7 %all-to-all-start.1 = ((f32[32,8,256]{2,1,0:T(8,128)}), f32[32,8,256]{2,1,0:T(8,128)S(1)}, u32[]{:S(2)}, u32[]{:S(2)}) async-start(f32[32,8,256]{2,1,0:T(8,128)} %shard_map.59), calls=%async_computation.1 | async-start | bytes 524288 | tf_op jit(solution)/shard_map/all_to_all | solution.py:85
  57.0 0.6 gather_fusion
  57.7 0.6 and_select_fusion.6.table
  58.2 8.5 %all-to-all-done.1.pieces = f32[32,8,256]{2,1,0:T(8,128)S(1)} async-done(((f32[32,8,256]{2,1,0:T(8,128)}), f32[32,8,256]{2,1,0:T(8,128)S(1)}, u32[]{:S(2)}, u32[]{:S(2)}) %all-to-all-start.1) | async-done | bytes 262176 | tf_op jit(solution)/shard_map/all_to_all | solution.py:85
  66.8 0.7 copy-done.2
  67.5 1.6 %shard_map.60 = f32[8,8,256]{2,1,0:T(8,128)} custom-call(s32[8]{0:T(128)} %and_select_fusion.6.table, f32[32,8,256]{2,1,0:T(8,128)} %copy-done.2), custom_call_target="tpu_custom_call" | custom-call | tf_op jit(solution)/shard_map/pallas_call | solution.py:88
  69.0 0.1 collective-permute-start.1
  69.1 1.7 %collective-permute-start.2 = (f32[8,8,256]{2,1,0:T(8,128)}, f32[8,8,256]{2,1,0:T(8,128)S(1)}, u32[]{:S(2)}, u32[]{:S(2)}) collective-permute-start(f32[8,8,256]{2,1,0:T(8,128)} %shard_map.60), channel_id=1, source_target_pairs={{0,4},{2,6},{4,0},{6,2},{1,5},{3,7},{5,1},{7,3},{8,12},{10,14},{12... | collective-permute-start | bytes 196616 | tf_op jit(solution)/shard_map/ppermute | solution.py:97
  70.9 1.8 %collective-permute-start.3 = (f32[8,8,256]{2,1,0:T(8,128)}, f32[8,8,256]{2,1,0:T(8,128)S(1)}, u32[]{:S(2)}, u32[]{:S(2)}) collective-permute-start(f32[8,8,256]{2,1,0:T(8,128)} %shard_map.60), channel_id=1, source_target_pairs={{0,6},{2,0},{4,2},{6,4},{1,7},{3,1},{5,3},{7,5},{8,14},{10,8},{12,... | collective-permute-start | bytes 196616 | tf_op jit(solution)/shard_map/ppermute | solution.py:97
  72.6 1.9 %collective-permute-done.1 = f32[8,8,256]{2,1,0:T(8,128)S(1)} collective-permute-done((f32[8,8,256]{2,1,0:T(8,128)}, f32[8,8,256]{2,1,0:T(8,128)S(1)}, u32[]{:S(2)}, u32[]{:S(2)}) %collective-permute-start.1) | collective-permute-done | bytes 65568 | tf_op jit(solution)/shard_map/ppermute | solution.py:97
  74.5 2.5 %collective-permute-done.2 = f32[8,8,256]{2,1,0:T(8,128)S(1)} collective-permute-done((f32[8,8,256]{2,1,0:T(8,128)}, f32[8,8,256]{2,1,0:T(8,128)S(1)}, u32[]{:S(2)}, u32[]{:S(2)}) %collective-permute-start.2) | collective-permute-done | bytes 65568 | tf_op jit(solution)/shard_map/ppermute | solution.py:97
  77.0 0.9 collective-permute-done.3
  77.9 0.9 pad_maximum_fusion.1
  78.8 4.1 %collective-permute-start.4 = (f32[4,8,8,256]{3,2,1,0:T(8,128)S(1)}, f32[4,8,8,256]{3,2,1,0:T(8,128)S(1)}, u32[]{:S(2)}, u32[]{:S(2)}) collective-permute-start(f32[4,8,8,256]{3,2,1,0:T(8,128)S(1)} %pad_maximum_fusion.1), channel_id=1, source_target_pairs={{0,1},{1,0},{2,3},{3,2},{4,5},{5,4},{6,7},{7,6},{8,9},{9,8},{10,11... | collective-permute-start | bytes 786440 | tf_op jit(solution)/shard_map/ppermute | solution.py:99
  83.0 0.1 broadcast_in_dim.43
  83.0 0.1 broadcast_in_dim.44
  83.2 1.0 collective-permute-done.4
  84.2 0.6 gather_fusion.1
  84.8 0.1 copy_select_fusion
  84.9 0.2 copy.18
  85.1 0.0 all-gather.3.cloned.1.call-done
  85.1 3.1 %fusion = f32[4,64,512]{2,1,0:T(8,128)} fusion(f32[4,64,512]{2,1,0:T(8,128)S(1)} %bitcast.47, f32[512,512]{1,0:T(8,128)} %all-gather.3.cloned.1.call-done), kind=kOutput, calls=%fused_computation.2 | convolution fusion | flops 805306368 | bytes 2097152 | tf_op jit(solution)/shard_map/dot_general | solution.py:34
  88.2 3.5 %all-to-all-start.2 = ((f32[4,64,512]{2,1,0:T(8,128)}), f32[4,64,512]{2,1,0:T(8,128)S(1)}, u32[]{:S(2)}, u32[]{:S(2)}) async-start(f32[4,64,512]{2,1,0:T(8,128)} %fusion), calls=%async_computation.2 | async-start | bytes 1048576 | tf_op jit(solution)/shard_map/all_to_all | solution.py:109
  91.7 0.0 all-gather.5.cloned.1.call-start
  91.8 0.5 all-gather.5.cloned.1.call-update
  92.3 8.6 %all-to-all-done.2 = f32[4,64,512]{2,1,0:T(8,128)S(1)} async-done(((f32[4,64,512]{2,1,0:T(8,128)}), f32[4,64,512]{2,1,0:T(8,128)S(1)}, u32[]{:S(2)}, u32[]{:S(2)}) %all-to-all-start.2) | async-done | bytes 524320 | tf_op jit(solution)/shard_map/all_to_all | solution.py:109
  100.9 0.0 copy-start.4
  101.0 1.1 broadcast_in_dim.49
  102.1 3.6 %all-to-all-start.3 = ((f32[8,64,512]{2,1,0:T(8,128)}), f32[8,64,512]{2,1,0:T(8,128)S(1)}, u32[]{:S(2)}, u32[]{:S(2)}) async-start(f32[8,64,512]{2,1,0:T(8,128)} %broadcast_in_dim.49), calls=%async_computation.3 | async-start | bytes 2097152 | tf_op jit(solution)/shard_map/all_to_all | solution.py:49
  105.6 18.2 %all-gather.5.cloned.1.call-done = f32[512,512]{1,0:T(8,128)} async-done(((f32[64,512]{1,0:T(8,128)}), f32[512,512]{1,0:T(8,128)}) %all-gather.5.cloned.1.call-update) | async-done | bytes 1048592 | tf_op jit(solution)/shard_map/all_gather | solution.py:78
  123.9 1.6 copy.19
  125.4 1.7 %all-to-all-done.3 = f32[8,64,512]{2,1,0:T(8,128)S(1)} async-done(((f32[8,64,512]{2,1,0:T(8,128)}), f32[8,64,512]{2,1,0:T(8,128)S(1)}, u32[]{:S(2)}, u32[]{:S(2)}) %all-to-all-start.3) | async-done | bytes 1048608 | tf_op jit(solution)/shard_map/all_to_all | solution.py:49
  127.1 1.8 %fusion.14 = f32[4,128,512]{2,1,0:T(8,128)S(1)} fusion(f32[4,128,512]{2,1,0:T(8,128)S(1)} %bitcast.45, f32[512,512,1]{1,0,2:T(8,128)S(1)} %bitcast.44), kind=kOutput, calls=%fused_computation.60 | convolution fusion | flops 1610612736 | bytes 3145728 | tf_op jit(solution)/shard_map/dot_general | solution.py:34
  129.0 18.7 %all_to_all.25 = f32[4,128,512]{2,1,0:T(8,128)S(1)} all-to-all(f32[4,128,512]{2,1,0:T(8,128)S(1)} %fusion.14), channel_id=1, replica_groups=mesh['x'=4,'zl'=2,'y'=4,'zh'=4,'core'=2] {'y'}, dimensions={0} | all-to-all | bytes 2097152 | tf_op jit(solution)/shard_map/all_to_all | solution.py:113
  147.7 0.8 fusion.3
  (23 shorter events, 0.2 us)
Async XLA Ops:
  8.0 77.1 %all-gather.3.cloned.1.call-start = ((), (), s32[]{:S(2)}) async-start(), calls=%async_computation.5 | async-start | bytes 1179648 | tf_op jit(solution)/shard_map/all_gather | solution.py:56
  8.0 17.0 %collective-permute-start = (f32[64,512]{1,0:T(8,128)}, f32[64,512]{1,0:T(8,128)S(1)}, u32[]{:S(2)}, u32[]{:S(2)}) collective-permute-start(f32[64,512]{1,0:T(8,128)} %param.6), channel_id=1, source_target_pairs={{0,0},{1,32},{2,64},{3,96},{4,128},{5,160},{6,192},{7,224},{8,8},{... | collective-permute-start | bytes 393224 | tf_op jit(solution)/shard_map/ppermute | solution.py:62
  15.0 31.6 %all-to-all-start = ((f32[8,24,768]{2,1,0:T(8,128)}), f32[8,24,768]{2,1,0:T(8,128)S(1)}, u32[]{:S(2)}, u32[]{:S(2)}) async-start(f32[8,24,768]{2,1,0:T(8,128)} %bitcast.43), calls=%async_computation | async-start | bytes 1179648 | tf_op jit(solution)/shard_map/all_to_all | solution.py:76
  23.3 0.7 copy-start
  25.1 24.2 %copy-start.6 = (f32[64,512]{1,0:T(8,128)}, f32[64,512]{1,0:T(8,128)S(1)}, u32[]{:S(2)}) copy-start(f32[64,512]{1,0:T(8,128)S(1)} %collective-permute-done) | copy-start | bytes 393220
  46.6 0.8 copy-start.1
  49.3 17.5 %all-to-all-start.1 = ((f32[32,8,256]{2,1,0:T(8,128)}), f32[32,8,256]{2,1,0:T(8,128)S(1)}, u32[]{:S(2)}, u32[]{:S(2)}) async-start(f32[32,8,256]{2,1,0:T(8,128)} %shard_map.59), calls=%async_computation.1 | async-start | bytes 524288 | tf_op jit(solution)/shard_map/all_to_all | solution.py:85
  66.7 0.7 copy-start.2
  69.0 5.4 %collective-permute-start.1 = (f32[8,8,256]{2,1,0:T(8,128)}, f32[8,8,256]{2,1,0:T(8,128)S(1)}, u32[]{:S(2)}, u32[]{:S(2)}) collective-permute-start(f32[8,8,256]{2,1,0:T(8,128)} %shard_map.60), channel_id=1, source_target_pairs={{0,2},{2,4},{4,6},{6,0},{1,3},{3,5},{5,7},{7,1},{8,10},{10,12},{12... | collective-permute-start | bytes 196616 | tf_op jit(solution)/shard_map/ppermute | solution.py:97
  69.1 7.9 %collective-permute-start.2 = (f32[8,8,256]{2,1,0:T(8,128)}, f32[8,8,256]{2,1,0:T(8,128)S(1)}, u32[]{:S(2)}, u32[]{:S(2)}) collective-permute-start(f32[8,8,256]{2,1,0:T(8,128)} %shard_map.60), channel_id=1, source_target_pairs={{0,4},{2,6},{4,0},{6,2},{1,5},{3,7},{5,1},{7,3},{8,12},{10,14},{12... | collective-permute-start | bytes 196616 | tf_op jit(solution)/shard_map/ppermute | solution.py:97
  70.9 7.0 %collective-permute-start.3 = (f32[8,8,256]{2,1,0:T(8,128)}, f32[8,8,256]{2,1,0:T(8,128)S(1)}, u32[]{:S(2)}, u32[]{:S(2)}) collective-permute-start(f32[8,8,256]{2,1,0:T(8,128)} %shard_map.60), channel_id=1, source_target_pairs={{0,6},{2,0},{4,2},{6,4},{1,7},{3,1},{5,3},{7,5},{8,14},{10,8},{12,... | collective-permute-start | bytes 196616 | tf_op jit(solution)/shard_map/ppermute | solution.py:97
  77.9 6.2 %copy-start.3 = (f32[8,8,256]{2,1,0:T(8,128)S(1)}, f32[8,8,256]{2,1,0:T(8,128)}, u32[]{:S(2)}) copy-start(f32[8,8,256]{2,1,0:T(8,128)} %shard_map.60) | copy-start | bytes 196612
  78.8 5.3 %collective-permute-start.4 = (f32[4,8,8,256]{3,2,1,0:T(8,128)S(1)}, f32[4,8,8,256]{3,2,1,0:T(8,128)S(1)}, u32[]{:S(2)}, u32[]{:S(2)}) collective-permute-start(f32[4,8,8,256]{3,2,1,0:T(8,128)S(1)} %pad_maximum_fusion.1), channel_id=1, source_target_pairs={{0,1},{1,0},{2,3},{3,2},{4,5},{5,4},{6,7},{7,6},{8,9},{9,8},{10,11... | collective-permute-start | bytes 786440 | tf_op jit(solution)/shard_map/ppermute | solution.py:99
  88.2 12.7 %all-to-all-start.2 = ((f32[4,64,512]{2,1,0:T(8,128)}), f32[4,64,512]{2,1,0:T(8,128)S(1)}, u32[]{:S(2)}, u32[]{:S(2)}) async-start(f32[4,64,512]{2,1,0:T(8,128)} %fusion), calls=%async_computation.2 | async-start | bytes 1048576 | tf_op jit(solution)/shard_map/all_to_all | solution.py:109
  91.7 32.2 %all-gather.5.cloned.1.call-start = ((), (), s32[]{:S(2)}) async-start(), calls=%async_computation.6 | async-start | bytes 1179648 | tf_op jit(solution)/shard_map/all_gather | solution.py:78
  100.9 1.1 copy-start.4
  102.1 25.0 %all-to-all-start.3 = ((f32[8,64,512]{2,1,0:T(8,128)}), f32[8,64,512]{2,1,0:T(8,128)S(1)}, u32[]{:S(2)}, u32[]{:S(2)}) async-start(f32[8,64,512]{2,1,0:T(8,128)} %broadcast_in_dim.49), calls=%async_computation.3 | async-start | bytes 2097152 | tf_op jit(solution)/shard_map/all_to_all | solution.py:49
  129.0 18.7 %copy-start.5 = (f32[128,512]{1,0:T(8,128)S(1)}, f32[128,512]{1,0:T(8,128)}, u32[]{:S(2)}) copy-start(f32[128,512]{1,0:T(8,128)} %param.7) | copy-start | bytes 786436
Sparse Core Ops, SparseCore 0:
  13.1 50.9 all-gather.2
Sparse Core Ops, SparseCore 1:
  94.0 29.8 all-gather.4

commit v2 on v1

v2 whole, which is shorter than its diff:
```python
import jax
import jax.numpy as jnp
from jax import lax
from jax.experimental import pallas as pl
from jax.experimental.pallas import tpu as pltpu
from jax.sharding import Mesh, PartitionSpec as P

BLK = 128
AXES = ("x", "zl", "y", "zh", "core")
SIZES = (4, 2, 4, 4, 2)
ROWS = ("x", "zl", "y")
COLS = ("zh", "core")
GROUP = ("x", "zl")
SWAP = [(0, 1), (1, 0)]
HI = lax.Precision.HIGHEST


def spread_kernel(table, keep, got, out):
    for p in range(16):
        source = table[p]
        column = pl.multiple_of(table[16 + p], BLK)
        own = table[32 + p] == 1
        for y in range(4):
            slot = table[48 + y]
            here = keep[source, slot, :, pl.ds(column, BLK)]
            there = got[source, slot, :, pl.ds(column, BLK)]
            out[(p // 2) * 4 + y, :, (p % 2) * BLK:(p % 2 + 1) * BLK] = jnp.where(own, here, there)


def pick_kernel(table, pieces, out):
    for j in range(8):
        out[j] = pieces[table[j]]


def contract(first, second):
    return lax.dot_general(
        first, second, (((0,), (0,)), ((), ())), precision=HI, preferred_element_type=jnp.float32
    )


def vmem():
    return pl.BlockSpec(memory_space=pltpu.VMEM)


def smem():
    return pl.BlockSpec(memory_space=pltpu.SMEM)


def shift(block, axis, k):
    return lax.ppermute(block, axis, [(i, (i + k) % 4) for i in range(4)])


def in_order(slots, index):
    return jnp.take(slots, (index - lax.iota(jnp.int32, 4)) % 4, axis=0)


def gather_cols_finish(parts, zh, core):
    near = jnp.stack(parts)
    far = lax.ppermute(near, "core", SWAP)
    first = jnp.where(core == 0, near, far)
    second = jnp.where(core == 0, far, near)
    both = in_order(jnp.stack([first, second], axis=1), zh)
    return both.reshape((8,) + both.shape[2:])


def per_device(root_cov, structure, child_factor, child_diag):
    x, zl, y = lax.axis_index("x"), lax.axis_index("zl"), lax.axis_index("y")
    zh, core = lax.axis_index("zh"), lax.axis_index("core")
    row_dev = (x * 2 + zl) * 4 + y

    halves = row_dev * 3 + lax.iota(jnp.int32, 3)
    tiles = halves // 2
    position = jnp.sum((structure[None, :] < tiles[:, None]).astype(jnp.int32), axis=1)
    member = jnp.any(structure[None, :] == tiles[:, None], axis=1)
    kind = jnp.where(member, (2 * position + halves % 2) % 4, -1)
    classes = lax.iota(jnp.int32, 4)
    slot = jnp.sum(
        jnp.where(kind[None, :] == classes[:, None], lax.iota(jnp.int32, 3)[None, :], 0), axis=1
    )
    owner = structure // 6
    table = jnp.concatenate([
        (zh - owner // 2) % 4,
        structure % 6 * BLK,
        (owner % 2 == core).astype(jnp.int32),
        slot,
    ])
    steps = 2 * lax.iota(jnp.int32, 8) + y // 2
    sources = (2 * jnp.take(structure, steps) + y % 2) // 3

    shares = root_cov.reshape(3, 4, 16, 768)
    mine = [lax.dynamic_index_in_dim(shares, (zh + k) % 4, 1, keepdims=False) for k in range(4)]
    landed = [mine[0]] + [shift(mine[k], "zh", k) for k in (1, 2, 3)]
    factor_pair = lax.ppermute(child_factor, "zl", SWAP)
    landed = jnp.stack(landed).reshape(4, 3, 2, 8, 768)
    keep = lax.dynamic_index_in_dim(landed, core, 2, keepdims=False)
    give = lax.dynamic_index_in_dim(landed, 1 - core, 2, keepdims=False)
    got = lax.ppermute(give, "core", SWAP)
    sends = pl.pallas_call(
        spread_kernel,
        out_shape=jax.ShapeDtypeStruct((32, 8, 256), jnp.float32),
        in_specs=[smem(), vmem(), vmem()],
        out_specs=vmem(),
    )(table, keep, got)

    sends, factor_pair, factor = lax.optimization_barrier((sends, factor_pair, child_factor))
    pieces = lax.all_to_all(sends, ROWS, 0, 0)
    pair = jnp.stack(
        [jnp.where(zl == 0, factor, factor_pair), jnp.where(zl == 0, factor_pair, factor)]
    )
    factor_x = [pair] + [shift(pair, "x", k) for k in (1, 2, 3)]
    turn = []
    for a in range(8):
        for b in range(4):
            for c in range(8):
                turn.append(((a * 4 + b) * 8 + c, (c * 4 + b) * 8 + a))
    turned = lax.ppermute(factor, AXES, turn)
    pieces, factor_x, turned = lax.optimization_barrier((pieces, factor_x, turned))

    piece = pl.pallas_call(
        pick_kernel,
        out_shape=jax.ShapeDtypeStruct((8, 8, 256), jnp.float32),
        in_specs=[smem(), vmem()],
        out_specs=vmem(),
    )(sources, pieces)
    brick = gather_cols_finish([piece] + [shift(piece, "zh", k) for k in (1, 2, 3)], zh, core)
    brick = brick.transpose(1, 0, 2, 3).reshape(512, 256)
    factor_mine = in_order(jnp.stack(factor_x), x).reshape(512, 512)

    share = contract(brick, factor_mine)
    share, turned = lax.optimization_barrier((share, turned))
    got = lax.all_to_all(share.reshape(4, 64, 512), "y", 0, 0)
    turned_parts = [turned] + [shift(turned, "zh", k) for k in (1, 2, 3)]
    got, turned_parts = lax.optimization_barrier((got, turned_parts))
    cross = -(got[0] + got[1] + got[2] + got[3])
    copies = jnp.broadcast_to(cross[None], (8, 64, 512))
    cross_group = lax.all_to_all(copies, GROUP, 0, 0).reshape(512, 512)
    factor_turned = gather_cols_finish(turned_parts, zh, core).reshape(512, 512)
    share = contract(factor_turned, cross_group)
    got = lax.all_to_all(share.reshape(4, 128, 512), "y", 0, 0)
    child = child_diag - (got[0] + got[1] + got[2] + got[3])
    return cross, child


def solution(mesh):
    fine = Mesh(mesh.devices.reshape(SIZES), AXES)
    spec = P(ROWS, COLS)
    return jax.shard_map(
        per_device,
        mesh=fine,
        in_specs=(spec, P(), spec, spec),
        out_specs=(spec, spec),
        check_vma=False,
    )
```

time: 157 us -> 144 us (0.917)
  starting transfers between devices: 35.7 us -> 63.5 us
  waiting for transfers between devices: 65.3 us -> 42.2 us
  between operations: 15.7 us -> 0.91 us
  blocking collectives: 18.7 us -> 17.1 us
    ppermute x5 -> x17, starting transfers between devices: 12.6 us -> 40.5 us  [the longest x12 27.9 us: shift(): return lax.ppermute(block, axis, [(i, (i + k) % 4) for i in range(4)])]
    ppermute x5 -> x17, waiting for transfers between devices: 6.24 us -> 31 us  [the longest x12 25.2 us: shift(): return lax.ppermute(block, axis, [(i, (i + k) % 4) for i in range(4)])]
    all_gather x2 -> x0, waiting for transfers between devices: 18.3 us -> none  [the longest x1 18.2 us: per_device(): factor_turned = lax.all_gather(turned, COLS, axis=0, tiled=True)]
    all_to_all x2 -> x1, waiting for transfers between devices: 23.2 us -> 11.2 us  [per_device(): cross_group = lax.all_to_all(copies, GROUP, 0, 0).reshape(512, 512)]
    all_to_all x1, waiting for transfers between devices: 8.62 us -> 0.01 us  [per_device(): got = lax.all_to_all(share.reshape(4, 64, 512), 'y', 0, 0)]
    all_to_all x1, waiting for transfers between devices: 8.52 us -> 0.01 us  [per_device(): pieces = lax.all_to_all(sends, ROWS, 0, 0)]
    all_to_all x2 -> x1, starting transfers between devices: 11.9 us -> 9.15 us  [per_device(): cross_group = lax.all_to_all(copies, GROUP, 0, 0).reshape(512, 512)]
    all_to_all x1, starting transfers between devices: 7.68 us -> 9.88 us  [per_device(): pieces = lax.all_to_all(sends, ROWS, 0, 0)]
  transfers between devices with their start and end apart: 11 -> 20, of which waited for: 9 -> 12; matrix products, arithmetic and copies ran while one was open for 6% -> 5% of each run, Pallas kernels for 2% -> 1%
where the time goes in v2:
time: 144 us; the launch traced here: 143 us
  starting transfers between devices  63.5 us (44%)
  waiting for transfers between devices  42.2 us (29%)
  blocking collectives  17.1 us (12%)
  local copies, waits for them, and re-layouts  8.11 us (6%)
  matrix products  3.73 us (3%)
  other arithmetic  3.65 us (3%)
  Pallas kernels  3.48 us (2%)
    ppermute x12, starting transfers between devices, shift(): return lax.ppermute(block, axis, [(i, (i + k) % 4) for i in range(4)])  27.9 us
    ppermute x12, waiting for transfers between devices, shift(): return lax.ppermute(block, axis, [(i, (i + k) % 4) for i in range(4)])  25.2 us
    all_to_all x1, blocking collectives, per_device(): got = lax.all_to_all(share.reshape(4, 128, 512), 'y', 0, 0)  17.1 us
    all_to_all x1, waiting for transfers between devices, per_device(): cross_group = lax.all_to_all(copies, GROUP, 0, 0).reshape(512, 512)  11.2 us
    all_to_all x1, starting transfers between devices, per_device(): pieces = lax.all_to_all(sends, ROWS, 0, 0)  9.88 us
    all_to_all x1, starting transfers between devices, per_device(): cross_group = lax.all_to_all(copies, GROUP, 0, 0).reshape(512, 512)  9.15 us
    ppermute x1, starting transfers between devices, per_device(): turned = lax.ppermute(factor, AXES, turn)  4.76 us
    all_to_all x1, starting transfers between devices, per_device(): got = lax.all_to_all(share.reshape(4, 64, 512), 'y', 0, 0)  3.94 us
  transfers between devices with their start and end apart: 20, of which 12 were waited for; matrix products, arithmetic and copies ran while one was open for 5% of the time, Pallas kernels for 1%

profile of v2, /device:TPU:1, one launch (start us, length us, event | category | flops | bytes accessed | tf_op | source)
XLA Modules:
  0.0 142.6 jit_solution(17733790933672551601)
XLA Ops:
  0.6 2.6 %collective-permute-start.4 = (f32[64,512]{1,0:T(8,128)}, f32[64,512]{1,0:T(8,128)S(1)}, u32[]{:S(2)}, u32[]{:S(2)}) collective-permute-start(f32[64,512]{1,0:T(8,128)} %param.8), channel_id=1, source_target_pairs={{0,32},{32,0},{1,33},{33,1},{2,34},{34,2},{3,35},{35,3},{4,36},{36... | collective-permute-start | bytes 393224 | tf_op jit(solution)/shard_map/ppermute | solution.py:93
  3.2 1.2 dynamic-slice_bitcast_fusion.5
  4.3 5.2 %collective-permute-start.2 = (f32[3,16,768]{2,1,0:T(8,128)S(1)}, f32[3,16,768]{2,1,0:T(8,128)S(1)}, u32[]{:S(2)}, u32[]{:S(2)}) collective-permute-start(f32[3,16,768]{2,1,0:T(8,128)S(1)} %get-tuple-element.42), channel_id=1, source_target_pairs={{0,6},{2,0},{4,2},{6,4},{1,7},{3,1},{5,3},{7,5},{8,14},{10,8},{12,... | collective-permute-start | bytes 442376 | tf_op jit(solution)/shard_map/ppermute | solution.py:50
  9.5 1.2 collective-permute-start.1
  10.7 2.1 %collective-permute-start = (f32[3,16,768]{2,1,0:T(8,128)S(1)}, f32[3,16,768]{2,1,0:T(8,128)S(1)}, u32[]{:S(2)}, u32[]{:S(2)}) collective-permute-start(f32[3,16,768]{2,1,0:T(8,128)S(1)} %get-tuple-element.44), channel_id=1, source_target_pairs={{0,2},{2,4},{4,6},{6,0},{1,3},{3,5},{5,7},{7,1},{8,10},{10,12},{12... | collective-permute-start | bytes 442376 | tf_op jit(solution)/shard_map/ppermute | solution.py:50
  12.8 0.6 copy-done
  13.9 0.6 gather_fusion
  15.2 6.6 %collective-permute-done.2 = f32[3,16,768]{2,1,0:T(8,128)S(1)} collective-permute-done((f32[3,16,768]{2,1,0:T(8,128)S(1)}, f32[3,16,768]{2,1,0:T(8,128)S(1)}, u32[]{:S(2)}, u32[]{:S(2)}) %collective-permute-start.2) | collective-permute-done | bytes 147488 | tf_op jit(solution)/shard_map/ppermute | solution.py:50
  21.9 0.8 dynamic-slice_bitcast_fusion
  22.6 2.4 %collective-permute-start.3 = (f32[4,3,8,768]{3,2,1,0:T(8,128)S(1)}, f32[4,3,8,768]{3,2,1,0:T(8,128)S(1)}, u32[]{:S(2)}, u32[]{:S(2)}) collective-permute-start(f32[4,3,8,768]{3,2,1,0:T(8,128)S(1)} %get-tuple-element.39), channel_id=1, source_target_pairs={{0,1},{1,0},{2,3},{3,2},{4,5},{5,4},{6,7},{7,6},{8,9},{9,8},{10,11... | collective-permute-start | bytes 884744 | tf_op jit(solution)/shard_map/ppermute | solution.py:97
  25.1 0.6 pad_add_fusion.table
  25.7 0.6 collective-permute-done.3.got
  26.3 0.7 copy-done.4
  27.0 1.9 %shard_map.59 = f32[32,8,256]{2,1,0:T(8,128)} custom-call(s32[52]{0:T(128)} %pad_add_fusion.table, f32[4,3,8,768]{3,2,1,0:T(8,128)} %get-tuple-element.40.keep, f32[4,3,8,768]{3,2,1,0:T(8,128)} %copy-done.4), custom_call_target="tpu_custom_call" | custom-call | tf_op jit(solution)/shard_map/pallas_call | solution.py:98
  28.9 9.9 %all-to-all-start = ((f32[32,8,256]{2,1,0:T(8,128)}), f32[32,8,256]{2,1,0:T(8,128)S(1)}, u32[]{:S(2)}, u32[]{:S(2)}) async-start(f32[32,8,256]{2,1,0:T(8,128)} %shard_map.59), calls=%async_computation | async-start | bytes 524288 | tf_op jit(solution)/shard_map/all_to_all | solution.py:106
  38.8 2.6 %collective-permute-start.7 = (f32[2,64,512]{2,1,0:T(8,128)S(1)}, f32[2,64,512]{2,1,0:T(8,128)S(1)}, u32[]{:S(2)}, u32[]{:S(2)}) collective-permute-start(f32[2,64,512]{2,1,0:T(8,128)S(1)} %pad_maximum_fusion.5), channel_id=1, source_target_pairs={{0,192},{64,0},{128,64},{192,128},{1,193},{65,1},{129,65},{193,129... | collective-permute-start | bytes 786440 | tf_op jit(solution)/shard_map/ppermute | solution.py:50
  41.4 0.5 collective-permute-start.6
  41.9 0.6 collective-permute-start.5
  42.5 4.8 %collective-permute-start.8 = (f32[64,512]{1,0:T(8,128)S(1)}, f32[64,512]{1,0:T(8,128)S(1)}, u32[]{:S(2)}, u32[]{:S(2)}) collective-permute-start(f32[64,512]{1,0:T(8,128)S(1)} %copy-done.6), channel_id=1, source_target_pairs={{0,0},{1,32},{2,64},{3,96},{4,128},{5,160},{6,192},{7,224},{8,8},{... | collective-permute-start | bytes 393224 | tf_op jit(solution)/shard_map/ppermute | solution.py:116
  47.5 2.7 %collective-permute-done.8 = f32[64,512]{1,0:T(8,128)S(1)} collective-permute-done((f32[64,512]{1,0:T(8,128)S(1)}, f32[64,512]{1,0:T(8,128)S(1)}, u32[]{:S(2)}, u32[]{:S(2)}) %collective-permute-start.8) | collective-permute-done | bytes 131104 | tf_op jit(solution)/shard_map/ppermute | solution.py:116
  50.3 7.6 %collective-permute-done.5 = f32[2,64,512]{2,1,0:T(8,128)S(1)} collective-permute-done((f32[2,64,512]{2,1,0:T(8,128)S(1)}, f32[2,64,512]{2,1,0:T(8,128)S(1)}, u32[]{:S(2)}, u32[]{:S(2)}) %collective-permute-start.5) | collective-permute-done | bytes 262176 | tf_op jit(solution)/shard_map/ppermute | solution.py:50
  57.9 0.7 copy-done.1
  58.6 1.6 %shard_map.60 = f32[8,8,256]{2,1,0:T(8,128)} custom-call(s32[8]{0:T(128)} %and_select_fusion.10.table, f32[32,8,256]{2,1,0:T(8,128)} %copy-done.1), custom_call_target="tpu_custom_call" | custom-call | tf_op jit(solution)/shard_map/pallas_call | solution.py:119
  60.2 4.4 %collective-permute-start.11 = (f32[8,8,256]{2,1,0:T(8,128)}, f32[8,8,256]{2,1,0:T(8,128)S(1)}, u32[]{:S(2)}, u32[]{:S(2)}) collective-permute-start(f32[8,8,256]{2,1,0:T(8,128)} %shard_map.60), channel_id=1, source_target_pairs={{0,6},{2,0},{4,2},{6,4},{1,7},{3,1},{5,3},{7,5},{8,14},{10,8},{12,... | collective-permute-start | bytes 196616 | tf_op jit(solution)/shard_map/ppermute | solution.py:50
  64.6 2.1 %collective-permute-start.10 = (f32[8,8,256]{2,1,0:T(8,128)}, f32[8,8,256]{2,1,0:T(8,128)S(1)}, u32[]{:S(2)}, u32[]{:S(2)}) collective-permute-start(f32[8,8,256]{2,1,0:T(8,128)} %shard_map.60), channel_id=1, source_target_pairs={{0,4},{2,6},{4,0},{6,2},{1,5},{3,7},{5,1},{7,3},{8,12},{10,14},{12... | collective-permute-start | bytes 196616 | tf_op jit(solution)/shard_map/ppermute | solution.py:50
  66.7 2.4 %collective-permute-start.9 = (f32[8,8,256]{2,1,0:T(8,128)}, f32[8,8,256]{2,1,0:T(8,128)S(1)}, u32[]{:S(2)}, u32[]{:S(2)}) collective-permute-start(f32[8,8,256]{2,1,0:T(8,128)} %shard_map.60), channel_id=1, source_target_pairs={{0,2},{2,4},{4,6},{6,0},{1,3},{3,5},{5,7},{7,1},{8,10},{10,12},{12... | collective-permute-start | bytes 196616 | tf_op jit(solution)/shard_map/ppermute | solution.py:50
  69.1 0.6 gather_fusion.2
  69.8 2.2 %collective-permute-done.10 = f32[8,8,256]{2,1,0:T(8,128)S(1)} collective-permute-done((f32[8,8,256]{2,1,0:T(8,128)}, f32[8,8,256]{2,1,0:T(8,128)S(1)}, u32[]{:S(2)}, u32[]{:S(2)}) %collective-permute-start.10) | collective-permute-done | bytes 65568 | tf_op jit(solution)/shard_map/ppermute | solution.py:50
  72.0 1.5 %collective-permute-done.9 = f32[8,8,256]{2,1,0:T(8,128)S(1)} collective-permute-done((f32[8,8,256]{2,1,0:T(8,128)}, f32[8,8,256]{2,1,0:T(8,128)S(1)}, u32[]{:S(2)}, u32[]{:S(2)}) %collective-permute-start.9) | collective-permute-done | bytes 65568 | tf_op jit(solution)/shard_map/ppermute | solution.py:50
  73.5 2.0 %collective-permute-start.12 = (f32[4,8,8,256]{3,2,1,0:T(8,128)S(1)}, f32[4,8,8,256]{3,2,1,0:T(8,128)S(1)}, u32[]{:S(2)}, u32[]{:S(2)}) collective-permute-start(f32[4,8,8,256]{3,2,1,0:T(8,128)S(1)} %pad_maximum_fusion.6), channel_id=1, source_target_pairs={{0,1},{1,0},{2,3},{3,2},{4,5},{5,4},{6,7},{7,6},{8,9},{9,8},{10,11... | collective-permute-start | bytes 786440 | tf_op jit(solution)/shard_map/ppermute | solution.py:59
  75.7 0.9 collective-permute-done.12
  76.8 0.6 gather_fusion.1
  77.5 1.9 %fusion.12 = f32[256,512]{1,0:T(8,128)} fusion(f32[512,256]{1,0:T(8,128)S(1)} %bitcast.73, f32[512,512]{1,0:T(8,128)S(1)} %bitcast.71), kind=kOutput, calls=%fused_computation.89 | convolution fusion | flops 805306368 | bytes 2097152 | tf_op jit(solution)/shard_map/dot_general | solution.py:36
  79.4 3.9 %all-to-all-start.1 = ((f32[4,64,512]{2,1,0:T(8,128)}), f32[4,64,512]{2,1,0:T(8,128)S(1)}, u32[]{:S(2)}, u32[]{:S(2)}) async-start(f32[4,64,512]{2,1,0:T(8,128)} %bitcast.28), calls=%async_computation.1 | async-start | bytes 1048576 | tf_op jit(solution)/shard_map/all_to_all | solution.py:131
  83.3 2.3 %collective-permute-start.15 = (f32[64,512]{1,0:T(8,128)S(1)}, f32[64,512]{1,0:T(8,128)S(1)}, u32[]{:S(2)}, u32[]{:S(2)}) collective-permute-start(f32[64,512]{1,0:T(8,128)S(1)} %collective-permute-done.8), channel_id=1, source_target_pairs={{0,6},{2,0},{4,2},{6,4},{1,7},{3,1},{5,3},{7,5},{8,14},{10,8},{12,... | collective-permute-start | bytes 393224 | tf_op jit(solution)/shard_map/ppermute | solution.py:50
  85.6 2.4 %collective-permute-start.14 = (f32[64,512]{1,0:T(8,128)S(1)}, f32[64,512]{1,0:T(8,128)S(1)}, u32[]{:S(2)}, u32[]{:S(2)}) collective-permute-start(f32[64,512]{1,0:T(8,128)S(1)} %collective-permute-done.8), channel_id=1, source_target_pairs={{0,4},{2,6},{4,0},{6,2},{1,5},{3,7},{5,1},{7,3},{8,12},{10,14},{12... | collective-permute-start | bytes 393224 | tf_op jit(solution)/shard_map/ppermute | solution.py:50
  87.9 2.4 %collective-permute-start.13 = (f32[64,512]{1,0:T(8,128)S(1)}, f32[64,512]{1,0:T(8,128)S(1)}, u32[]{:S(2)}, u32[]{:S(2)}) collective-permute-start(f32[64,512]{1,0:T(8,128)S(1)} %collective-permute-done.8), channel_id=1, source_target_pairs={{0,2},{2,4},{4,6},{6,0},{1,3},{3,5},{5,7},{7,1},{8,10},{10,12},{12... | collective-permute-start | bytes 393224 | tf_op jit(solution)/shard_map/ppermute | solution.py:50
  90.3 3.2 %collective-permute-done.14 = f32[64,512]{1,0:T(8,128)S(1)} collective-permute-done((f32[64,512]{1,0:T(8,128)S(1)}, f32[64,512]{1,0:T(8,128)S(1)}, u32[]{:S(2)}, u32[]{:S(2)}) %collective-permute-start.14) | collective-permute-done | bytes 131104 | tf_op jit(solution)/shard_map/ppermute | solution.py:50
  93.5 3.9 %collective-permute-done.13 = f32[64,512]{1,0:T(8,128)S(1)} collective-permute-done((f32[64,512]{1,0:T(8,128)S(1)}, f32[64,512]{1,0:T(8,128)S(1)}, u32[]{:S(2)}, u32[]{:S(2)}) %collective-permute-start.13) | collective-permute-done | bytes 131104 | tf_op jit(solution)/shard_map/ppermute | solution.py:50
  97.5 1.1 broadcast_in_dim.58
  98.6 9.2 %all-to-all-start.2 = ((f32[8,64,512]{2,1,0:T(8,128)}), f32[8,64,512]{2,1,0:T(8,128)S(1)}, u32[]{:S(2)}, u32[]{:S(2)}) async-start(f32[8,64,512]{2,1,0:T(8,128)} %broadcast_in_dim.58), calls=%async_computation.2 | async-start | bytes 2097152 | tf_op jit(solution)/shard_map/all_to_all | solution.py:136
  107.8 0.9 collective-permute-start.16
  108.7 1.5 %collective-permute-done.16 = f32[4,64,512]{2,1,0:T(8,128)S(1)} collective-permute-done((f32[4,64,512]{2,1,0:T(8,128)S(1)}, f32[4,64,512]{2,1,0:T(8,128)S(1)}, u32[]{:S(2)}, u32[]{:S(2)}) %collective-permute-start.16) | collective-permute-done | bytes 524320 | tf_op jit(solution)/shard_map/ppermute | solution.py:59
  110.4 0.6 gather_fusion.3
  111.6 11.2 %all-to-all-done.2 = f32[8,64,512]{2,1,0:T(8,128)S(1)} async-done(((f32[8,64,512]{2,1,0:T(8,128)}), f32[8,64,512]{2,1,0:T(8,128)S(1)}, u32[]{:S(2)}, u32[]{:S(2)}) %all-to-all-start.2) | async-done | bytes 1048608 | tf_op jit(solution)/shard_map/all_to_all | solution.py:136
  122.8 1.8 %fusion.13 = f32[4,128,512]{2,1,0:T(8,128)S(1)} fusion(f32[4,128,512]{2,1,0:T(8,128)S(1)} %bitcast.70, f32[512,512,1]{1,0,2:T(8,128)S(1)} %bitcast.69), kind=kOutput, calls=%fused_computation.90 | convolution fusion | flops 1610612736 | bytes 3145728 | tf_op jit(solution)/shard_map/dot_general | solution.py:36
  124.7 17.1 %all_to_all.20 = f32[4,128,512]{2,1,0:T(8,128)S(1)} all-to-all(f32[4,128,512]{2,1,0:T(8,128)S(1)} %fusion.13), channel_id=1, replica_groups=mesh['x'=4,'zl'=2,'y'=4,'zh'=4,'core'=2] {'y'}, dimensions={0} | all-to-all | bytes 2097152 | tf_op jit(solution)/shard_map/all_to_all | solution.py:139
  141.7 0.8 fusion.1
  (54 shorter events, 2.9 us)
Async XLA Ops:
  0.6 28.2 %collective-permute-start.4 = (f32[64,512]{1,0:T(8,128)}, f32[64,512]{1,0:T(8,128)S(1)}, u32[]{:S(2)}, u32[]{:S(2)}) collective-permute-start(f32[64,512]{1,0:T(8,128)} %param.8), channel_id=1, source_target_pairs={{0,32},{32,0},{1,33},{33,1},{2,34},{34,2},{3,35},{35,3},{4,36},{36... | collective-permute-start | bytes 393224 | tf_op jit(solution)/shard_map/ppermute | solution.py:93
  4.3 17.5 %collective-permute-start.2 = (f32[3,16,768]{2,1,0:T(8,128)S(1)}, f32[3,16,768]{2,1,0:T(8,128)S(1)}, u32[]{:S(2)}, u32[]{:S(2)}) collective-permute-start(f32[3,16,768]{2,1,0:T(8,128)S(1)} %get-tuple-element.42), channel_id=1, source_target_pairs={{0,6},{2,0},{4,2},{6,4},{1,7},{3,1},{5,3},{7,5},{8,14},{10,8},{12,... | collective-permute-start | bytes 442376 | tf_op jit(solution)/shard_map/ppermute | solution.py:50
  9.5 12.3 %collective-permute-start.1 = (f32[3,16,768]{2,1,0:T(8,128)S(1)}, f32[3,16,768]{2,1,0:T(8,128)S(1)}, u32[]{:S(2)}, u32[]{:S(2)}) collective-permute-start(f32[3,16,768]{2,1,0:T(8,128)S(1)} %get-tuple-element.43), channel_id=1, source_target_pairs={{0,4},{2,6},{4,0},{6,2},{1,5},{3,7},{5,1},{7,3},{8,12},{10,14},{12... | collective-permute-start | bytes 442376 | tf_op jit(solution)/shard_map/ppermute | solution.py:50
  10.7 11.1 %collective-permute-start = (f32[3,16,768]{2,1,0:T(8,128)S(1)}, f32[3,16,768]{2,1,0:T(8,128)S(1)}, u32[]{:S(2)}, u32[]{:S(2)}) collective-permute-start(f32[3,16,768]{2,1,0:T(8,128)S(1)} %get-tuple-element.44), channel_id=1, source_target_pairs={{0,2},{2,4},{4,6},{6,0},{1,3},{3,5},{5,7},{7,1},{8,10},{10,12},{12... | collective-permute-start | bytes 442376 | tf_op jit(solution)/shard_map/ppermute | solution.py:50
  12.8 0.7 copy-start
  22.6 3.6 %collective-permute-start.3 = (f32[4,3,8,768]{3,2,1,0:T(8,128)S(1)}, f32[4,3,8,768]{3,2,1,0:T(8,128)S(1)}, u32[]{:S(2)}, u32[]{:S(2)}) collective-permute-start(f32[4,3,8,768]{3,2,1,0:T(8,128)S(1)} %get-tuple-element.39), channel_id=1, source_target_pairs={{0,1},{1,0},{2,3},{3,2},{4,5},{5,4},{6,7},{7,6},{8,9},{9,8},{10,11... | collective-permute-start | bytes 884744 | tf_op jit(solution)/shard_map/ppermute | solution.py:97
  26.3 0.7 copy-start.4
  28.9 9.9 %copy-start.6 = (f32[64,512]{1,0:T(8,128)S(1)}, f32[64,512]{1,0:T(8,128)}, u32[]{:S(2)}) copy-start(f32[64,512]{1,0:T(8,128)} %param.8) | copy-start | bytes 393220
  28.9 29.1 %all-to-all-start = ((f32[32,8,256]{2,1,0:T(8,128)}), f32[32,8,256]{2,1,0:T(8,128)S(1)}, u32[]{:S(2)}, u32[]{:S(2)}) async-start(f32[32,8,256]{2,1,0:T(8,128)} %shard_map.59), calls=%async_computation | async-start | bytes 524288 | tf_op jit(solution)/shard_map/all_to_all | solution.py:106
  38.8 11.4 %collective-permute-start.7 = (f32[2,64,512]{2,1,0:T(8,128)S(1)}, f32[2,64,512]{2,1,0:T(8,128)S(1)}, u32[]{:S(2)}, u32[]{:S(2)}) collective-permute-start(f32[2,64,512]{2,1,0:T(8,128)S(1)} %pad_maximum_fusion.5), channel_id=1, source_target_pairs={{0,192},{64,0},{128,64},{192,128},{1,193},{65,1},{129,65},{193,129... | collective-permute-start | bytes 786440 | tf_op jit(solution)/shard_map/ppermute | solution.py:50
  41.4 9.0 %collective-permute-start.6 = (f32[2,64,512]{2,1,0:T(8,128)S(1)}, f32[2,64,512]{2,1,0:T(8,128)S(1)}, u32[]{:S(2)}, u32[]{:S(2)}) collective-permute-start(f32[2,64,512]{2,1,0:T(8,128)S(1)} %pad_maximum_fusion.5), channel_id=1, source_target_pairs={{0,128},{64,192},{128,0},{192,64},{1,129},{65,193},{129,1},{193,65... | collective-permute-start | bytes 786440 | tf_op jit(solution)/shard_map/ppermute | solution.py:50
  41.9 16.0 %collective-permute-start.5 = (f32[2,64,512]{2,1,0:T(8,128)S(1)}, f32[2,64,512]{2,1,0:T(8,128)S(1)}, u32[]{:S(2)}, u32[]{:S(2)}) collective-permute-start(f32[2,64,512]{2,1,0:T(8,128)S(1)} %pad_maximum_fusion.5), channel_id=1, source_target_pairs={{0,64},{64,128},{128,192},{192,0},{1,65},{65,129},{129,193},{193,1... | collective-permute-start | bytes 786440 | tf_op jit(solution)/shard_map/ppermute | solution.py:50
  42.5 7.7 %collective-permute-start.8 = (f32[64,512]{1,0:T(8,128)S(1)}, f32[64,512]{1,0:T(8,128)S(1)}, u32[]{:S(2)}, u32[]{:S(2)}) collective-permute-start(f32[64,512]{1,0:T(8,128)S(1)} %copy-done.6), channel_id=1, source_target_pairs={{0,0},{1,32},{2,64},{3,96},{4,128},{5,160},{6,192},{7,224},{8,8},{... | collective-permute-start | bytes 393224 | tf_op jit(solution)/shard_map/ppermute | solution.py:116
  57.9 0.7 copy-start.1
  60.2 9.5 %collective-permute-start.11 = (f32[8,8,256]{2,1,0:T(8,128)}, f32[8,8,256]{2,1,0:T(8,128)S(1)}, u32[]{:S(2)}, u32[]{:S(2)}) collective-permute-start(f32[8,8,256]{2,1,0:T(8,128)} %shard_map.60), channel_id=1, source_target_pairs={{0,6},{2,0},{4,2},{6,4},{1,7},{3,1},{5,3},{7,5},{8,14},{10,8},{12,... | collective-permute-start | bytes 196616 | tf_op jit(solution)/shard_map/ppermute | solution.py:50
  64.6 7.4 %collective-permute-start.10 = (f32[8,8,256]{2,1,0:T(8,128)}, f32[8,8,256]{2,1,0:T(8,128)S(1)}, u32[]{:S(2)}, u32[]{:S(2)}) collective-permute-start(f32[8,8,256]{2,1,0:T(8,128)} %shard_map.60), channel_id=1, source_target_pairs={{0,4},{2,6},{4,0},{6,2},{1,5},{3,7},{5,1},{7,3},{8,12},{10,14},{12... | collective-permute-start | bytes 196616 | tf_op jit(solution)/shard_map/ppermute | solution.py:50
  66.7 6.8 %collective-permute-start.9 = (f32[8,8,256]{2,1,0:T(8,128)}, f32[8,8,256]{2,1,0:T(8,128)S(1)}, u32[]{:S(2)}, u32[]{:S(2)}) collective-permute-start(f32[8,8,256]{2,1,0:T(8,128)} %shard_map.60), channel_id=1, source_target_pairs={{0,2},{2,4},{4,6},{6,0},{1,3},{3,5},{5,7},{7,1},{8,10},{10,12},{12... | collective-permute-start | bytes 196616 | tf_op jit(solution)/shard_map/ppermute | solution.py:50
  69.1 4.4 %copy-start.2 = (f32[8,8,256]{2,1,0:T(8,128)S(1)}, f32[8,8,256]{2,1,0:T(8,128)}, u32[]{:S(2)}) copy-start(f32[8,8,256]{2,1,0:T(8,128)} %shard_map.60) | copy-start | bytes 196612
  73.5 3.1 %collective-permute-start.12 = (f32[4,8,8,256]{3,2,1,0:T(8,128)S(1)}, f32[4,8,8,256]{3,2,1,0:T(8,128)S(1)}, u32[]{:S(2)}, u32[]{:S(2)}) collective-permute-start(f32[4,8,8,256]{3,2,1,0:T(8,128)S(1)} %pad_maximum_fusion.6), channel_id=1, source_target_pairs={{0,1},{1,0},{2,3},{3,2},{4,5},{5,4},{6,7},{7,6},{8,9},{9,8},{10,11... | collective-permute-start | bytes 786440 | tf_op jit(solution)/shard_map/ppermute | solution.py:59
  79.4 18.1 %all-to-all-start.1 = ((f32[4,64,512]{2,1,0:T(8,128)}), f32[4,64,512]{2,1,0:T(8,128)S(1)}, u32[]{:S(2)}, u32[]{:S(2)}) async-start(f32[4,64,512]{2,1,0:T(8,128)} %bitcast.28), calls=%async_computation.1 | async-start | bytes 1048576 | tf_op jit(solution)/shard_map/all_to_all | solution.py:131
  83.3 7.0 %collective-permute-start.15 = (f32[64,512]{1,0:T(8,128)S(1)}, f32[64,512]{1,0:T(8,128)S(1)}, u32[]{:S(2)}, u32[]{:S(2)}) collective-permute-start(f32[64,512]{1,0:T(8,128)S(1)} %collective-permute-done.8), channel_id=1, source_target_pairs={{0,6},{2,0},{4,2},{6,4},{1,7},{3,1},{5,3},{7,5},{8,14},{10,8},{12,... | collective-permute-start | bytes 393224 | tf_op jit(solution)/shard_map/ppermute | solution.py:50
  85.6 7.9 %collective-permute-start.14 = (f32[64,512]{1,0:T(8,128)S(1)}, f32[64,512]{1,0:T(8,128)S(1)}, u32[]{:S(2)}, u32[]{:S(2)}) collective-permute-start(f32[64,512]{1,0:T(8,128)S(1)} %collective-permute-done.8), channel_id=1, source_target_pairs={{0,4},{2,6},{4,0},{6,2},{1,5},{3,7},{5,1},{7,3},{8,12},{10,14},{12... | collective-permute-start | bytes 393224 | tf_op jit(solution)/shard_map/ppermute | solution.py:50
  87.9 9.5 %collective-permute-start.13 = (f32[64,512]{1,0:T(8,128)S(1)}, f32[64,512]{1,0:T(8,128)S(1)}, u32[]{:S(2)}, u32[]{:S(2)}) collective-permute-start(f32[64,512]{1,0:T(8,128)S(1)} %collective-permute-done.8), channel_id=1, source_target_pairs={{0,2},{2,4},{4,6},{6,0},{1,3},{3,5},{5,7},{7,1},{8,10},{10,12},{12... | collective-permute-start | bytes 393224 | tf_op jit(solution)/shard_map/ppermute | solution.py:50
  97.5 1.2 copy-start.3
  98.6 24.2 %all-to-all-start.2 = ((f32[8,64,512]{2,1,0:T(8,128)}), f32[8,64,512]{2,1,0:T(8,128)S(1)}, u32[]{:S(2)}, u32[]{:S(2)}) async-start(f32[8,64,512]{2,1,0:T(8,128)} %broadcast_in_dim.58), calls=%async_computation.2 | async-start | bytes 2097152 | tf_op jit(solution)/shard_map/all_to_all | solution.py:136
  107.8 2.4 %collective-permute-start.16 = (f32[4,64,512]{2,1,0:T(8,128)S(1)}, f32[4,64,512]{2,1,0:T(8,128)S(1)}, u32[]{:S(2)}, u32[]{:S(2)}) collective-permute-start(f32[4,64,512]{2,1,0:T(8,128)S(1)} %pad_maximum_fusion.4), channel_id=1, source_target_pairs={{0,1},{1,0},{2,3},{3,2},{4,5},{5,4},{6,7},{7,6},{8,9},{9,8},{10,11... | collective-permute-start | bytes 1572872 | tf_op jit(solution)/shard_map/ppermute | solution.py:59
  124.7 17.1 %copy-start.5 = (f32[128,512]{1,0:T(8,128)S(1)}, f32[128,512]{1,0:T(8,128)}, u32[]{:S(2)}) copy-start(f32[128,512]{1,0:T(8,128)} %param.9) | copy-start | bytes 786436

commit v3 on v0

v3 whole, which is shorter than its diff:
```python
import jax
import jax.numpy as jnp
from jax import lax
from jax.experimental import pallas as pl
from jax.experimental.pallas import tpu as pltpu
from jax.sharding import Mesh, PartitionSpec as P

BLK = 128
AXES = ("x", "zl", "y", "zh", "core")
SIZES = (4, 2, 4, 4, 2)
CLASSED = ("y", "x", "zl")
ROWS = ("x", "zl", "y")
COLS = ("zh", "core")
GROUP = ("x", "zl")
SWAP = [(0, 1), (1, 0)]
HI = lax.Precision.HIGHEST


def class_kernel(where, structure, root, out, sems):
    row_dev = where[0]
    place = []
    for k in range(3):
        half = row_dev * 3 + k
        tile = half // 2
        before = jnp.int32(0)
        member = jnp.int32(0)
        for i in range(16):
            before += (structure[i] < tile).astype(jnp.int32)
            member += (structure[i] == tile).astype(jnp.int32)
        place.append(jnp.where(member > 0, (2 * before + half % 2) % 4, -1))
    copies = []
    for y in range(4):
        k = jnp.where(place[1] == y, 1, jnp.where(place[2] == y, 2, 0))
        copies.append(
            pltpu.make_async_copy(root.at[pl.ds(pl.multiple_of(k * 64, 64), 64)], out.at[y], sems.at[y])
        )
    for copy in copies:
        copy.start()
    for copy in copies:
        copy.wait()


def cut_kernel(table, pieces, own, down, down_two):
    zh = table[24]
    for d, out in enumerate((own, down, down_two)):
        for q in range(4):
            place = 4 * jnp.maximum(zh - d, 0) + q
            column = pl.multiple_of(table[8 + place], BLK)
            for j in range(8):
                out[q // 2, j, :, (q % 2) * BLK:(q % 2 + 1) * BLK] = pieces[table[j], :, pl.ds(column, BLK)]


def contract(first, second):
    return lax.dot_general(
        first, second, (((0,), (0,)), ((), ())), precision=HI, preferred_element_type=jnp.float32
    )


def vmem():
    return pl.BlockSpec(memory_space=pltpu.VMEM)


def smem():
    return pl.BlockSpec(memory_space=pltpu.SMEM)


def anywhere():
    return pl.BlockSpec(memory_space=pl.ANY)


def shift(block, axis, k):
    return lax.ppermute(block, axis, [(i, (i + k) % 4) for i in range(4)])


def turn(block, k):
    pairs = []
    for a in range(8):
        for b in range(4):
            for c in range(8):
                target = (a // 2 - k) % 4 * 2 + a % 2
                pairs.append(((a * 4 + b) * 8 + c, (c * 4 + b) * 8 + target))
    return lax.ppermute(block, AXES, pairs)


def at(array, index, axis=0):
    return lax.dynamic_index_in_dim(array, index, axis, keepdims=False)


def per_device(root_cov, structure, child_factor, child_diag):
    x, zl, y = lax.axis_index("x"), lax.axis_index("zl"), lax.axis_index("y")
    zh, core = lax.axis_index("zh"), lax.axis_index("core")
    group, col = x * 2 + zl, zh * 2 + core
    fours = lax.iota(jnp.int32, 4)

    turned = [turn(child_factor, k) for k in range(4)]

    sends = pl.pallas_call(
        class_kernel,
        out_shape=jax.ShapeDtypeStruct((4, 64, 768), jnp.float32),
        in_specs=[smem(), smem(), anywhere()],
        out_specs=anywhere(),
        scratch_shapes=[pltpu.SemaphoreType.DMA((4,))],
    )((group * 4 + y)[None], structure, root_cov)
    pieces = lax.all_to_all(sends.reshape(32, 8, 768), CLASSED, 0, 0)
    pieces, turned = lax.optimization_barrier((pieces, turned))

    steps = 2 * lax.iota(jnp.int32, 8) + y // 2
    source = (2 * jnp.take(structure, steps) + y % 2) // 3
    table = jnp.concatenate([source % 4 * 8 + source // 4, structure % 6 * BLK, zh[None]])
    cut = jax.ShapeDtypeStruct((2, 8, 8, 256), jnp.float32)
    own, down, down_two = pl.pallas_call(
        cut_kernel,
        out_shape=(cut, cut, cut),
        in_specs=[smem(), vmem()],
        out_specs=(vmem(), vmem(), vmem()),
    )(table, pieces)
    down = lax.ppermute(down, COLS, [(7, 5), (6, 4), (5, 3), (3, 1), (2, 0)])
    down_two = lax.ppermute(down_two, COLS, [(6, 2), (5, 1), (4, 0)])
    near = jnp.stack(turned)
    far = lax.ppermute(near, "core", SWAP)
    factor_x = [child_factor] + [shift(child_factor, "x", k) for k in (1, 2, 3)]
    down, down_two, near, far, factor_x = lax.optimization_barrier(
        (down, down_two, near, far, factor_x)
    )
    holder = structure // 6
    hops = lax.dynamic_slice(holder // 2, (4 * zh,), (4,)) - zh
    hops = jnp.repeat(hops, BLK).reshape(2, 1, 1, 256)
    mine = jnp.where(hops == 0, own, jnp.where(hops == 1, down, down_two))
    keep, give = at(mine, core), at(mine, 1 - core)
    got = lax.ppermute(give, "core", SWAP)
    side = jnp.repeat(lax.dynamic_slice(holder % 2, (2 * col,), (2,)), BLK)
    piece = jnp.where(side == core, keep, got)

    brick = lax.all_to_all(jnp.broadcast_to(piece[None], (8, 8, 8, 256)), GROUP, 0, 0)
    both = jnp.stack([jnp.where(core == 0, near, far), jnp.where(core == 0, far, near)], axis=1)
    factor_turned = jnp.take(both, (fours - zh) % 4, axis=0)
    factor_turned = factor_turned.reshape(8, 8, 8, 512).transpose(1, 0, 2, 3).reshape(512, 512)
    brick, factor_turned = lax.optimization_barrier((brick, factor_turned))

    share = contract(brick.reshape(512, 256), factor_turned)
    row = jnp.stack(factor_x)
    share, row = lax.optimization_barrier((share, row))
    got = lax.all_to_all(share.reshape(4, 64, 512), "y", 0, 0)
    other = lax.ppermute(row, "zl", SWAP)
    got, other = lax.optimization_barrier((got, other))
    cross = -(got[0] + got[1] + got[2] + got[3])

    near = jnp.stack([cross] + [shift(cross, "zh", k) for k in (1, 2, 3)])
    far = lax.ppermute(near, "core", SWAP)
    order = (x - zh + fours) % 4
    same = jnp.take(jnp.where(zl == core, row, other), order, axis=0)
    opposite = jnp.take(jnp.where(zl == core, other, row), order, axis=0)
    share = contract(near.reshape(256, 512), same.reshape(256, 512))
    share = share + contract(far.reshape(256, 512), opposite.reshape(256, 512))
    share, cross = lax.optimization_barrier((share, cross))
    got = lax.all_to_all(share.reshape(4, 128, 512), "y", 0, 0)
    child = child_diag - (got[0] + got[1] + got[2] + got[3])
    return turn(cross, 0), child


def solution(mesh):
    fine = Mesh(mesh.devices.reshape(SIZES), AXES)
    spec = P(ROWS, COLS)
    return jax.shard_map(
        per_device,
        mesh=fine,
        in_specs=(spec, P(), spec, spec),
        out_specs=(spec, spec),
        check_vma=False,
    )
```

time: 641 us -> 158 us (0.25)
  the two profiles are of different devices: /device:TPU:64 before, /device:TPU:1 now
where the time goes in v3:
time: 158 us; the launch traced here: 156 us
  starting transfers between devices  62.6 us (40%)
  waiting for transfers between devices  50.8 us (32%)
  Pallas kernels  27.7 us (18%)
  local copies, waits for them, and re-layouts  5.88 us (4%)
  matrix products  5.09 us (3%)
  other arithmetic  3.38 us (2%)
    pallas_call x1, Pallas kernels, per_device(): pl.pallas_call(class_kernel, out_shape=jax.ShapeDtypeStruct((4, 64, 768),...  25.7 us
    ppermute x5, starting transfers between devices, turn(): return lax.ppermute(block, AXES, pairs)  15.2 us
    ppermute x6, starting transfers between devices, shift(): return lax.ppermute(block, axis, [(i, (i + k) % 4) for i in range(4)])  12.1 us
    ppermute x6, waiting for transfers between devices, shift(): return lax.ppermute(block, axis, [(i, (i + k) % 4) for i in range(4)])  9.86 us
    all_to_all x1, starting transfers between devices, per_device(): pieces = lax.all_to_all(sends.reshape(32, 8, 768), CLASSED, 0, 0)  9.37 us
    ppermute x1, waiting for transfers between devices, per_device(): down = lax.ppermute(down, COLS, [(7, 5), (6, 4), (5, 3), (3, 1), (2, 0)])  9.36 us
    all_to_all x1, waiting for transfers between devices, per_device(): lax.all_to_all(jnp.broadcast_to(piece[None], (8, 8, 8, 256)), GROUP, 0, 0)  8 us
    all_to_all x1, waiting for transfers between devices, per_device(): got = lax.all_to_all(share.reshape(4, 128, 512), 'y', 0, 0)  7.96 us
  transfers between devices with their start and end apart: 21, of which 13 were waited for; matrix products, arithmetic and copies ran while one was open for 3% of the time, Pallas kernels for 1%

profile of v3, /device:TPU:1, one launch (start us, length us, event | category | flops | bytes accessed | tf_op | source)
XLA Modules:
  0.0 156.4 jit_solution(3686879398527819289)
XLA Ops:
  0.6 25.7 %shard_map.59 = f32[4,64,768]{2,1,0:T(8,128)} custom-call(s32[1]{0:T(128)} %bitcast.3.where, s32[16]{0:T(128)} %structure.1, f32[192,768]{1,0:T(8,128)} %root.1), custom_call_target="tpu_custom_call" | custom-call | tf_op jit(solution)/shard_map/pallas_call | solution.py:97
  26.4 9.4 %all-to-all-start = ((f32[32,8,768]{2,1,0:T(8,128)}), f32[32,8,768]{2,1,0:T(8,128)S(1)}, u32[]{:S(2)}, u32[]{:S(2)}) async-start(f32[32,8,768]{2,1,0:T(8,128)} %bitcast.62), calls=%async_computation | async-start | bytes 1572864 | tf_op jit(solution)/shard_map/all_to_all | solution.py:104
  35.8 2.8 %collective-permute-start.8 = (f32[64,512]{1,0:T(8,128)S(1)}, f32[64,512]{1,0:T(8,128)S(1)}, u32[]{:S(2)}, u32[]{:S(2)}) collective-permute-start(f32[64,512]{1,0:T(8,128)S(1)} %copy-done.7), channel_id=1, source_target_pairs={{0,128},{64,192},{128,0},{192,64},{1,129},{65,193},{129,1},{193,65... | collective-permute-start | bytes 393224 | tf_op jit(solution)/shard_map/ppermute | solution.py:72
  38.6 5.3 %collective-permute-start.3 = (f32[64,512]{1,0:T(8,128)S(1)}, f32[64,512]{1,0:T(8,128)S(1)}, u32[]{:S(2)}, u32[]{:S(2)}) collective-permute-start(f32[64,512]{1,0:T(8,128)S(1)} %copy-done.7), channel_id=1, source_target_pairs={{0,2},{1,34},{2,66},{3,98},{4,130},{5,162},{6,194},{7,226},{8,10},... | collective-permute-start | bytes 393224 | tf_op jit(solution)/shard_map/ppermute | solution.py:82
  43.9 2.1 %collective-permute-start.2 = (f32[64,512]{1,0:T(8,128)S(1)}, f32[64,512]{1,0:T(8,128)S(1)}, u32[]{:S(2)}, u32[]{:S(2)}) collective-permute-start(f32[64,512]{1,0:T(8,128)S(1)} %copy-done.7), channel_id=1, source_target_pairs={{0,4},{1,36},{2,68},{3,100},{4,132},{5,164},{6,196},{7,228},{8,12}... | collective-permute-start | bytes 393224 | tf_op jit(solution)/shard_map/ppermute | solution.py:82
  46.0 4.2 %collective-permute-start = (f32[64,512]{1,0:T(8,128)S(1)}, f32[64,512]{1,0:T(8,128)S(1)}, u32[]{:S(2)}, u32[]{:S(2)}) collective-permute-start(f32[64,512]{1,0:T(8,128)S(1)} %copy-done.7), channel_id=1, source_target_pairs={{0,0},{1,32},{2,64},{3,96},{4,128},{5,160},{6,192},{7,224},{8,8},{... | collective-permute-start | bytes 393224 | tf_op jit(solution)/shard_map/ppermute | solution.py:82
  50.3 0.6 copy-done
  51.2 0.6 gather_fusion
  52.0 2.5 %collective-permute-done.3 = f32[64,512]{1,0:T(8,128)S(1)} collective-permute-done((f32[64,512]{1,0:T(8,128)S(1)}, f32[64,512]{1,0:T(8,128)S(1)}, u32[]{:S(2)}, u32[]{:S(2)}) %collective-permute-start.3) | collective-permute-done | bytes 131104 | tf_op jit(solution)/shard_map/ppermute | solution.py:82
  54.6 5.1 %collective-permute-start.7 = (f32[64,512]{1,0:T(8,128)S(1)}, f32[64,512]{1,0:T(8,128)S(1)}, u32[]{:S(2)}, u32[]{:S(2)}) collective-permute-start(f32[64,512]{1,0:T(8,128)S(1)} %copy-done.7), channel_id=1, source_target_pairs={{0,64},{64,128},{128,192},{192,0},{1,65},{65,129},{129,193},{193,1... | collective-permute-start | bytes 393224 | tf_op jit(solution)/shard_map/ppermute | solution.py:72
  59.6 0.6 collective-permute-done.2
  60.3 3.5 %collective-permute-start.6 = (f32[4,64,512]{2,1,0:T(8,128)S(1)}, f32[4,64,512]{2,1,0:T(8,128)S(1)}, u32[]{:S(2)}, u32[]{:S(2)}) collective-permute-start(f32[4,64,512]{2,1,0:T(8,128)S(1)} %pad_maximum_fusion.1), channel_id=1, source_target_pairs={{0,1},{1,0},{2,3},{3,2},{4,5},{5,4},{6,7},{7,6},{8,9},{9,8},{10,11... | collective-permute-start | bytes 1572872 | tf_op jit(solution)/shard_map/ppermute | solution.py:120
  64.1 0.6 pad_add_fusion.table
  64.6 2.0 %shard_map.60 = (f32[2,8,8,256]{3,2,1,0:T(8,128)}, f32[2,8,8,256]{3,2,1,0:T(8,128)}, f32[2,8,8,256]{3,2,1,0:T(8,128)}) custom-call(s32[25]{0:T(128)} %pad_add_fusion.table, f32[32,8,768]{2,1,0:T(8,128)} %copy-done.1), custom_call_target="tpu_custom_call" | custom-call | tf_op jit(solution)/shard_map/pallas_call | solution.py:111
  66.6 1.3 collective-permute-start.4
  67.9 1.3 collective-permute-start.5
  69.3 9.4 %collective-permute-done.4 = f32[2,8,8,256]{3,2,1,0:T(8,128)S(1)} collective-permute-done((f32[2,8,8,256]{3,2,1,0:T(8,128)}, f32[2,8,8,256]{3,2,1,0:T(8,128)S(1)}, u32[]{:S(2)}, u32[]{:S(2)}) %collective-permute-start.4) | collective-permute-done | bytes 131104 | tf_op jit(solution)/shard_map/ppermute | solution.py:117
  78.6 1.1 collective-permute-done.5
  79.7 0.9 select_select_fusion
  80.8 1.2 collective-permute-done.10
  82.0 0.8 broadcast_in_dim.70
  82.9 6.6 %all-to-all-start.1 = ((f32[8,8,8,256]{3,2,1,0:T(8,128)}), f32[8,8,8,256]{3,2,1,0:T(8,128)S(1)}, u32[]{:S(2)}, u32[]{:S(2)}) async-start(f32[8,8,8,256]{3,2,1,0:T(8,128)} %broadcast_in_dim.70), calls=%async_computation.1 | async-start | bytes 1048576 | tf_op jit(solution)/shard_map/all_to_all | solution.py:134
  89.5 0.1 select_bitcast_fusion.2
  89.7 0.6 gather_fusion.1
  90.4 0.2 select_bitcast_fusion
  90.7 8.0 %all-to-all-done.1 = f32[8,8,8,256]{3,2,1,0:T(8,128)S(1)} async-done(((f32[8,8,8,256]{3,2,1,0:T(8,128)}), f32[8,8,8,256]{3,2,1,0:T(8,128)S(1)}, u32[]{:S(2)}, u32[]{:S(2)}) %all-to-all-start.1) | async-done | bytes 524320 | tf_op jit(solution)/shard_map/all_to_all | solution.py:134
  98.7 1.9 %fusion.19 = f32[256,512]{1,0:T(8,128)} fusion(f32[512,256]{1,0:T(8,128)S(1)} %bitcast.63, f32[512,512]{1,0:T(8,128)S(1)} %bitcast.61), kind=kOutput, calls=%fused_computation.84 | convolution fusion | flops 805306368 | bytes 2097152 | tf_op jit(solution)/shard_map/dot_general | solution.py:54
  100.6 0.7 collective-permute-start.11
  101.2 4.0 %all-to-all-start.2 = ((f32[4,64,512]{2,1,0:T(8,128)}), f32[4,64,512]{2,1,0:T(8,128)S(1)}, u32[]{:S(2)}, u32[]{:S(2)}) async-start(f32[4,64,512]{2,1,0:T(8,128)} %bitcast.22), calls=%async_computation.2 | async-start | bytes 1048576 | tf_op jit(solution)/shard_map/all_to_all | solution.py:143
  105.2 7.0 %all-to-all-done.2 = f32[4,64,512]{2,1,0:T(8,128)S(1)} async-done(((f32[4,64,512]{2,1,0:T(8,128)}), f32[4,64,512]{2,1,0:T(8,128)S(1)}, u32[]{:S(2)}, u32[]{:S(2)}) %all-to-all-start.2) | async-done | bytes 524320 | tf_op jit(solution)/shard_map/all_to_all | solution.py:143
  112.3 4.2 %collective-permute-start.13 = (f32[64,512]{1,0:T(8,128)S(1)}, f32[64,512]{1,0:T(8,128)S(1)}, u32[]{:S(2)}, u32[]{:S(2)}) collective-permute-start(f32[64,512]{1,0:T(8,128)S(1)} %fusion.23), channel_id=1, source_target_pairs={{0,4},{2,6},{4,0},{6,2},{1,5},{3,7},{5,1},{7,3},{8,12},{10,14},{12... | collective-permute-start | bytes 393224 | tf_op jit(solution)/shard_map/ppermute | solution.py:72
  116.6 2.7 %collective-permute-done.14 = f32[64,512]{1,0:T(8,128)S(1)} collective-permute-done((f32[64,512]{1,0:T(8,128)S(1)}, f32[64,512]{1,0:T(8,128)S(1)}, u32[]{:S(2)}, u32[]{:S(2)}) %collective-permute-start.14) | collective-permute-done | bytes 131104 | tf_op jit(solution)/shard_map/ppermute | solution.py:72
  119.3 2.4 %collective-permute-done.13 = f32[64,512]{1,0:T(8,128)S(1)} collective-permute-done((f32[64,512]{1,0:T(8,128)S(1)}, f32[64,512]{1,0:T(8,128)S(1)}, u32[]{:S(2)}, u32[]{:S(2)}) %collective-permute-start.13) | collective-permute-done | bytes 131104 | tf_op jit(solution)/shard_map/ppermute | solution.py:72
  121.7 4.8 %collective-permute-done.12 = f32[64,512]{1,0:T(8,128)S(1)} collective-permute-done((f32[64,512]{1,0:T(8,128)S(1)}, f32[64,512]{1,0:T(8,128)S(1)}, u32[]{:S(2)}, u32[]{:S(2)}) %collective-permute-start.12) | collective-permute-done | bytes 131104 | tf_op jit(solution)/shard_map/ppermute | solution.py:72
  126.5 0.6 copy-done.2
  127.1 4.4 %collective-permute-start.15 = (f32[4,64,512]{2,1,0:T(8,128)S(1)}, f32[4,64,512]{2,1,0:T(8,128)S(1)}, u32[]{:S(2)}, u32[]{:S(2)}) collective-permute-start(f32[4,64,512]{2,1,0:T(8,128)S(1)} %pad_maximum_fusion.3), channel_id=1, source_target_pairs={{0,1},{1,0},{2,3},{3,2},{4,5},{5,4},{6,7},{7,6},{8,9},{9,8},{10,11... | collective-permute-start | bytes 1572872 | tf_op jit(solution)/shard_map/ppermute | solution.py:149
  131.6 0.1 broadcast_select_fusion.1
  131.7 0.6 gather_fusion.2
  132.3 0.6 gather_fusion.3
  132.9 0.2 collective-permute-done.15
  133.0 1.1 convolution_bitcast_fusion
  134.2 2.1 %fusion = f32[512,512]{1,0:T(8,128)} fusion(f32[512,512]{1,0:T(8,128)S(1)} %convolution_bitcast_fusion, f32[4,64,512]{2,1,0:T(8,128)S(1)} %gather_fusion.2, pred[4]{0:T(512)(128)(4,1)S(1)} %compare_and_fusion, f32[1,64,512]{2,1,0:T(8,128)S(1)} %bitcast.65, f32[1,64,512]{2,1,0:T(8,128)S(1)} %bitcast.67, f32[1,64,512]{2,1,0:T(8,128)S(1)} %bitcast.69, ...), kind=kOutput, calls=%fused_computation.6 | convolution fusion | flops 806092800 | bytes 3145732 | tf_op jit(solution)/shard_map/dot_general | solution.py:54
  136.3 4.1 %all-to-all-start.3 = ((f32[4,128,512]{2,1,0:T(8,128)}), f32[4,128,512]{2,1,0:T(8,128)S(1)}, u32[]{:S(2)}, u32[]{:S(2)}) async-start(f32[4,128,512]{2,1,0:T(8,128)} %bitcast.29), calls=%async_computation.3 | async-start | bytes 2097152 | tf_op jit(solution)/shard_map/all_to_all | solution.py:156
  140.4 3.5 %collective-permute-start.16 = (f32[64,512]{1,0:T(8,128)S(1)}, f32[64,512]{1,0:T(8,128)S(1)}, u32[]{:S(2)}, u32[]{:S(2)}) collective-permute-start(f32[64,512]{1,0:T(8,128)S(1)} %copy-done.6), channel_id=1, source_target_pairs={{0,0},{1,32},{2,64},{3,96},{4,128},{5,160},{6,192},{7,224},{8,8},{... | collective-permute-start | bytes 393224 | tf_op jit(solution)/shard_map/ppermute | solution.py:82
  143.9 3.1 %collective-permute-done.16 = f32[64,512]{1,0:T(8,128)S(1)} collective-permute-done((f32[64,512]{1,0:T(8,128)S(1)}, f32[64,512]{1,0:T(8,128)S(1)}, u32[]{:S(2)}, u32[]{:S(2)}) %collective-permute-start.16) | collective-permute-done | bytes 131104 | tf_op jit(solution)/shard_map/ppermute | solution.py:82
  147.0 8.0 %all-to-all-done.3 = f32[4,128,512]{2,1,0:T(8,128)S(1)} async-done(((f32[4,128,512]{2,1,0:T(8,128)}), f32[4,128,512]{2,1,0:T(8,128)S(1)}, u32[]{:S(2)}, u32[]{:S(2)}) %all-to-all-start.3) | async-done | bytes 1048608 | tf_op jit(solution)/shard_map/all_to_all | solution.py:156
  154.9 0.8 fusion.4
  155.8 0.7 copy.14
  (57 shorter events, 1.5 us)
Async XLA Ops:
  26.4 9.4 %copy-start.7 = (f32[64,512]{1,0:T(8,128)S(1)}, f32[64,512]{1,0:T(8,128)}, u32[]{:S(2)}) copy-start(f32[64,512]{1,0:T(8,128)} %param.8) | copy-start | bytes 393220
  26.4 33.8 %all-to-all-start = ((f32[32,8,768]{2,1,0:T(8,128)}), f32[32,8,768]{2,1,0:T(8,128)S(1)}, u32[]{:S(2)}, u32[]{:S(2)}) async-start(f32[32,8,768]{2,1,0:T(8,128)} %bitcast.62), calls=%async_computation | async-start | bytes 1572864 | tf_op jit(solution)/shard_map/all_to_all | solution.py:104
  35.8 32.1 %collective-permute-start.8 = (f32[64,512]{1,0:T(8,128)S(1)}, f32[64,512]{1,0:T(8,128)S(1)}, u32[]{:S(2)}, u32[]{:S(2)}) collective-permute-start(f32[64,512]{1,0:T(8,128)S(1)} %copy-done.7), channel_id=1, source_target_pairs={{0,128},{64,192},{128,0},{192,64},{1,129},{65,193},{129,1},{193,65... | collective-permute-start | bytes 393224 | tf_op jit(solution)/shard_map/ppermute | solution.py:72
  38.6 16.0 %collective-permute-start.3 = (f32[64,512]{1,0:T(8,128)S(1)}, f32[64,512]{1,0:T(8,128)S(1)}, u32[]{:S(2)}, u32[]{:S(2)}) collective-permute-start(f32[64,512]{1,0:T(8,128)S(1)} %copy-done.7), channel_id=1, source_target_pairs={{0,2},{1,34},{2,66},{3,98},{4,130},{5,162},{6,194},{7,226},{8,10},... | collective-permute-start | bytes 393224 | tf_op jit(solution)/shard_map/ppermute | solution.py:82
  43.9 16.3 %collective-permute-start.2 = (f32[64,512]{1,0:T(8,128)S(1)}, f32[64,512]{1,0:T(8,128)S(1)}, u32[]{:S(2)}, u32[]{:S(2)}) collective-permute-start(f32[64,512]{1,0:T(8,128)S(1)} %copy-done.7), channel_id=1, source_target_pairs={{0,4},{1,36},{2,68},{3,100},{4,132},{5,164},{6,196},{7,228},{8,12}... | collective-permute-start | bytes 393224 | tf_op jit(solution)/shard_map/ppermute | solution.py:82
  46.0 14.2 %collective-permute-start.1 = (f32[64,512]{1,0:T(8,128)S(1)}, f32[64,512]{1,0:T(8,128)S(1)}, u32[]{:S(2)}, u32[]{:S(2)}) collective-permute-start(f32[64,512]{1,0:T(8,128)S(1)} %copy-done.7), channel_id=1, source_target_pairs={{0,6},{1,38},{2,70},{3,102},{4,134},{5,166},{6,198},{7,230},{8,14}... | collective-permute-start | bytes 393224 | tf_op jit(solution)/shard_map/ppermute | solution.py:82
  46.0 14.2 %collective-permute-start = (f32[64,512]{1,0:T(8,128)S(1)}, f32[64,512]{1,0:T(8,128)S(1)}, u32[]{:S(2)}, u32[]{:S(2)}) collective-permute-start(f32[64,512]{1,0:T(8,128)S(1)} %copy-done.7), channel_id=1, source_target_pairs={{0,0},{1,32},{2,64},{3,96},{4,128},{5,160},{6,192},{7,224},{8,8},{... | collective-permute-start | bytes 393224 | tf_op jit(solution)/shard_map/ppermute | solution.py:82
  50.3 0.7 copy-start
  54.6 14.7 %collective-permute-start.7 = (f32[64,512]{1,0:T(8,128)S(1)}, f32[64,512]{1,0:T(8,128)S(1)}, u32[]{:S(2)}, u32[]{:S(2)}) collective-permute-start(f32[64,512]{1,0:T(8,128)S(1)} %copy-done.7), channel_id=1, source_target_pairs={{0,64},{64,128},{128,192},{192,0},{1,65},{65,129},{129,193},{193,1... | collective-permute-start | bytes 393224 | tf_op jit(solution)/shard_map/ppermute | solution.py:72
  60.2 9.1 %collective-permute-start.9 = (f32[64,512]{1,0:T(8,128)S(1)}, f32[64,512]{1,0:T(8,128)S(1)}, u32[]{:S(2)}, u32[]{:S(2)}) collective-permute-start(f32[64,512]{1,0:T(8,128)S(1)} %copy-done.7), channel_id=1, source_target_pairs={{0,192},{64,0},{128,64},{192,128},{1,193},{65,1},{129,65},{193,129... | collective-permute-start | bytes 393224 | tf_op jit(solution)/shard_map/ppermute | solution.py:72
  60.2 4.4 %copy-start.1 = (f32[32,8,768]{2,1,0:T(8,128)}, f32[32,8,768]{2,1,0:T(8,128)S(1)}, u32[]{:S(2)}) copy-start(f32[32,8,768]{2,1,0:T(8,128)S(1)} %all-to-all-done.pieces) | copy-start | bytes 2359300
  60.3 19.5 %collective-permute-start.6 = (f32[4,64,512]{2,1,0:T(8,128)S(1)}, f32[4,64,512]{2,1,0:T(8,128)S(1)}, u32[]{:S(2)}, u32[]{:S(2)}) collective-permute-start(f32[4,64,512]{2,1,0:T(8,128)S(1)} %pad_maximum_fusion.1), channel_id=1, source_target_pairs={{0,1},{1,0},{2,3},{3,2},{4,5},{5,4},{6,7},{7,6},{8,9},{9,8},{10,11... | collective-permute-start | bytes 1572872 | tf_op jit(solution)/shard_map/ppermute | solution.py:120
  66.6 12.0 %collective-permute-start.4 = (f32[2,8,8,256]{3,2,1,0:T(8,128)}, f32[2,8,8,256]{3,2,1,0:T(8,128)S(1)}, u32[]{:S(2)}, u32[]{:S(2)}) collective-permute-start(f32[2,8,8,256]{3,2,1,0:T(8,128)} %get-tuple-element.29), channel_id=1, source_target_pairs={{7,5},{6,4},{5,3},{3,1},{2,0},{15,13},{14,12},{13,11},{11,9},{10,8... | collective-permute-start | bytes 393224 | tf_op jit(solution)/shard_map/ppermute | solution.py:117
  67.9 11.8 %collective-permute-start.5 = (f32[2,8,8,256]{3,2,1,0:T(8,128)}, f32[2,8,8,256]{3,2,1,0:T(8,128)S(1)}, u32[]{:S(2)}, u32[]{:S(2)}) collective-permute-start(f32[2,8,8,256]{3,2,1,0:T(8,128)} %get-tuple-element.30), channel_id=1, source_target_pairs={{6,2},{5,1},{4,0},{14,10},{13,9},{12,8},{22,18},{21,17},{20,16},{3... | collective-permute-start | bytes 393224 | tf_op jit(solution)/shard_map/ppermute | solution.py:118
  80.7 1.3 collective-permute-start.10
  82.9 15.9 %all-to-all-start.1 = ((f32[8,8,8,256]{3,2,1,0:T(8,128)}), f32[8,8,8,256]{3,2,1,0:T(8,128)S(1)}, u32[]{:S(2)}, u32[]{:S(2)}) async-start(f32[8,8,8,256]{3,2,1,0:T(8,128)} %broadcast_in_dim.70), calls=%async_computation.1 | async-start | bytes 1048576 | tf_op jit(solution)/shard_map/all_to_all | solution.py:134
  100.6 11.6 %collective-permute-start.11 = (f32[4,64,512]{2,1,0:T(8,128)S(1)}, f32[4,64,512]{2,1,0:T(8,128)S(1)}, u32[]{:S(2)}, u32[]{:S(2)}) collective-permute-start(f32[4,64,512]{2,1,0:T(8,128)S(1)} %pad_maximum_fusion.2), channel_id=1, source_target_pairs={{0,32},{32,0},{1,33},{33,1},{2,34},{34,2},{3,35},{35,3},{4,36},{36... | collective-permute-start | bytes 1572872 | tf_op jit(solution)/shard_map/ppermute | solution.py:144
  101.2 11.0 %all-to-all-start.2 = ((f32[4,64,512]{2,1,0:T(8,128)}), f32[4,64,512]{2,1,0:T(8,128)S(1)}, u32[]{:S(2)}, u32[]{:S(2)}) async-start(f32[4,64,512]{2,1,0:T(8,128)} %bitcast.22), calls=%async_computation.2 | async-start | bytes 1048576 | tf_op jit(solution)/shard_map/all_to_all | solution.py:143
  112.2 4.3 %copy-start.5 = (f32[64,512]{1,0:T(8,128)}, f32[64,512]{1,0:T(8,128)S(1)}, u32[]{:S(2)}) copy-start(f32[64,512]{1,0:T(8,128)S(1)} %fusion.23) | copy-start | bytes 393220
  112.3 7.0 %collective-permute-start.14 = (f32[64,512]{1,0:T(8,128)S(1)}, f32[64,512]{1,0:T(8,128)S(1)}, u32[]{:S(2)}, u32[]{:S(2)}) collective-permute-start(f32[64,512]{1,0:T(8,128)S(1)} %fusion.23), channel_id=1, source_target_pairs={{0,6},{2,0},{4,2},{6,4},{1,7},{3,1},{5,3},{7,5},{8,14},{10,8},{12,... | collective-permute-start | bytes 393224 | tf_op jit(solution)/shard_map/ppermute | solution.py:72
  112.3 9.3 %collective-permute-start.13 = (f32[64,512]{1,0:T(8,128)S(1)}, f32[64,512]{1,0:T(8,128)S(1)}, u32[]{:S(2)}, u32[]{:S(2)}) collective-permute-start(f32[64,512]{1,0:T(8,128)S(1)} %fusion.23), channel_id=1, source_target_pairs={{0,4},{2,6},{4,0},{6,2},{1,5},{3,7},{5,1},{7,3},{8,12},{10,14},{12... | collective-permute-start | bytes 393224 | tf_op jit(solution)/shard_map/ppermute | solution.py:72
  116.5 9.9 %collective-permute-start.12 = (f32[64,512]{1,0:T(8,128)S(1)}, f32[64,512]{1,0:T(8,128)S(1)}, u32[]{:S(2)}, u32[]{:S(2)}) collective-permute-start(f32[64,512]{1,0:T(8,128)S(1)} %fusion.23), channel_id=1, source_target_pairs={{0,2},{2,4},{4,6},{6,0},{1,3},{3,5},{5,7},{7,1},{8,10},{10,12},{12... | collective-permute-start | bytes 393224 | tf_op jit(solution)/shard_map/ppermute | solution.py:72
  126.4 0.7 copy-start.2
  127.1 6.0 %collective-permute-start.15 = (f32[4,64,512]{2,1,0:T(8,128)S(1)}, f32[4,64,512]{2,1,0:T(8,128)S(1)}, u32[]{:S(2)}, u32[]{:S(2)}) collective-permute-start(f32[4,64,512]{2,1,0:T(8,128)S(1)} %pad_maximum_fusion.3), channel_id=1, source_target_pairs={{0,1},{1,0},{2,3},{3,2},{4,5},{5,4},{6,7},{7,6},{8,9},{9,8},{10,11... | collective-permute-start | bytes 1572872 | tf_op jit(solution)/shard_map/ppermute | solution.py:149
  132.9 1.3 copy-start.3
  136.3 4.1 %copy-start.6 = (f32[64,512]{1,0:T(8,128)S(1)}, f32[64,512]{1,0:T(8,128)}, u32[]{:S(2)}) copy-start(f32[64,512]{1,0:T(8,128)} %copy-done.5) | copy-start | bytes 393220
  136.3 18.6 %copy-start.4 = (f32[128,512]{1,0:T(8,128)S(1)}, f32[128,512]{1,0:T(8,128)}, u32[]{:S(2)}) copy-start(f32[128,512]{1,0:T(8,128)} %param.9) | copy-start | bytes 786436
  136.3 18.6 %all-to-all-start.3 = ((f32[4,128,512]{2,1,0:T(8,128)}), f32[4,128,512]{2,1,0:T(8,128)S(1)}, u32[]{:S(2)}, u32[]{:S(2)}) async-start(f32[4,128,512]{2,1,0:T(8,128)} %bitcast.29), calls=%async_computation.3 | async-start | bytes 2097152 | tf_op jit(solution)/shard_map/all_to_all | solution.py:156
  140.4 6.6 %collective-permute-start.16 = (f32[64,512]{1,0:T(8,128)S(1)}, f32[64,512]{1,0:T(8,128)S(1)}, u32[]{:S(2)}, u32[]{:S(2)}) collective-permute-start(f32[64,512]{1,0:T(8,128)S(1)} %copy-done.6), channel_id=1, source_target_pairs={{0,0},{1,32},{2,64},{3,96},{4,128},{5,160},{6,192},{7,224},{8,8},{... | collective-permute-start | bytes 393224 | tf_op jit(solution)/shard_map/ppermute | solution.py:82

commit v4 on v3

v4 whole, which is shorter than its diff:
```python
import jax
import jax.numpy as jnp
from jax import lax
from jax.experimental import pallas as pl
from jax.experimental.pallas import tpu as pltpu
from jax.sharding import Mesh, PartitionSpec as P

BLK = 128
AXES = ("x", "zl", "y", "zh", "core")
SIZES = (4, 2, 4, 4, 2)
CLASSED = ("y", "x", "zl")
ROWS = ("x", "zl", "y")
COLS = ("zh", "core")
GROUP = ("x", "zl")
SWAP = [(0, 1), (1, 0)]
HI = lax.Precision.HIGHEST


def class_kernel(structure, root, out):
    row_dev = (lax.axis_index("x") * 2 + lax.axis_index("zl")) * 4 + lax.axis_index("y")
    place = []
    for k in range(3):
        half = row_dev * 3 + k
        tile = half // 2
        before = jnp.int32(0)
        member = jnp.int32(0)
        for i in range(16):
            before += (structure[i] < tile).astype(jnp.int32)
            member += (structure[i] == tile).astype(jnp.int32)
        place.append(jnp.where(member > 0, (2 * before + half % 2) % 4, -1))
    for y in range(4):
        k = jnp.where(place[1] == y, 1, jnp.where(place[2] == y, 2, 0))
        out[y] = root[pl.ds(pl.multiple_of(k * 64, 64), 64), :]


def cut_kernel(structure, pieces, *outs):
    zh, y = lax.axis_index("zh"), lax.axis_index("y")
    for k, out in enumerate(outs):
        for core in range(2):
            half = 2 * structure[2 * ((zh + k) % 4 * 2 + core) + y // 2] + y % 2
            source = half // 3
            out[core] = pieces[source % 4 * 8 + source // 4]


def columns_kernel(structure, own, one, two, three, got, out):
    zh, core, y = lax.axis_index("zh"), lax.axis_index("core"), lax.axis_index("y")
    for side in range(2):
        for k in range(4):
            group = (zh + k) % 4 * 2 + (core if side == 0 else 1 - core)
            tiles = []
            for t in range(2):
                tile = structure[2 * group + t]
                holder = tile // 6
                hop = (zh - holder // 2 + 4) % 4
                column = pl.multiple_of(tile % 6 * BLK, BLK)
                there = got[hop, :, pl.ds(column, BLK)]
                here = [ref[core, :, pl.ds(column, BLK)] for ref in (own, one, two, three)]
                here = jnp.where(hop == 0, here[0], jnp.where(hop == 1, here[1], jnp.where(hop == 2, here[2], here[3])))
                tiles.append(jnp.where(holder % 2 == core, here, there))
            pair = jnp.concatenate(tiles, axis=1)
            pair = pltpu.roll(pair, (4 - y) % 4 * 64, 1)
            out[:, (side * 4 + k) * 256:(side * 4 + k + 1) * 256] = pair


def dot(first, second, axis):
    return lax.dot_general(
        first, second, (((axis,), (0,)), ((), ())), precision=HI, preferred_element_type=jnp.float32
    )


def vmem():
    return pl.BlockSpec(memory_space=pltpu.VMEM)


def smem():
    return pl.BlockSpec(memory_space=pltpu.SMEM)


def anywhere():
    return pl.BlockSpec(memory_space=pl.ANY)


def shift(block, axis, k):
    return lax.ppermute(block, axis, [(i, (i + k) % 4) for i in range(4)])


def turn(block, k):
    pairs = []
    for a in range(8):
        for b in range(4):
            for c in range(8):
                target = (a // 2 - k) % 4 * 2 + a % 2
                pairs.append(((a * 4 + b) * 8 + c, (c * 4 + b) * 8 + target))
    return lax.ppermute(block, AXES, pairs)


def at(array, index, axis=0):
    return lax.dynamic_index_in_dim(array, index, axis, keepdims=False)


def call(kernel, shapes, structure, *operands):
    return pl.pallas_call(
        kernel,
        out_shape=shapes,
        in_specs=[smem()] + [vmem()] * len(operands),
        out_specs=jax.tree.map(lambda _: vmem(), shapes),
    )(structure, *operands)


def of(*shape):
    return jax.ShapeDtypeStruct(shape, jnp.float32)


def per_device(root_cov, structure, child_factor, child_diag):
    x, zl = lax.axis_index("x"), lax.axis_index("zl")
    zh, core = lax.axis_index("zh"), lax.axis_index("core")
    fours = lax.iota(jnp.int32, 4)

    sends = call(class_kernel, of(4, 64, 768), structure, root_cov)
    turned = [turn(child_factor, k) for k in range(4)]
    pieces = lax.all_to_all(sends.reshape(32, 8, 768), CLASSED, 0, 0)
    pieces, turned, factor = lax.optimization_barrier((pieces, turned, child_factor))

    cut = call(cut_kernel, [of(2, 8, 768)] * 4, structure, pieces)
    landed = [cut[0]] + [shift(cut[k], "zh", k) for k in (1, 2, 3)]
    give = jnp.stack([at(part, 1 - core) for part in landed])
    got = lax.ppermute(give, "core", SWAP)
    piece = call(columns_kernel, of(8, 2048), structure, *landed, got)
    other = lax.ppermute(factor, "zl", SWAP)

    rows = lax.all_to_all(jnp.broadcast_to(piece[None], (8, 8, 2048)), GROUP, 0, 0).reshape(64, 2048)

    turned = jnp.stack(turned)
    near = [turned] + [shift(turned, "y", -k) for k in (1, 2, 3)]
    far = [lax.ppermute(part, "core", SWAP) for part in near]
    near = jnp.stack(near, axis=1).reshape(1024, 512)
    far = jnp.stack(far, axis=1).reshape(1024, 512)

    cross = -(dot(rows[:, :1024], near, 1) + dot(rows[:, 1024:], far, 1))
    cross, factor, other = lax.optimization_barrier((cross, factor, other))

    near = jnp.stack([cross] + [shift(cross, "zh", -k) for k in (1, 2, 3)])
    far = lax.ppermute(near, "core", SWAP)
    pair = jnp.stack([jnp.where(zl == core, factor, other), jnp.where(zl == core, other, factor)])
    pairs = jnp.stack([pair] + [shift(pair, "x", -k) for k in (1, 2, 3)])
    pairs = jnp.take(pairs, (zh - x + fours) % 4, axis=0)
    share = dot(near.reshape(256, 512), pairs[:, 0].reshape(256, 512), 0)
    share = share + dot(far.reshape(256, 512), pairs[:, 1].reshape(256, 512), 0)
    share, cross = lax.optimization_barrier((share, cross))
    got = lax.all_to_all(share.reshape(4, 128, 512), "y", 0, 0)
    child = child_diag - (got[0] + got[1] + got[2] + got[3])
    return turn(cross, 0), child


def solution(mesh):
    fine = Mesh(mesh.devices.reshape(SIZES), AXES)
    spec = P(ROWS, COLS)
    return jax.shard_map(
        per_device,
        mesh=fine,
        in_specs=(spec, P(), spec, spec),
        out_specs=(spec, spec),
        check_vma=False,
    )
```

time: 158 us -> 131 us (0.83)
  Pallas kernels: 27.7 us -> 6.16 us
  waiting for transfers between devices: 50.8 us -> 38.5 us
  starting transfers between devices: 62.6 us -> 67 us
  other arithmetic: 3.38 us -> 5.76 us
  matrix products: 5.09 us -> 7.4 us
    pallas_call x2 -> x3, Pallas kernels: 27.7 us -> 6.16 us  [call(): pl.pallas_call(kernel, out_shape=shapes, in_specs=[smem()] + [vmem()] * l...]
    all_to_all x2 -> x1, waiting for transfers between devices: 15 us -> 1.35 us  [per_device(): lax.all_to_all(jnp.broadcast_to(piece[None], (8, 8, 2048)), GROUP, 0, 0)]
    ppermute x6 -> x12, starting transfers between devices: 12.1 us -> 24.2 us  [shift(): return lax.ppermute(block, axis, [(i, (i + k) % 4) for i in range(4)])]
    ppermute x3 -> x5, waiting for transfers between devices: 10.4 us -> 0.01 us  [the longest x4 0.01 us: per_device(): far = [lax.ppermute(part, 'core', SWAP) for part in near]]
    ppermute x5, waiting for transfers between devices: 6.15 us -> 13.1 us  [turn(): return lax.ppermute(block, AXES, pairs)]
    all_to_all x2 -> x1, starting transfers between devices: 10.6 us -> 3.97 us  [per_device(): lax.all_to_all(jnp.broadcast_to(piece[None], (8, 8, 2048)), GROUP, 0, 0)]
    ppermute x6 -> x12, waiting for transfers between devices: 9.86 us -> 16.2 us  [shift(): return lax.ppermute(block, axis, [(i, (i + k) % 4) for i in range(4)])]
    ppermute x2 -> x1, starting transfers between devices: 7.92 us -> 2.36 us  [per_device(): far = lax.ppermute(near, 'core', SWAP)]
  transfers between devices with their start and end apart: 21 -> 27, of which waited for: 13 -> 12; matrix products, arithmetic and copies ran while one was open for 3% -> 10% of each run, Pallas kernels for 1% -> 3%
where the time goes in v4:
time: 131 us; the launch traced here: 130 us
  starting transfers between devices  67 us (51%)
  waiting for transfers between devices  38.5 us (29%)
  matrix products  7.4 us (6%)
  Pallas kernels  6.16 us (5%)
  other arithmetic  5.76 us (4%)
  local copies, waits for them, and re-layouts  4.63 us (4%)
    ppermute x12, starting transfers between devices, shift(): return lax.ppermute(block, axis, [(i, (i + k) % 4) for i in range(4)])  24.2 us
    ppermute x5, starting transfers between devices, turn(): return lax.ppermute(block, AXES, pairs)  18.6 us
    ppermute x12, waiting for transfers between devices, shift(): return lax.ppermute(block, axis, [(i, (i + k) % 4) for i in range(4)])  16.2 us
    ppermute x5, waiting for transfers between devices, turn(): return lax.ppermute(block, AXES, pairs)  13.1 us
    all_to_all x1, starting transfers between devices, per_device(): pieces = lax.all_to_all(sends.reshape(32, 8, 768), CLASSED, 0, 0)  9.23 us
    dot_general x4, matrix products, dot(): lax.dot_general(first, second, (((axis,), (0,)), ((), ())), precision=HI,...  7.4 us
    all_to_all x1, waiting for transfers between devices, per_device(): got = lax.all_to_all(share.reshape(4, 128, 512), 'y', 0, 0)  6.45 us
    pallas_call x3, Pallas kernels, call(): pl.pallas_call(kernel, out_shape=shapes, in_specs=[smem()] + [vmem()] * l...  6.16 us
  transfers between devices with their start and end apart: 27, of which 12 were waited for; matrix products, arithmetic and copies ran while one was open for 10% of the time, Pallas kernels for 3%

profile of v4, /device:TPU:1, one launch (start us, length us, event | category | flops | bytes accessed | tf_op | source)
XLA Modules:
  0.0 130.3 jit_solution(17858984930738144134)
XLA Ops:
  0.6 2.2 %shard_map.59 = f32[4,64,768]{2,1,0:T(8,128)} custom-call(s32[16]{0:T(128)} %structure.5, f32[192,768]{1,0:T(8,128)} %root.1), custom_call_target="tpu_custom_call" | custom-call | tf_op jit(solution)/shard_map/pallas_call | solution.py:102
  2.8 9.2 %all-to-all-start = ((f32[32,8,768]{2,1,0:T(8,128)}), f32[32,8,768]{2,1,0:T(8,128)S(1)}, u32[]{:S(2)}, u32[]{:S(2)}) async-start(f32[32,8,768]{2,1,0:T(8,128)} %bitcast.55), calls=%async_computation | async-start | bytes 1572864 | tf_op jit(solution)/shard_map/all_to_all | solution.py:121
  12.0 4.3 %collective-permute-start = (f32[64,512]{1,0:T(8,128)S(1)}, f32[64,512]{1,0:T(8,128)S(1)}, u32[]{:S(2)}, u32[]{:S(2)}) collective-permute-start(f32[64,512]{1,0:T(8,128)S(1)} %copy-done.2), channel_id=1, source_target_pairs={{0,0},{1,32},{2,64},{3,96},{4,128},{5,160},{6,192},{7,224},{8,8},{... | collective-permute-start | bytes 393224 | tf_op jit(solution)/shard_map/ppermute | solution.py:94
  16.3 4.0 %collective-permute-start.1 = (f32[64,512]{1,0:T(8,128)S(1)}, f32[64,512]{1,0:T(8,128)S(1)}, u32[]{:S(2)}, u32[]{:S(2)}) collective-permute-start(f32[64,512]{1,0:T(8,128)S(1)} %copy-done.2), channel_id=1, source_target_pairs={{0,6},{1,38},{2,70},{3,102},{4,134},{5,166},{6,198},{7,230},{8,14}... | collective-permute-start | bytes 393224 | tf_op jit(solution)/shard_map/ppermute | solution.py:94
  20.3 5.6 %collective-permute-start.2 = (f32[64,512]{1,0:T(8,128)S(1)}, f32[64,512]{1,0:T(8,128)S(1)}, u32[]{:S(2)}, u32[]{:S(2)}) collective-permute-start(f32[64,512]{1,0:T(8,128)S(1)} %copy-done.2), channel_id=1, source_target_pairs={{0,4},{1,36},{2,68},{3,100},{4,132},{5,164},{6,196},{7,228},{8,12}... | collective-permute-start | bytes 393224 | tf_op jit(solution)/shard_map/ppermute | solution.py:94
  26.0 1.2 collective-permute-start.3
  27.2 1.7 %collective-permute-done = f32[64,512]{1,0:T(8,128)S(1)} collective-permute-done((f32[64,512]{1,0:T(8,128)S(1)}, f32[64,512]{1,0:T(8,128)S(1)}, u32[]{:S(2)}, u32[]{:S(2)}) %collective-permute-start) | collective-permute-done | bytes 131104 | tf_op jit(solution)/shard_map/ppermute | solution.py:94
  28.9 2.3 %collective-permute-done.2 = f32[64,512]{1,0:T(8,128)S(1)} collective-permute-done((f32[64,512]{1,0:T(8,128)S(1)}, f32[64,512]{1,0:T(8,128)S(1)}, u32[]{:S(2)}, u32[]{:S(2)}) %collective-permute-start.2) | collective-permute-done | bytes 131104 | tf_op jit(solution)/shard_map/ppermute | solution.py:94
  31.3 4.1 %collective-permute-done.3 = f32[64,512]{1,0:T(8,128)S(1)} collective-permute-done((f32[64,512]{1,0:T(8,128)S(1)}, f32[64,512]{1,0:T(8,128)S(1)}, u32[]{:S(2)}, u32[]{:S(2)}) %collective-permute-start.3) | collective-permute-done | bytes 131104 | tf_op jit(solution)/shard_map/ppermute | solution.py:94
  35.5 2.9 %collective-permute-start.9 = (f32[4,64,512]{2,1,0:T(8,128)S(1)}, f32[4,64,512]{2,1,0:T(8,128)S(1)}, u32[]{:S(2)}, u32[]{:S(2)}) collective-permute-start(f32[4,64,512]{2,1,0:T(8,128)S(1)} %get-tuple-element.35), channel_id=1, source_target_pairs={{0,16},{8,24},{16,0},{24,8},{1,17},{9,25},{17,1},{25,9},{2,18},{10... | collective-permute-start | bytes 1572872 | tf_op jit(solution)/shard_map/ppermute | solution.py:84
  38.7 2.3 %collective-permute-start.8 = (f32[4,64,512]{2,1,0:T(8,128)S(1)}, f32[4,64,512]{2,1,0:T(8,128)}, u32[]{:S(2)}, u32[]{:S(2)}) collective-permute-start(f32[4,64,512]{2,1,0:T(8,128)S(1)} %get-tuple-element.35), channel_id=1, source_target_pairs={{0,24},{8,0},{16,8},{24,16},{1,25},{9,1},{17,9},{25,17},{2,26},{10... | collective-permute-start | bytes 1572872 | tf_op jit(solution)/shard_map/ppermute | solution.py:84
  41.0 1.9 %shard_map.60 = (f32[2,8,768]{2,1,0:T(8,128)}, f32[2,8,768]{2,1,0:T(8,128)}, f32[2,8,768]{2,1,0:T(8,128)}, f32[2,8,768]{2,1,0:T(8,128)}) custom-call(s32[16]{0:T(128)} %structure.5, f32[32,8,768]{2,1,0:T(8,128)} %copy-done), custom_call_target="tpu_custom_call" | custom-call | tf_op jit(solution)/shard_map/pallas_call | solution.py:102
  42.9 3.2 %collective-permute-start.6 = (f32[2,8,768]{2,1,0:T(8,128)}, f32[2,8,768]{2,1,0:T(8,128)S(1)}, u32[]{:S(2)}, u32[]{:S(2)}) collective-permute-start(f32[2,8,768]{2,1,0:T(8,128)} %get-tuple-element.21), channel_id=1, source_target_pairs={{0,6},{2,0},{4,2},{6,4},{1,7},{3,1},{5,3},{7,5},{8,14},{10,8},{12,... | collective-permute-start | bytes 147464 | tf_op jit(solution)/shard_map/ppermute | solution.py:84
  46.1 5.6 %collective-permute-start.5 = (f32[2,8,768]{2,1,0:T(8,128)}, f32[2,8,768]{2,1,0:T(8,128)S(1)}, u32[]{:S(2)}, u32[]{:S(2)}) collective-permute-start(f32[2,8,768]{2,1,0:T(8,128)} %get-tuple-element.20), channel_id=1, source_target_pairs={{0,4},{2,6},{4,0},{6,2},{1,5},{3,7},{5,1},{7,3},{8,12},{10,14},{12... | collective-permute-start | bytes 147464 | tf_op jit(solution)/shard_map/ppermute | solution.py:84
  51.7 0.7 constant_dynamic-slice_fusion.3
  52.5 1.5 %collective-permute-start.4 = (f32[2,8,768]{2,1,0:T(8,128)}, f32[2,8,768]{2,1,0:T(8,128)S(1)}, u32[]{:S(2)}, u32[]{:S(2)}) collective-permute-start(f32[2,8,768]{2,1,0:T(8,128)} %get-tuple-element.19), channel_id=1, source_target_pairs={{0,2},{2,4},{4,6},{6,0},{1,3},{3,5},{5,7},{7,1},{8,10},{10,12},{12... | collective-permute-start | bytes 147464 | tf_op jit(solution)/shard_map/ppermute | solution.py:84
  54.0 4.3 %collective-permute-done.4.one = f32[2,8,768]{2,1,0:T(8,128)S(1)} collective-permute-done((f32[2,8,768]{2,1,0:T(8,128)}, f32[2,8,768]{2,1,0:T(8,128)S(1)}, u32[]{:S(2)}, u32[]{:S(2)}) %collective-permute-start.4) | collective-permute-done | bytes 49184 | tf_op jit(solution)/shard_map/ppermute | solution.py:84
  58.4 1.8 %collective-permute-start.7 = (f32[4,8,768]{2,1,0:T(8,128)S(1)}, f32[4,8,768]{2,1,0:T(8,128)S(1)}, u32[]{:S(2)}, u32[]{:S(2)}) collective-permute-start(f32[4,8,768]{2,1,0:T(8,128)S(1)} %pad_maximum_fusion.6), channel_id=1, source_target_pairs={{0,1},{1,0},{2,3},{3,2},{4,5},{5,4},{6,7},{7,6},{8,9},{9,8},{10,11... | collective-permute-start | bytes 294920 | tf_op jit(solution)/shard_map/ppermute | solution.py:127
  60.2 0.9 collective-permute-done.7.got
  61.2 0.6 copy-done.6
  61.8 2.1 %shard_map.61 = f32[8,2048]{1,0:T(8,128)} custom-call(s32[16]{0:T(128)} %structure.5, f32[2,8,768]{2,1,0:T(8,128)} %get-tuple-element.18.own, f32[2,8,768]{2,1,0:T(8,128)} %copy-done.5, f32[2,8,768]{2,1,0:T(8,128)} %copy-done.4, f32[2,8,768]{2,1,0:T(8,128)} %copy-done.3, f32[4,8,768]{2,1,0:T(8,128)} %copy-done.6), custom_call_target="tpu_custom_call" | custom-call | tf_op jit(solution)/shard_map/pallas_call | solution.py:102
  63.9 1.7 %broadcast_in_dim.16 = f32[8,8,2048]{2,1,0:T(8,128)} broadcast(f32[8,2048]{1,0:T(8,128)} %shard_map.61), dimensions={1,2} | broadcast | bytes 589824 | tf_op jit(solution)/shard_map/broadcast_in_dim | solution.py:131
  65.6 4.0 %all-to-all-start.1 = ((f32[8,8,2048]{2,1,0:T(8,128)}), f32[8,8,2048]{2,1,0:T(8,128)S(1)}, u32[]{:S(2)}, u32[]{:S(2)}) async-start(f32[8,8,2048]{2,1,0:T(8,128)} %broadcast_in_dim.16), calls=%async_computation.1 | async-start | bytes 1048576 | tf_op jit(solution)/shard_map/all_to_all | solution.py:131
  69.5 0.6 collective-permute-start.11
  70.8 2.0 %collective-permute-start.15 = (f32[64,512]{1,0:T(8,128)S(1)}, f32[64,512]{1,0:T(8,128)S(1)}, u32[]{:S(2)}, u32[]{:S(2)}) collective-permute-start(f32[64,512]{1,0:T(8,128)S(1)} %copy-done.2), channel_id=1, source_target_pairs={{0,32},{32,0},{1,33},{33,1},{2,34},{34,2},{3,35},{35,3},{4,36},{36... | collective-permute-start | bytes 393224 | tf_op jit(solution)/shard_map/ppermute | solution.py:129
  72.8 2.8 %pad_maximum_fusion = f32[4,4,64,512]{3,2,1,0:T(8,128)} fusion(f32[4,1,64,512]{3,2,1,0:T(8,128)} %bitcast.12, f32[4,1,64,512]{3,2,1,0:T(8,128)S(1)} %bitcast.63, f32[4,1,64,512]{3,2,1,0:T(8,128)} %bitcast.9, f32[4,1,64,512]{3,2,1,0:T(8,128)S(1)} %get-tuple-element.34), kind=kLoop, calls=%fused_computation.1 | loop fusion | flops 1572864 | bytes 4194304 | tf_op jit(solution)/shard_map/stack | solution.py:136
  75.6 1.6 %pad_maximum_fusion.1 = f32[4,4,64,512]{3,2,0,1:T(8,128)S(1)} fusion(f32[4,1,64,512]{3,2,0,1:T(8,128)} %bitcast.17, f32[4,1,64,512]{3,2,0,1:T(8,128)} %bitcast.16, f32[4,1,64,512]{3,2,0,1:T(8,128)} %bitcast.15, f32[4,1,64,512]{3,2,0,1:T(8,128)S(1)} %bitcast.64), kind=kLoop, calls=%fused_computation.2 | loop fusion | flops 1572864 | bytes 4194304 | tf_op jit(solution)/shard_map/stack | solution.py:137
  77.4 1.3 %all-to-all-done.1 = f32[8,8,2048]{2,1,0:T(8,128)S(1)} async-done(((f32[8,8,2048]{2,1,0:T(8,128)}), f32[8,8,2048]{2,1,0:T(8,128)S(1)}, u32[]{:S(2)}, u32[]{:S(2)}) %all-to-all-start.1) | async-done | bytes 524320 | tf_op jit(solution)/shard_map/all_to_all | solution.py:131
  78.8 3.0 %fusion.10 = f32[64,512]{1,0:T(8,128)S(1)} fusion(f32[1024,512]{1,0:T(8,128)} %bitcast.54, f32[64,2048]{1,0:T(8,128)S(1)} %bitcast.56), kind=kOutput, calls=%fused_computation.17 | convolution fusion | flops 402653184 | bytes 2490368 | tf_op jit(solution)/shard_map/dot_general | solution.py:66
  81.8 1.4 %fusion.7 = f32[64,512]{1,0:T(8,128)S(1)} fusion(f32[64,512]{1,0:T(8,128)S(1)} %fusion.10, f32[1024,512]{1,0:T(8,128)S(1)} %bitcast.53, f32[64,2048]{1,0:T(8,128)S(1)} %bitcast.57), kind=kOutput, calls=%fused_computation.16 | convolution fusion | flops 402718720 | bytes 2621440 | tf_op jit(solution)/shard_map/dot_general | solution.py:66
  83.1 2.5 %collective-permute-start.16 = (f32[64,512]{1,0:T(8,128)S(1)}, f32[64,512]{1,0:T(8,128)S(1)}, u32[]{:S(2)}, u32[]{:S(2)}) collective-permute-start(f32[64,512]{1,0:T(8,128)S(1)} %fusion.7), channel_id=1, source_target_pairs={{0,6},{2,0},{4,2},{6,4},{1,7},{3,1},{5,3},{7,5},{8,14},{10,8},{12,... | collective-permute-start | bytes 393224 | tf_op jit(solution)/shard_map/ppermute | solution.py:84
  85.7 0.9 collective-permute-start.19
  86.9 0.6 collective-permute-start.21
  87.5 3.6 %collective-permute-start.17 = (f32[64,512]{1,0:T(8,128)S(1)}, f32[64,512]{1,0:T(8,128)S(1)}, u32[]{:S(2)}, u32[]{:S(2)}) collective-permute-start(f32[64,512]{1,0:T(8,128)S(1)} %fusion.7), channel_id=1, source_target_pairs={{0,4},{2,6},{4,0},{6,2},{1,5},{3,7},{5,1},{7,3},{8,12},{10,14},{12... | collective-permute-start | bytes 393224 | tf_op jit(solution)/shard_map/ppermute | solution.py:84
  91.1 0.8 collective-permute-done.16
  91.9 0.5 collective-permute-start.18
  92.4 4.4 %collective-permute-done.17 = f32[64,512]{1,0:T(8,128)S(1)} collective-permute-done((f32[64,512]{1,0:T(8,128)S(1)}, f32[64,512]{1,0:T(8,128)S(1)}, u32[]{:S(2)}, u32[]{:S(2)}) %collective-permute-start.17) | collective-permute-done | bytes 131104 | tf_op jit(solution)/shard_map/ppermute | solution.py:84
  96.8 6.6 %collective-permute-done.18 = f32[64,512]{1,0:T(8,128)S(1)} collective-permute-done((f32[64,512]{1,0:T(8,128)S(1)}, f32[64,512]{1,0:T(8,128)S(1)}, u32[]{:S(2)}, u32[]{:S(2)}) %collective-permute-start.18) | collective-permute-done | bytes 131104 | tf_op jit(solution)/shard_map/ppermute | solution.py:84
  103.5 2.4 %collective-permute-start.22 = (f32[4,64,512]{2,1,0:T(8,128)S(1)}, f32[4,64,512]{2,1,0:T(8,128)S(1)}, u32[]{:S(2)}, u32[]{:S(2)}) collective-permute-start(f32[4,64,512]{2,1,0:T(8,128)S(1)} %pad_maximum_fusion.4), channel_id=1, source_target_pairs={{0,1},{1,0},{2,3},{3,2},{4,5},{5,4},{6,7},{7,6},{8,9},{9,8},{10,11... | collective-permute-start | bytes 1572872 | tf_op jit(solution)/shard_map/ppermute | solution.py:143
  106.0 0.6 gather_fusion
  107.4 1.0 fusion.18
  108.4 2.0 %convolution_add_fusion = f32[512,512]{1,0:T(8,128)} fusion(f32[512,512]{1,0:T(8,128)S(1)} %fusion.18, f32[256,512]{1,0:T(8,128)S(1)} %bitcast.58, f32[256,512]{1,0:T(8,128)S(1)} %bitcast.59), kind=kOutput, calls=%fused_computation.3 | convolution fusion | flops 805568512 | bytes 3145728 | tf_op jit(solution)/shard_map/dot_general | solution.py:66
  110.5 3.5 %all-to-all-start.2 = ((f32[4,128,512]{2,1,0:T(8,128)}), f32[4,128,512]{2,1,0:T(8,128)S(1)}, u32[]{:S(2)}, u32[]{:S(2)}) async-start(f32[4,128,512]{2,1,0:T(8,128)} %bitcast.34), calls=%async_computation.2 | async-start | bytes 2097152 | tf_op jit(solution)/shard_map/all_to_all | solution.py:150
  114.0 3.5 %collective-permute-start.23 = (f32[64,512]{1,0:T(8,128)S(1)}, f32[64,512]{1,0:T(8,128)S(1)}, u32[]{:S(2)}, u32[]{:S(2)}) collective-permute-start(f32[64,512]{1,0:T(8,128)S(1)} %fusion.7), channel_id=1, source_target_pairs={{0,0},{1,32},{2,64},{3,96},{4,128},{5,160},{6,192},{7,224},{8,8},{... | collective-permute-start | bytes 393224 | tf_op jit(solution)/shard_map/ppermute | solution.py:94
  117.5 4.9 %collective-permute-done.23 = f32[64,512]{1,0:T(8,128)S(1)} collective-permute-done((f32[64,512]{1,0:T(8,128)S(1)}, f32[64,512]{1,0:T(8,128)S(1)}, u32[]{:S(2)}, u32[]{:S(2)}) %collective-permute-start.23) | collective-permute-done | bytes 131104 | tf_op jit(solution)/shard_map/ppermute | solution.py:94
  122.3 6.5 %all-to-all-done.2 = f32[4,128,512]{2,1,0:T(8,128)S(1)} async-done(((f32[4,128,512]{2,1,0:T(8,128)}), f32[4,128,512]{2,1,0:T(8,128)S(1)}, u32[]{:S(2)}, u32[]{:S(2)}) %all-to-all-start.2) | async-done | bytes 1048608 | tf_op jit(solution)/shard_map/all_to_all | solution.py:150
  128.8 0.8 fusion.1
  129.6 0.7 copy.11
  (49 shorter events, 2.6 us)
Async XLA Ops:
  0.6 11.4 %copy-start.2 = (f32[64,512]{1,0:T(8,128)S(1)}, f32[64,512]{1,0:T(8,128)}, u32[]{:S(2)}) copy-start(f32[64,512]{1,0:T(8,128)} %param.6) | copy-start | bytes 393220
  2.8 32.6 %all-to-all-start = ((f32[32,8,768]{2,1,0:T(8,128)}), f32[32,8,768]{2,1,0:T(8,128)S(1)}, u32[]{:S(2)}, u32[]{:S(2)}) async-start(f32[32,8,768]{2,1,0:T(8,128)} %bitcast.55), calls=%async_computation | async-start | bytes 1572864 | tf_op jit(solution)/shard_map/all_to_all | solution.py:121
  12.0 16.9 %collective-permute-start = (f32[64,512]{1,0:T(8,128)S(1)}, f32[64,512]{1,0:T(8,128)S(1)}, u32[]{:S(2)}, u32[]{:S(2)}) collective-permute-start(f32[64,512]{1,0:T(8,128)S(1)} %copy-done.2), channel_id=1, source_target_pairs={{0,0},{1,32},{2,64},{3,96},{4,128},{5,160},{6,192},{7,224},{8,8},{... | collective-permute-start | bytes 393224 | tf_op jit(solution)/shard_map/ppermute | solution.py:94
  16.3 12.6 %collective-permute-start.1 = (f32[64,512]{1,0:T(8,128)S(1)}, f32[64,512]{1,0:T(8,128)S(1)}, u32[]{:S(2)}, u32[]{:S(2)}) collective-permute-start(f32[64,512]{1,0:T(8,128)S(1)} %copy-done.2), channel_id=1, source_target_pairs={{0,6},{1,38},{2,70},{3,102},{4,134},{5,166},{6,198},{7,230},{8,14}... | collective-permute-start | bytes 393224 | tf_op jit(solution)/shard_map/ppermute | solution.py:94
  20.3 10.9 %collective-permute-start.2 = (f32[64,512]{1,0:T(8,128)S(1)}, f32[64,512]{1,0:T(8,128)S(1)}, u32[]{:S(2)}, u32[]{:S(2)}) collective-permute-start(f32[64,512]{1,0:T(8,128)S(1)} %copy-done.2), channel_id=1, source_target_pairs={{0,4},{1,36},{2,68},{3,100},{4,132},{5,164},{6,196},{7,228},{8,12}... | collective-permute-start | bytes 393224 | tf_op jit(solution)/shard_map/ppermute | solution.py:94
  26.0 9.4 %collective-permute-start.3 = (f32[64,512]{1,0:T(8,128)S(1)}, f32[64,512]{1,0:T(8,128)S(1)}, u32[]{:S(2)}, u32[]{:S(2)}) collective-permute-start(f32[64,512]{1,0:T(8,128)S(1)} %copy-done.2), channel_id=1, source_target_pairs={{0,2},{1,34},{2,66},{3,98},{4,130},{5,162},{6,194},{7,226},{8,10},... | collective-permute-start | bytes 393224 | tf_op jit(solution)/shard_map/ppermute | solution.py:94
  35.4 5.7 %copy-start = (f32[32,8,768]{2,1,0:T(8,128)}, f32[32,8,768]{2,1,0:T(8,128)S(1)}, u32[]{:S(2)}) copy-start(f32[32,8,768]{2,1,0:T(8,128)S(1)} %all-to-all-done.pieces) | copy-start | bytes 2359300
  35.5 34.8 %collective-permute-start.9 = (f32[4,64,512]{2,1,0:T(8,128)S(1)}, f32[4,64,512]{2,1,0:T(8,128)S(1)}, u32[]{:S(2)}, u32[]{:S(2)}) collective-permute-start(f32[4,64,512]{2,1,0:T(8,128)S(1)} %get-tuple-element.35), channel_id=1, source_target_pairs={{0,16},{8,24},{16,0},{24,8},{1,17},{9,25},{17,1},{25,9},{2,18},{10... | collective-permute-start | bytes 1572872 | tf_op jit(solution)/shard_map/ppermute | solution.py:84
  38.3 32.4 %collective-permute-start.10 = (f32[4,64,512]{2,1,0:T(8,128)S(1)}, f32[4,64,512]{2,1,0:T(8,128)}, u32[]{:S(2)}, u32[]{:S(2)}) collective-permute-start(f32[4,64,512]{2,1,0:T(8,128)S(1)} %get-tuple-element.35), channel_id=1, source_target_pairs={{0,8},{8,16},{16,24},{24,0},{1,9},{9,17},{17,25},{25,1},{2,10},{10... | collective-permute-start | bytes 1572872 | tf_op jit(solution)/shard_map/ppermute | solution.py:84
  38.7 31.5 %collective-permute-start.8 = (f32[4,64,512]{2,1,0:T(8,128)S(1)}, f32[4,64,512]{2,1,0:T(8,128)}, u32[]{:S(2)}, u32[]{:S(2)}) collective-permute-start(f32[4,64,512]{2,1,0:T(8,128)S(1)} %get-tuple-element.35), channel_id=1, source_target_pairs={{0,24},{8,0},{16,8},{24,16},{1,25},{9,1},{17,9},{25,17},{2,26},{10... | collective-permute-start | bytes 1572872 | tf_op jit(solution)/shard_map/ppermute | solution.py:84
  42.9 9.5 %collective-permute-start.6 = (f32[2,8,768]{2,1,0:T(8,128)}, f32[2,8,768]{2,1,0:T(8,128)S(1)}, u32[]{:S(2)}, u32[]{:S(2)}) collective-permute-start(f32[2,8,768]{2,1,0:T(8,128)} %get-tuple-element.21), channel_id=1, source_target_pairs={{0,6},{2,0},{4,2},{6,4},{1,7},{3,1},{5,3},{7,5},{8,14},{10,8},{12,... | collective-permute-start | bytes 147464 | tf_op jit(solution)/shard_map/ppermute | solution.py:84
  46.1 7.9 %collective-permute-start.5 = (f32[2,8,768]{2,1,0:T(8,128)}, f32[2,8,768]{2,1,0:T(8,128)S(1)}, u32[]{:S(2)}, u32[]{:S(2)}) collective-permute-start(f32[2,8,768]{2,1,0:T(8,128)} %get-tuple-element.20), channel_id=1, source_target_pairs={{0,4},{2,6},{4,0},{6,2},{1,5},{3,7},{5,1},{7,3},{8,12},{10,14},{12... | collective-permute-start | bytes 147464 | tf_op jit(solution)/shard_map/ppermute | solution.py:84
  52.5 8.7 %copy-start.3 = (f32[2,8,768]{2,1,0:T(8,128)}, f32[2,8,768]{2,1,0:T(8,128)S(1)}, u32[]{:S(2)}) copy-start(f32[2,8,768]{2,1,0:T(8,128)S(1)} %collective-permute-done.6.three) | copy-start | bytes 147460
  52.5 5.9 %collective-permute-start.4 = (f32[2,8,768]{2,1,0:T(8,128)}, f32[2,8,768]{2,1,0:T(8,128)S(1)}, u32[]{:S(2)}, u32[]{:S(2)}) collective-permute-start(f32[2,8,768]{2,1,0:T(8,128)} %get-tuple-element.19), channel_id=1, source_target_pairs={{0,2},{2,4},{4,6},{6,0},{1,3},{3,5},{5,7},{7,1},{8,10},{10,12},{12... | collective-permute-start | bytes 147464 | tf_op jit(solution)/shard_map/ppermute | solution.py:84
  54.0 7.2 %copy-start.4 = (f32[2,8,768]{2,1,0:T(8,128)}, f32[2,8,768]{2,1,0:T(8,128)S(1)}, u32[]{:S(2)}) copy-start(f32[2,8,768]{2,1,0:T(8,128)S(1)} %collective-permute-done.5.two) | copy-start | bytes 147460
  58.4 2.8 %copy-start.5 = (f32[2,8,768]{2,1,0:T(8,128)}, f32[2,8,768]{2,1,0:T(8,128)S(1)}, u32[]{:S(2)}) copy-start(f32[2,8,768]{2,1,0:T(8,128)S(1)} %collective-permute-done.4.one) | copy-start | bytes 147460
  58.4 2.8 %collective-permute-start.7 = (f32[4,8,768]{2,1,0:T(8,128)S(1)}, f32[4,8,768]{2,1,0:T(8,128)S(1)}, u32[]{:S(2)}, u32[]{:S(2)}) collective-permute-start(f32[4,8,768]{2,1,0:T(8,128)S(1)} %pad_maximum_fusion.6), channel_id=1, source_target_pairs={{0,1},{1,0},{2,3},{3,2},{4,5},{5,4},{6,7},{7,6},{8,9},{9,8},{10,11... | collective-permute-start | bytes 294920 | tf_op jit(solution)/shard_map/ppermute | solution.py:127
  61.2 0.6 copy-start.6
  65.6 13.2 %all-to-all-start.1 = ((f32[8,8,2048]{2,1,0:T(8,128)}), f32[8,8,2048]{2,1,0:T(8,128)S(1)}, u32[]{:S(2)}, u32[]{:S(2)}) async-start(f32[8,8,2048]{2,1,0:T(8,128)} %broadcast_in_dim.16), calls=%async_computation.1 | async-start | bytes 1048576 | tf_op jit(solution)/shard_map/all_to_all | solution.py:131
  69.5 6.1 %collective-permute-start.11 = (f32[4,64,512]{2,1,0:T(8,128)S(1)}, f32[4,64,512]{2,1,0:T(8,128)S(1)}, u32[]{:S(2)}, u32[]{:S(2)}) collective-permute-start(f32[4,64,512]{2,1,0:T(8,128)S(1)} %get-tuple-element.35), channel_id=1, source_target_pairs={{0,1},{1,0},{2,3},{3,2},{4,5},{5,4},{6,7},{7,6},{8,9},{9,8},{10,11... | collective-permute-start | bytes 1572872 | tf_op jit(solution)/shard_map/ppermute | solution.py:135
  70.2 5.4 %collective-permute-start.12 = (f32[4,64,512]{2,1,0:T(8,128)}, f32[4,64,512]{2,1,0:T(8,128)}, u32[]{:S(2)}, u32[]{:S(2)}) collective-permute-start(f32[4,64,512]{2,1,0:T(8,128)} %collective-permute-done.8), channel_id=1, source_target_pairs={{0,1},{1,0},{2,3},{3,2},{4,5},{5,4},{6,7},{7,6},{8,9},{9,8},{10,11... | collective-permute-start | bytes 1572872 | tf_op jit(solution)/shard_map/ppermute | solution.py:135
  70.3 5.3 %collective-permute-start.13 = (f32[4,64,512]{2,1,0:T(8,128)S(1)}, f32[4,64,512]{2,1,0:T(8,128)}, u32[]{:S(2)}, u32[]{:S(2)}) collective-permute-start(f32[4,64,512]{2,1,0:T(8,128)S(1)} %collective-permute-done.9), channel_id=1, source_target_pairs={{0,1},{1,0},{2,3},{3,2},{4,5},{5,4},{6,7},{7,6},{8,9},{9,8},{10,11... | collective-permute-start | bytes 1572872 | tf_op jit(solution)/shard_map/ppermute | solution.py:135
  70.7 4.9 %collective-permute-start.14 = (f32[4,64,512]{2,1,0:T(8,128)}, f32[4,64,512]{2,1,0:T(8,128)}, u32[]{:S(2)}, u32[]{:S(2)}) collective-permute-start(f32[4,64,512]{2,1,0:T(8,128)} %collective-permute-done.10), channel_id=1, source_target_pairs={{0,1},{1,0},{2,3},{3,2},{4,5},{5,4},{6,7},{7,6},{8,9},{9,8},{10,11... | collective-permute-start | bytes 1572872 | tf_op jit(solution)/shard_map/ppermute | solution.py:135
  70.8 12.3 %collective-permute-start.15 = (f32[64,512]{1,0:T(8,128)S(1)}, f32[64,512]{1,0:T(8,128)S(1)}, u32[]{:S(2)}, u32[]{:S(2)}) collective-permute-start(f32[64,512]{1,0:T(8,128)S(1)} %copy-done.2), channel_id=1, source_target_pairs={{0,32},{32,0},{1,33},{33,1},{2,34},{34,2},{3,35},{35,3},{4,36},{36... | collective-permute-start | bytes 393224 | tf_op jit(solution)/shard_map/ppermute | solution.py:129
  83.1 8.8 %collective-permute-start.16 = (f32[64,512]{1,0:T(8,128)S(1)}, f32[64,512]{1,0:T(8,128)S(1)}, u32[]{:S(2)}, u32[]{:S(2)}) collective-permute-start(f32[64,512]{1,0:T(8,128)S(1)} %fusion.7), channel_id=1, source_target_pairs={{0,6},{2,0},{4,2},{6,4},{1,7},{3,1},{5,3},{7,5},{8,14},{10,8},{12,... | collective-permute-start | bytes 393224 | tf_op jit(solution)/shard_map/ppermute | solution.py:84
  85.7 20.2 %collective-permute-start.19 = (f32[2,64,512]{2,1,0:T(8,128)S(1)}, f32[2,64,512]{2,1,0:T(8,128)S(1)}, u32[]{:S(2)}, u32[]{:S(2)}) collective-permute-start(f32[2,64,512]{2,1,0:T(8,128)S(1)} %get-tuple-element.37), channel_id=1, source_target_pairs={{0,192},{64,0},{128,64},{192,128},{1,193},{65,1},{129,65},{193,129... | collective-permute-start | bytes 786440 | tf_op jit(solution)/shard_map/ppermute | solution.py:84
  86.6 19.2 %collective-permute-start.20 = (f32[2,64,512]{2,1,0:T(8,128)S(1)}, f32[2,64,512]{2,1,0:T(8,128)S(1)}, u32[]{:S(2)}, u32[]{:S(2)}) collective-permute-start(f32[2,64,512]{2,1,0:T(8,128)S(1)} %get-tuple-element.37), channel_id=1, source_target_pairs={{0,128},{64,192},{128,0},{192,64},{1,129},{65,193},{129,1},{193,65... | collective-permute-start | bytes 786440 | tf_op jit(solution)/shard_map/ppermute | solution.py:84
  86.9 19.0 %collective-permute-start.21 = (f32[2,64,512]{2,1,0:T(8,128)S(1)}, f32[2,64,512]{2,1,0:T(8,128)S(1)}, u32[]{:S(2)}, u32[]{:S(2)}) collective-permute-start(f32[2,64,512]{2,1,0:T(8,128)S(1)} %get-tuple-element.37), channel_id=1, source_target_pairs={{0,64},{64,128},{128,192},{192,0},{1,65},{65,129},{129,193},{193,1... | collective-permute-start | bytes 786440 | tf_op jit(solution)/shard_map/ppermute | solution.py:84
  87.5 9.4 %collective-permute-start.17 = (f32[64,512]{1,0:T(8,128)S(1)}, f32[64,512]{1,0:T(8,128)S(1)}, u32[]{:S(2)}, u32[]{:S(2)}) collective-permute-start(f32[64,512]{1,0:T(8,128)S(1)} %fusion.7), channel_id=1, source_target_pairs={{0,4},{2,6},{4,0},{6,2},{1,5},{3,7},{5,1},{7,3},{8,12},{10,14},{12... | collective-permute-start | bytes 393224 | tf_op jit(solution)/shard_map/ppermute | solution.py:84
  91.9 11.5 %collective-permute-start.18 = (f32[64,512]{1,0:T(8,128)S(1)}, f32[64,512]{1,0:T(8,128)S(1)}, u32[]{:S(2)}, u32[]{:S(2)}) collective-permute-start(f32[64,512]{1,0:T(8,128)S(1)} %fusion.7), channel_id=1, source_target_pairs={{0,2},{2,4},{4,6},{6,0},{1,3},{3,5},{5,7},{7,1},{8,10},{10,12},{12... | collective-permute-start | bytes 393224 | tf_op jit(solution)/shard_map/ppermute | solution.py:84
  103.5 3.9 %collective-permute-start.22 = (f32[4,64,512]{2,1,0:T(8,128)S(1)}, f32[4,64,512]{2,1,0:T(8,128)S(1)}, u32[]{:S(2)}, u32[]{:S(2)}) collective-permute-start(f32[4,64,512]{2,1,0:T(8,128)S(1)} %pad_maximum_fusion.4), channel_id=1, source_target_pairs={{0,1},{1,0},{2,3},{3,2},{4,5},{5,4},{6,7},{7,6},{8,9},{9,8},{10,11... | collective-permute-start | bytes 1572872 | tf_op jit(solution)/shard_map/ppermute | solution.py:143
  108.4 20.4 %copy-start.1 = (f32[128,512]{1,0:T(8,128)S(1)}, f32[128,512]{1,0:T(8,128)}, u32[]{:S(2)}) copy-start(f32[128,512]{1,0:T(8,128)} %param.7) | copy-start | bytes 786436
  110.5 18.3 %all-to-all-start.2 = ((f32[4,128,512]{2,1,0:T(8,128)}), f32[4,128,512]{2,1,0:T(8,128)S(1)}, u32[]{:S(2)}, u32[]{:S(2)}) async-start(f32[4,128,512]{2,1,0:T(8,128)} %bitcast.34), calls=%async_computation.2 | async-start | bytes 2097152 | tf_op jit(solution)/shard_map/all_to_all | solution.py:150
  114.0 8.4 %collective-permute-start.23 = (f32[64,512]{1,0:T(8,128)S(1)}, f32[64,512]{1,0:T(8,128)S(1)}, u32[]{:S(2)}, u32[]{:S(2)}) collective-permute-start(f32[64,512]{1,0:T(8,128)S(1)} %fusion.7), channel_id=1, source_target_pairs={{0,0},{1,32},{2,64},{3,96},{4,128},{5,160},{6,192},{7,224},{8,8},{... | collective-permute-start | bytes 393224 | tf_op jit(solution)/shard_map/ppermute | solution.py:94

commit v5 on v4

--- a/solution.py
+++ b/solution.py
@@ -112,43 +112,45 @@
 
 
 def per_device(root_cov, structure, child_factor, child_diag):
-    x, zl = lax.axis_index("x"), lax.axis_index("zl")
+    x, zl, y = lax.axis_index("x"), lax.axis_index("zl"), lax.axis_index("y")
     zh, core = lax.axis_index("zh"), lax.axis_index("core")
-    fours = lax.iota(jnp.int32, 4)
 
     sends = call(class_kernel, of(4, 64, 768), structure, root_cov)
     turned = [turn(child_factor, k) for k in range(4)]
+    other = lax.ppermute(child_factor, "zl", SWAP)
     pieces = lax.all_to_all(sends.reshape(32, 8, 768), CLASSED, 0, 0)
-    pieces, turned, factor = lax.optimization_barrier((pieces, turned, child_factor))
 
     cut = call(cut_kernel, [of(2, 8, 768)] * 4, structure, pieces)
     landed = [cut[0]] + [shift(cut[k], "zh", k) for k in (1, 2, 3)]
     give = jnp.stack([at(part, 1 - core) for part in landed])
     got = lax.ppermute(give, "core", SWAP)
     piece = call(columns_kernel, of(8, 2048), structure, *landed, got)
-    other = lax.ppermute(factor, "zl", SWAP)
 
-    rows = lax.all_to_all(jnp.broadcast_to(piece[None], (8, 8, 2048)), GROUP, 0, 0).reshape(64, 2048)
+    factor, other, turned, _ = lax.optimization_barrier((child_factor, other, jnp.stack(turned), cut))
+    pair = jnp.stack([jnp.where(zl == core, factor, other), jnp.where(zl == core, other, factor)])
+    block = jnp.stack([pair] + [shift(pair, "y", -k) for k in (1, 2, 3)], axis=1)
+    columns = [block] + [shift(block, "x", -k) for k in (1, 2, 3)]
 
-    turned = jnp.stack(turned)
     near = [turned] + [shift(turned, "y", -k) for k in (1, 2, 3)]
     far = [lax.ppermute(part, "core", SWAP) for part in near]
     near = jnp.stack(near, axis=1).reshape(1024, 512)
     far = jnp.stack(far, axis=1).reshape(1024, 512)
 
+    rows = lax.all_to_all(jnp.broadcast_to(piece[None], (8, 8, 2048)), GROUP, 0, 0).reshape(64, 2048)
+
     cross = -(dot(rows[:, :1024], near, 1) + dot(rows[:, 1024:], far, 1))
-    cross, factor, other = lax.optimization_barrier((cross, factor, other))
 
-    near = jnp.stack([cross] + [shift(cross, "zh", -k) for k in (1, 2, 3)])
+    slices = [lax.dynamic_slice(cross, (0, (y - k) % 4 * BLK), (64, BLK)) for k in range(4)]
+    slab = jnp.stack([slices[0]] + [shift(slices[k], "y", -k) for k in (1, 2, 3)])
+    near = jnp.stack([slab] + [shift(slab, "zh", -k) for k in (1, 2, 3)])
     far = lax.ppermute(near, "core", SWAP)
-    pair = jnp.stack([jnp.where(zl == core, factor, other), jnp.where(zl == core, other, factor)])
-    pairs = jnp.stack([pair] + [shift(pair, "x", -k) for k in (1, 2, 3)])
-    pairs = jnp.take(pairs, (zh - x + fours) % 4, axis=0)
-    share = dot(near.reshape(256, 512), pairs[:, 0].reshape(256, 512), 0)
-    share = share + dot(far.reshape(256, 512), pairs[:, 1].reshape(256, 512), 0)
-    share, cross = lax.optimization_barrier((share, cross))
-    got = lax.all_to_all(share.reshape(4, 128, 512), "y", 0, 0)
-    child = child_diag - (got[0] + got[1] + got[2] + got[3])
+    cross, _ = lax.optimization_barrier((cross, slab))
+
+    child = child_diag
+    for side, held in enumerate((near, far)):
+        for k in range(4):
+            part = at(held, (x + k - zh) % 4).reshape(256, 128)
+            child = child - dot(part, columns[k][side].reshape(256, 512), 0)
     return turn(cross, 0), child
 
 

time: 131 us -> 149 us (1.14)
  matrix products: 7.4 us -> 14 us
  waiting for transfers between devices: 38.5 us -> 45 us
  starting transfers between devices: 67 us -> 69.8 us
  local copies, waits for them, and re-layouts: 4.63 us -> 6.28 us
    ppermute x12 -> x18, waiting for transfers between devices: 16.2 us -> 31 us  [shift(): return lax.ppermute(block, axis, [(i, (i + k) % 4) for i in range(4)])]
    dot_general x4 -> x10, matrix products: 7.4 us -> 14 us  [dot(): lax.dot_general(first, second, (((axis,), (0,)), ((), ())), precision=HI,...]
    all_to_all x1 -> x0, waiting for transfers between devices: 6.45 us -> none  [per_device(): got = lax.all_to_all(share.reshape(4, 128, 512), 'y', 0, 0)]
    all_to_all x1, starting transfers between devices: 3.97 us -> 7.8 us  [per_device(): lax.all_to_all(jnp.broadcast_to(piece[None], (8, 8, 2048)), GROUP, 0, 0)]
    all_to_all x1 -> x0, starting transfers between devices: 3.51 us -> none  [per_device(): got = lax.all_to_all(share.reshape(4, 128, 512), 'y', 0, 0)]
    ppermute x1, starting transfers between devices: 1.85 us -> 4.55 us  [per_device(): got = lax.ppermute(give, 'core', SWAP)]
    ppermute x12 -> x18, starting transfers between devices: 24.2 us -> 26.9 us  [shift(): return lax.ppermute(block, axis, [(i, (i + k) % 4) for i in range(4)])]
    unnamed x15 -> x21, local copies, waits for them, and re-layouts: 1.32 us -> 3.58 us
  transfers between devices with their start and end apart: 27 -> 32, of which waited for: 12 -> 14; matrix products, arithmetic and copies ran while one was open for 10% -> 13% of each run, Pallas kernels for 3% -> 3%
where the time goes in v5:
time: 149 us; the launch traced here: 147 us
  starting transfers between devices  69.8 us (47%)
  waiting for transfers between devices  45 us (30%)
  matrix products  14 us (9%)
  local copies, waits for them, and re-layouts  6.28 us (4%)
  Pallas kernels  6.17 us (4%)
  other arithmetic  4.71 us (3%)
    ppermute x18, waiting for transfers between devices, shift(): return lax.ppermute(block, axis, [(i, (i + k) % 4) for i in range(4)])  31 us
    ppermute x18, starting transfers between devices, shift(): return lax.ppermute(block, axis, [(i, (i + k) % 4) for i in range(4)])  26.9 us
    ppermute x5, starting transfers between devices, turn(): return lax.ppermute(block, AXES, pairs)  18.6 us
    dot_general x10, matrix products, dot(): lax.dot_general(first, second, (((axis,), (0,)), ((), ())), precision=HI,...  14 us
    ppermute x5, waiting for transfers between devices, turn(): return lax.ppermute(block, AXES, pairs)  13.6 us
    all_to_all x1, starting transfers between devices, per_device(): pieces = lax.all_to_all(sends.reshape(32, 8, 768), CLASSED, 0, 0)  9.23 us
    all_to_all x1, starting transfers between devices, per_device(): lax.all_to_all(jnp.broadcast_to(piece[None], (8, 8, 2048)), GROUP, 0, 0)  7.8 us
    pallas_call x3, Pallas kernels, call(): pl.pallas_call(kernel, out_shape=shapes, in_specs=[smem()] + [vmem()] * l...  6.17 us
  transfers between devices with their start and end apart: 32, of which 14 were waited for; matrix products, arithmetic and copies ran while one was open for 13% of the time, Pallas kernels for 3%

profile of v5, /device:TPU:1, one launch (start us, length us, event | category | flops | bytes accessed | tf_op | source)
XLA Modules:
  0.0 147.0 jit_solution(5958050987089865684)
XLA Ops:
  0.6 2.2 %shard_map.59 = f32[4,64,768]{2,1,0:T(8,128)} custom-call(s32[16]{0:T(128)} %structure.5, f32[192,768]{1,0:T(8,128)} %root.1), custom_call_target="tpu_custom_call" | custom-call | tf_op jit(solution)/shard_map/pallas_call | solution.py:102
  2.8 9.2 %all-to-all-start = ((f32[32,8,768]{2,1,0:T(8,128)}), f32[32,8,768]{2,1,0:T(8,128)S(1)}, u32[]{:S(2)}, u32[]{:S(2)}) async-start(f32[32,8,768]{2,1,0:T(8,128)} %bitcast.131), calls=%async_computation | async-start | bytes 1572864 | tf_op jit(solution)/shard_map/all_to_all | solution.py:121
  12.1 5.1 %collective-permute-start.8 = (f32[64,512]{1,0:T(8,128)S(1)}, f32[64,512]{1,0:T(8,128)S(1)}, u32[]{:S(2)}, u32[]{:S(2)}) collective-permute-start(f32[64,512]{1,0:T(8,128)S(1)} %copy-done.5), channel_id=1, source_target_pairs={{0,2},{1,34},{2,66},{3,98},{4,130},{5,162},{6,194},{7,226},{8,10},... | collective-permute-start | bytes 393224 | tf_op jit(solution)/shard_map/ppermute | solution.py:94
  17.2 4.0 %collective-permute-start.7 = (f32[64,512]{1,0:T(8,128)S(1)}, f32[64,512]{1,0:T(8,128)S(1)}, u32[]{:S(2)}, u32[]{:S(2)}) collective-permute-start(f32[64,512]{1,0:T(8,128)S(1)} %copy-done.5), channel_id=1, source_target_pairs={{0,4},{1,36},{2,68},{3,100},{4,132},{5,164},{6,196},{7,228},{8,12}... | collective-permute-start | bytes 393224 | tf_op jit(solution)/shard_map/ppermute | solution.py:94
  21.6 3.5 %collective-permute-start.5 = (f32[64,512]{1,0:T(8,128)S(1)}, f32[64,512]{1,0:T(8,128)S(1)}, u32[]{:S(2)}, u32[]{:S(2)}) collective-permute-start(f32[64,512]{1,0:T(8,128)S(1)} %copy-done.5), channel_id=1, source_target_pairs={{0,0},{1,32},{2,64},{3,96},{4,128},{5,160},{6,192},{7,224},{8,8},{... | collective-permute-start | bytes 393224 | tf_op jit(solution)/shard_map/ppermute | solution.py:94
  25.3 3.7 %collective-permute-done.8 = f32[64,512]{1,0:T(8,128)S(1)} collective-permute-done((f32[64,512]{1,0:T(8,128)S(1)}, f32[64,512]{1,0:T(8,128)S(1)}, u32[]{:S(2)}, u32[]{:S(2)}) %collective-permute-start.8) | collective-permute-done | bytes 131104 | tf_op jit(solution)/shard_map/ppermute | solution.py:94
  29.0 8.8 %collective-permute-done.7 = f32[64,512]{1,0:T(8,128)S(1)} collective-permute-done((f32[64,512]{1,0:T(8,128)S(1)}, f32[64,512]{1,0:T(8,128)S(1)}, u32[]{:S(2)}, u32[]{:S(2)}) %collective-permute-start.7) | collective-permute-done | bytes 131104 | tf_op jit(solution)/shard_map/ppermute | solution.py:94
  37.9 0.9 copy-done
  38.8 1.9 %shard_map.60 = (f32[2,8,768]{2,1,0:T(8,128)}, f32[2,8,768]{2,1,0:T(8,128)}, f32[2,8,768]{2,1,0:T(8,128)}, f32[2,8,768]{2,1,0:T(8,128)}) custom-call(s32[16]{0:T(128)} %structure.5, f32[32,8,768]{2,1,0:T(8,128)} %copy-done), custom_call_target="tpu_custom_call" | custom-call | tf_op jit(solution)/shard_map/pallas_call | solution.py:102
  40.7 1.2 collective-permute-start.11
  41.9 2.5 %collective-permute-start.10 = (f32[4,64,512]{2,1,0:T(8,128)S(1)}, f32[4,64,512]{2,1,0:T(8,128)S(1)}, u32[]{:S(2)}, u32[]{:S(2)}) collective-permute-start(f32[4,64,512]{2,1,0:T(8,128)S(1)} %pad_maximum_fusion.3), channel_id=1, source_target_pairs={{0,16},{8,24},{16,0},{24,8},{1,17},{9,25},{17,1},{25,9},{2,18},{10... | collective-permute-start | bytes 1572872 | tf_op jit(solution)/shard_map/ppermute | solution.py:84
  44.4 1.1 collective-permute-start.9
  45.5 3.6 %collective-permute-start.2 = (f32[2,8,768]{2,1,0:T(8,128)}, f32[2,8,768]{2,1,0:T(8,128)S(1)}, u32[]{:S(2)}, u32[]{:S(2)}) collective-permute-start(f32[2,8,768]{2,1,0:T(8,128)} %get-tuple-element.13), channel_id=1, source_target_pairs={{0,6},{2,0},{4,2},{6,4},{1,7},{3,1},{5,3},{7,5},{8,14},{10,8},{12,... | collective-permute-start | bytes 147464 | tf_op jit(solution)/shard_map/ppermute | solution.py:84
  49.1 0.7 constant_dynamic-slice_fusion.6
  49.9 0.7 collective-permute-done.2.three
  50.6 2.7 %collective-permute-start.1 = (f32[2,8,768]{2,1,0:T(8,128)}, f32[2,8,768]{2,1,0:T(8,128)S(1)}, u32[]{:S(2)}, u32[]{:S(2)}) collective-permute-start(f32[2,8,768]{2,1,0:T(8,128)} %get-tuple-element.12), channel_id=1, source_target_pairs={{0,4},{2,6},{4,0},{6,2},{1,5},{3,7},{5,1},{7,3},{8,12},{10,14},{12... | collective-permute-start | bytes 147464 | tf_op jit(solution)/shard_map/ppermute | solution.py:84
  53.3 4.3 %collective-permute-done.1.two = f32[2,8,768]{2,1,0:T(8,128)S(1)} collective-permute-done((f32[2,8,768]{2,1,0:T(8,128)}, f32[2,8,768]{2,1,0:T(8,128)S(1)}, u32[]{:S(2)}, u32[]{:S(2)}) %collective-permute-start.1) | collective-permute-done | bytes 49184 | tf_op jit(solution)/shard_map/ppermute | solution.py:84
  57.7 4.5 %collective-permute-start.3 = (f32[4,8,768]{2,1,0:T(8,128)S(1)}, f32[4,8,768]{2,1,0:T(8,128)S(1)}, u32[]{:S(2)}, u32[]{:S(2)}) collective-permute-start(f32[4,8,768]{2,1,0:T(8,128)S(1)} %pad_maximum_fusion.7), channel_id=1, source_target_pairs={{0,1},{1,0},{2,3},{3,2},{4,5},{5,4},{6,7},{7,6},{8,9},{9,8},{10,11... | collective-permute-start | bytes 294920 | tf_op jit(solution)/shard_map/ppermute | solution.py:126
  63.8 2.1 %shard_map.61 = f32[8,2048]{1,0:T(8,128)} custom-call(s32[16]{0:T(128)} %structure.5, f32[2,8,768]{2,1,0:T(8,128)} %get-tuple-element.10.own, f32[2,8,768]{2,1,0:T(8,128)} %copy-done.6, f32[2,8,768]{2,1,0:T(8,128)} %copy-done.8, f32[2,8,768]{2,1,0:T(8,128)} %copy-done.7, f32[4,8,768]{2,1,0:T(8,128)} %copy-done.9), custom_call_target="tpu_custom_call" | custom-call | tf_op jit(solution)/shard_map/pallas_call | solution.py:102
  65.9 1.7 %broadcast_in_dim.2 = f32[8,8,2048]{2,1,0:T(8,128)} broadcast(f32[8,2048]{1,0:T(8,128)} %shard_map.61), dimensions={1,2} | broadcast | bytes 589824 | tf_op jit(solution)/shard_map/broadcast_in_dim | solution.py:139
  67.6 7.8 %all-to-all-start.1 = ((f32[8,8,2048]{2,1,0:T(8,128)}), f32[8,8,2048]{2,1,0:T(8,128)}, u32[]{:S(2)}, u32[]{:S(2)}) async-start(f32[8,8,2048]{2,1,0:T(8,128)} %broadcast_in_dim.2), calls=%async_computation.1 | async-start | bytes 1048576 | tf_op jit(solution)/shard_map/all_to_all | solution.py:139
  75.4 1.7 %collective-permute-done.25 = f32[2,64,512]{2,1,0:T(8,128)S(1)} collective-permute-done((f32[2,64,512]{2,1,0:T(8,128)S(1)}, f32[2,64,512]{2,1,0:T(8,128)S(1)}, u32[]{:S(2)}, u32[]{:S(2)}) %collective-permute-start.25) | collective-permute-done | bytes 262176 | tf_op jit(solution)/shard_map/ppermute | solution.py:84
  77.6 1.2 collective-permute-start.12
  79.6 4.7 %collective-permute-done.23 = f32[2,64,512]{2,1,0:T(8,128)S(1)} collective-permute-done((f32[2,64,512]{2,1,0:T(8,128)S(1)}, f32[2,64,512]{2,1,0:T(8,128)S(1)}, u32[]{:S(2)}, u32[]{:S(2)}) %collective-permute-start.23) | collective-permute-done | bytes 262176 | tf_op jit(solution)/shard_map/ppermute | solution.py:84
  85.0 1.2 pad_maximum_fusion.2
  86.2 2.7 %collective-permute-start.28 = (f32[2,4,64,512]{3,2,1,0:T(8,128)S(1)}, f32[2,4,64,512]{3,2,1,0:T(8,128)}, u32[]{:S(2)}, u32[]{:S(2)}) collective-permute-start(f32[2,4,64,512]{3,2,1,0:T(8,128)S(1)} %pad_maximum_fusion.2), channel_id=1, source_target_pairs={{0,64},{64,128},{128,192},{192,0},{1,65},{65,129},{129,193},{193,1... | collective-permute-start | bytes 3145736 | tf_op jit(solution)/shard_map/ppermute | solution.py:84
  88.9 1.6 %pad_maximum_fusion = f32[4,4,64,512]{3,2,1,0:T(8,128)} fusion(f32[4,1,64,512]{3,2,1,0:T(8,128)S(1)} %bitcast.133, f32[4,1,64,512]{3,2,1,0:T(8,128)S(1)} %bitcast.134, f32[4,1,64,512]{3,2,1,0:T(8,128)S(1)} %bitcast.135, f32[4,1,64,512]{3,2,1,0:T(8,128)S(1)} %bitcast.132), kind=kLoop, calls=%fused_computation | loop fusion | flops 1572864 | bytes 4194304 | tf_op jit(solution)/shard_map/stack | solution.py:136
  90.5 5.5 %collective-permute-start.27 = (f32[2,4,64,512]{3,2,1,0:T(8,128)S(1)}, f32[2,4,64,512]{3,2,1,0:T(8,128)}, u32[]{:S(2)}, u32[]{:S(2)}) collective-permute-start(f32[2,4,64,512]{3,2,1,0:T(8,128)S(1)} %pad_maximum_fusion.2), channel_id=1, source_target_pairs={{0,128},{64,192},{128,0},{192,64},{1,129},{65,193},{129,1},{193,65... | collective-permute-start | bytes 3145736 | tf_op jit(solution)/shard_map/ppermute | solution.py:84
  96.0 1.7 %pad_maximum_fusion.1 = f32[4,4,64,512]{3,2,0,1:T(8,128)S(1)} fusion(f32[4,1,64,512]{3,2,0,1:T(8,128)} %bitcast.17, f32[4,1,64,512]{3,2,0,1:T(8,128)} %bitcast.16, f32[4,1,64,512]{3,2,0,1:T(8,128)} %bitcast.15, f32[4,1,64,512]{3,2,0,1:T(8,128)} %bitcast.14), kind=kLoop, calls=%fused_computation.1 | loop fusion | flops 1572864 | bytes 4194304 | tf_op jit(solution)/shard_map/stack | solution.py:137
  98.0 3.1 %fusion.16 = f32[64,512]{1,0:T(8,128)S(1)} fusion(f32[1024,512]{1,0:T(8,128)} %bitcast.130, f32[64,2048]{1,0:T(8,128)} %bitcast.1), kind=kOutput, calls=%fused_computation.33 | convolution fusion | flops 402653184 | bytes 2490368 | tf_op jit(solution)/shard_map/dot_general | solution.py:66
  101.1 2.4 %fusion.13 = f32[64,512]{1,0:T(8,128)S(1)} fusion(f32[64,512]{1,0:T(8,128)S(1)} %fusion.16, f32[1024,512]{1,0:T(8,128)S(1)} %bitcast.129, f32[64,2048]{1,0:T(8,128)} %bitcast.1), kind=kOutput, calls=%fused_computation.32 | convolution fusion | flops 402718720 | bytes 2621440 | tf_op jit(solution)/shard_map/dot_general | solution.py:66
  103.6 2.7 %collective-permute-start.17 = (f32[64,128]{1,0:T(8,128)S(1)}, f32[64,128]{1,0:T(8,128)S(1)}, u32[]{:S(2)}, u32[]{:S(2)}) collective-permute-start(f32[64,128]{1,0:T(8,128)S(1)} %get-tuple-element.26), channel_id=1, source_target_pairs={{0,16},{8,24},{16,0},{24,8},{1,17},{9,25},{17,1},{25,9},{2,18},{10... | collective-permute-start | bytes 98312 | tf_op jit(solution)/shard_map/ppermute | solution.py:84
  106.3 1.7 %collective-permute-done.18 = f32[64,128]{1,0:T(8,128)S(1)} collective-permute-done((f32[64,128]{1,0:T(8,128)S(1)}, f32[64,128]{1,0:T(8,128)S(1)}, u32[]{:S(2)}, u32[]{:S(2)}) %collective-permute-start.18) | collective-permute-done | bytes 32800 | tf_op jit(solution)/shard_map/ppermute | solution.py:84
  107.9 1.5 %collective-permute-done.16 = f32[64,128]{1,0:T(8,128)S(1)} collective-permute-done((f32[64,128]{1,0:T(8,128)S(1)}, f32[64,128]{1,0:T(8,128)S(1)}, u32[]{:S(2)}, u32[]{:S(2)}) %collective-permute-start.16) | collective-permute-done | bytes 32800 | tf_op jit(solution)/shard_map/ppermute | solution.py:84
  109.6 2.8 %collective-permute-start.21 = (f32[4,64,128]{2,1,0:T(8,128)S(1)}, f32[4,64,128]{2,1,0:T(8,128)S(1)}, u32[]{:S(2)}, u32[]{:S(2)}) collective-permute-start(f32[4,64,128]{2,1,0:T(8,128)S(1)} %get-tuple-element.23), channel_id=1, source_target_pairs={{0,4},{2,6},{4,0},{6,2},{1,5},{3,7},{5,1},{7,3},{8,12},{10,14},{12... | collective-permute-start | bytes 393224 | tf_op jit(solution)/shard_map/ppermute | solution.py:84
  112.3 0.8 collective-permute-start.20
  113.1 4.4 %collective-permute-done.22 = f32[4,64,128]{2,1,0:T(8,128)S(1)} collective-permute-done((f32[4,64,128]{2,1,0:T(8,128)S(1)}, f32[4,64,128]{2,1,0:T(8,128)S(1)}, u32[]{:S(2)}, u32[]{:S(2)}) %collective-permute-start.22) | collective-permute-done | bytes 131104 | tf_op jit(solution)/shard_map/ppermute | solution.py:84
  117.5 1.7 %collective-permute-done.21 = f32[4,64,128]{2,1,0:T(8,128)S(1)} collective-permute-done((f32[4,64,128]{2,1,0:T(8,128)S(1)}, f32[4,64,128]{2,1,0:T(8,128)S(1)}, u32[]{:S(2)}, u32[]{:S(2)}) %collective-permute-start.21) | collective-permute-done | bytes 131104 | tf_op jit(solution)/shard_map/ppermute | solution.py:84
  119.2 5.5 %collective-permute-start.19 = (f32[64,512]{1,0:T(8,128)S(1)}, f32[64,512]{1,0:T(8,128)}, u32[]{:S(2)}, u32[]{:S(2)}) collective-permute-start(f32[64,512]{1,0:T(8,128)S(1)} %fusion.13), channel_id=1, source_target_pairs={{0,0},{1,32},{2,64},{3,96},{4,128},{5,160},{6,192},{7,224},{8,8},{... | collective-permute-start | bytes 393224 | tf_op jit(solution)/shard_map/ppermute | solution.py:94
  124.7 1.5 %collective-permute-done.20 = f32[4,64,128]{2,1,0:T(8,128)S(1)} collective-permute-done((f32[4,64,128]{2,1,0:T(8,128)S(1)}, f32[4,64,128]{2,1,0:T(8,128)S(1)}, u32[]{:S(2)}, u32[]{:S(2)}) %collective-permute-start.20) | collective-permute-done | bytes 131104 | tf_op jit(solution)/shard_map/ppermute | solution.py:84
  126.9 1.0 collective-permute-done.19
  128.4 1.5 %convolution_bitcast_fusion.4 = f32[128,512]{1,0:T(8,128)S(1)} fusion(f32[2,4,64,512]{3,2,1,0:T(8,128)} %collective-permute-done.28, f32[4,4,64,128]{3,2,1,0:T(8,128)S(1)} %pad_maximum_fusion.4, s32[]{:T(128)S(6)} %select_n.110), kind=kOutput, calls=%fused_computation.6 | convolution fusion | flops 201326592 | bytes 917508 | tf_op jit(solution)/shard_map/dot_general | solution.py:66
  129.9 8.8 %collective-permute-done.27 = f32[2,4,64,512]{3,2,1,0:T(8,128)} collective-permute-done((f32[2,4,64,512]{3,2,1,0:T(8,128)S(1)}, f32[2,4,64,512]{3,2,1,0:T(8,128)}, u32[]{:S(2)}, u32[]{:S(2)}) %collective-permute-start.27) | collective-permute-done | bytes 1048608 | tf_op jit(solution)/shard_map/ppermute | solution.py:84
  138.7 1.5 %convolution_bitcast_fusion.5 = f32[128,512]{1,0:T(8,128)S(1)} fusion(f32[2,4,64,512]{3,2,1,0:T(8,128)} %collective-permute-done.27, f32[4,4,64,128]{3,2,1,0:T(8,128)S(1)} %pad_maximum_fusion.4, s32[]{:T(128)S(6)} %select_n.108), kind=kOutput, calls=%fused_computation.7 | convolution fusion | flops 201326592 | bytes 917508 | tf_op jit(solution)/shard_map/dot_general | solution.py:66
  140.2 1.5 %convolution_bitcast_fusion = f32[128,512]{1,0:T(8,128)S(1)} fusion(f32[2,4,64,512]{3,2,1,0:T(8,128)} %collective-permute-done.28, f32[4,4,64,128]{3,2,1,0:T(8,128)S(1)} %collective-permute-done.29, s32[]{:T(128)S(6)} %select_n.110), kind=kOutput, calls=%fused_computation.2 | convolution fusion | flops 201326592 | bytes 917508 | tf_op jit(solution)/shard_map/dot_general | solution.py:66
  141.7 1.5 %convolution_bitcast_fusion.1 = f32[128,512]{1,0:T(8,128)S(1)} fusion(f32[2,4,64,512]{3,2,1,0:T(8,128)} %collective-permute-done.27, f32[4,4,64,128]{3,2,1,0:T(8,128)S(1)} %collective-permute-done.29, s32[]{:T(128)S(6)} %select_n.108), kind=kOutput, calls=%fused_computation.3 | convolution fusion | flops 201326592 | bytes 917508 | tf_op jit(solution)/shard_map/dot_general | solution.py:66
  144.2 1.2 fusion.7
  145.4 1.6 %copy.17 = f32[64,512]{1,0:T(8,128)} copy(f32[64,512]{1,0:T(8,128)} %collective-permute-done.19) | data formatting | bytes 262144
  (66 shorter events, 6.9 us)
Async XLA Ops:
  0.6 11.4 %copy-start.5 = (f32[64,512]{1,0:T(8,128)S(1)}, f32[64,512]{1,0:T(8,128)}, u32[]{:S(2)}) copy-start(f32[64,512]{1,0:T(8,128)} %param.6) | copy-start | bytes 393220
  2.8 35.1 %all-to-all-start = ((f32[32,8,768]{2,1,0:T(8,128)}), f32[32,8,768]{2,1,0:T(8,128)S(1)}, u32[]{:S(2)}, u32[]{:S(2)}) async-start(f32[32,8,768]{2,1,0:T(8,128)} %bitcast.131), calls=%async_computation | async-start | bytes 1572864 | tf_op jit(solution)/shard_map/all_to_all | solution.py:121
  12.1 16.9 %collective-permute-start.8 = (f32[64,512]{1,0:T(8,128)S(1)}, f32[64,512]{1,0:T(8,128)S(1)}, u32[]{:S(2)}, u32[]{:S(2)}) collective-permute-start(f32[64,512]{1,0:T(8,128)S(1)} %copy-done.5), channel_id=1, source_target_pairs={{0,2},{1,34},{2,66},{3,98},{4,130},{5,162},{6,194},{7,226},{8,10},... | collective-permute-start | bytes 393224 | tf_op jit(solution)/shard_map/ppermute | solution.py:94
  17.2 20.6 %collective-permute-start.7 = (f32[64,512]{1,0:T(8,128)S(1)}, f32[64,512]{1,0:T(8,128)S(1)}, u32[]{:S(2)}, u32[]{:S(2)}) collective-permute-start(f32[64,512]{1,0:T(8,128)S(1)} %copy-done.5), channel_id=1, source_target_pairs={{0,4},{1,36},{2,68},{3,100},{4,132},{5,164},{6,196},{7,228},{8,12}... | collective-permute-start | bytes 393224 | tf_op jit(solution)/shard_map/ppermute | solution.py:94
  21.1 16.7 %collective-permute-start.6 = (f32[64,512]{1,0:T(8,128)S(1)}, f32[64,512]{1,0:T(8,128)S(1)}, u32[]{:S(2)}, u32[]{:S(2)}) collective-permute-start(f32[64,512]{1,0:T(8,128)S(1)} %copy-done.5), channel_id=1, source_target_pairs={{0,6},{1,38},{2,70},{3,102},{4,134},{5,166},{6,198},{7,230},{8,14}... | collective-permute-start | bytes 393224 | tf_op jit(solution)/shard_map/ppermute | solution.py:94
  21.6 16.2 %collective-permute-start.5 = (f32[64,512]{1,0:T(8,128)S(1)}, f32[64,512]{1,0:T(8,128)S(1)}, u32[]{:S(2)}, u32[]{:S(2)}) collective-permute-start(f32[64,512]{1,0:T(8,128)S(1)} %copy-done.5), channel_id=1, source_target_pairs={{0,0},{1,32},{2,64},{3,96},{4,128},{5,160},{6,192},{7,224},{8,8},{... | collective-permute-start | bytes 393224 | tf_op jit(solution)/shard_map/ppermute | solution.py:94
  25.2 15.6 %collective-permute-start.4 = (f32[64,512]{1,0:T(8,128)S(1)}, f32[64,512]{1,0:T(8,128)S(1)}, u32[]{:S(2)}, u32[]{:S(2)}) collective-permute-start(f32[64,512]{1,0:T(8,128)S(1)} %copy-done.5), channel_id=1, source_target_pairs={{0,32},{32,0},{1,33},{33,1},{2,34},{34,2},{3,35},{35,3},{4,36},{36... | collective-permute-start | bytes 393224 | tf_op jit(solution)/shard_map/ppermute | solution.py:120
  37.9 0.9 copy-start
  40.7 38.1 %collective-permute-start.11 = (f32[4,64,512]{2,1,0:T(8,128)S(1)}, f32[4,64,512]{2,1,0:T(8,128)S(1)}, u32[]{:S(2)}, u32[]{:S(2)}) collective-permute-start(f32[4,64,512]{2,1,0:T(8,128)S(1)} %pad_maximum_fusion.3), channel_id=1, source_target_pairs={{0,8},{8,16},{16,24},{24,0},{1,9},{9,17},{17,25},{25,1},{2,10},{10... | collective-permute-start | bytes 1572872 | tf_op jit(solution)/shard_map/ppermute | solution.py:84
  41.9 37.2 %collective-permute-start.10 = (f32[4,64,512]{2,1,0:T(8,128)S(1)}, f32[4,64,512]{2,1,0:T(8,128)S(1)}, u32[]{:S(2)}, u32[]{:S(2)}) collective-permute-start(f32[4,64,512]{2,1,0:T(8,128)S(1)} %pad_maximum_fusion.3), channel_id=1, source_target_pairs={{0,16},{8,24},{16,0},{24,8},{1,17},{9,25},{17,1},{25,9},{2,18},{10... | collective-permute-start | bytes 1572872 | tf_op jit(solution)/shard_map/ppermute | solution.py:84
  44.4 34.9 %collective-permute-start.9 = (f32[4,64,512]{2,1,0:T(8,128)S(1)}, f32[4,64,512]{2,1,0:T(8,128)S(1)}, u32[]{:S(2)}, u32[]{:S(2)}) collective-permute-start(f32[4,64,512]{2,1,0:T(8,128)S(1)} %pad_maximum_fusion.3), channel_id=1, source_target_pairs={{0,24},{8,0},{16,8},{24,16},{1,25},{9,1},{17,9},{25,17},{2,26},{10... | collective-permute-start | bytes 1572872 | tf_op jit(solution)/shard_map/ppermute | solution.py:84
  45.5 12.1 %collective-permute-start = (f32[2,8,768]{2,1,0:T(8,128)}, f32[2,8,768]{2,1,0:T(8,128)S(1)}, u32[]{:S(2)}, u32[]{:S(2)}) collective-permute-start(f32[2,8,768]{2,1,0:T(8,128)} %get-tuple-element.11), channel_id=1, source_target_pairs={{0,2},{2,4},{4,6},{6,0},{1,3},{3,5},{5,7},{7,1},{8,10},{10,12},{12... | collective-permute-start | bytes 147464 | tf_op jit(solution)/shard_map/ppermute | solution.py:84
  45.5 5.1 %collective-permute-start.2 = (f32[2,8,768]{2,1,0:T(8,128)}, f32[2,8,768]{2,1,0:T(8,128)S(1)}, u32[]{:S(2)}, u32[]{:S(2)}) collective-permute-start(f32[2,8,768]{2,1,0:T(8,128)} %get-tuple-element.13), channel_id=1, source_target_pairs={{0,6},{2,0},{4,2},{6,4},{1,7},{3,1},{5,3},{7,5},{8,14},{10,8},{12,... | collective-permute-start | bytes 147464 | tf_op jit(solution)/shard_map/ppermute | solution.py:84
  50.6 12.9 %copy-start.7 = (f32[2,8,768]{2,1,0:T(8,128)}, f32[2,8,768]{2,1,0:T(8,128)S(1)}, u32[]{:S(2)}) copy-start(f32[2,8,768]{2,1,0:T(8,128)S(1)} %collective-permute-done.2.three) | copy-start | bytes 147460
  50.6 7.1 %collective-permute-start.1 = (f32[2,8,768]{2,1,0:T(8,128)}, f32[2,8,768]{2,1,0:T(8,128)S(1)}, u32[]{:S(2)}, u32[]{:S(2)}) collective-permute-start(f32[2,8,768]{2,1,0:T(8,128)} %get-tuple-element.12), channel_id=1, source_target_pairs={{0,4},{2,6},{4,0},{6,2},{1,5},{3,7},{5,1},{7,3},{8,12},{10,14},{12... | collective-permute-start | bytes 147464 | tf_op jit(solution)/shard_map/ppermute | solution.py:84
  57.6 5.8 %copy-start.8 = (f32[2,8,768]{2,1,0:T(8,128)}, f32[2,8,768]{2,1,0:T(8,128)S(1)}, u32[]{:S(2)}) copy-start(f32[2,8,768]{2,1,0:T(8,128)S(1)} %collective-permute-done.1.two) | copy-start | bytes 147460
  57.7 5.8 %copy-start.6 = (f32[2,8,768]{2,1,0:T(8,128)}, f32[2,8,768]{2,1,0:T(8,128)S(1)}, u32[]{:S(2)}) copy-start(f32[2,8,768]{2,1,0:T(8,128)S(1)} %collective-permute-done.one) | copy-start | bytes 147460
  57.7 5.5 %collective-permute-start.3 = (f32[4,8,768]{2,1,0:T(8,128)S(1)}, f32[4,8,768]{2,1,0:T(8,128)S(1)}, u32[]{:S(2)}, u32[]{:S(2)}) collective-permute-start(f32[4,8,768]{2,1,0:T(8,128)S(1)} %pad_maximum_fusion.7), channel_id=1, source_target_pairs={{0,1},{1,0},{2,3},{3,2},{4,5},{5,4},{6,7},{7,6},{8,9},{9,8},{10,11... | collective-permute-start | bytes 294920 | tf_op jit(solution)/shard_map/ppermute | solution.py:126
  62.3 14.8 %collective-permute-start.25 = (f32[2,64,512]{2,1,0:T(8,128)S(1)}, f32[2,64,512]{2,1,0:T(8,128)S(1)}, u32[]{:S(2)}, u32[]{:S(2)}) collective-permute-start(f32[2,64,512]{2,1,0:T(8,128)S(1)} %get-tuple-element.19), channel_id=1, source_target_pairs={{0,8},{8,16},{16,24},{24,0},{1,9},{9,17},{17,25},{25,1},{2,10},{10... | collective-permute-start | bytes 786440 | tf_op jit(solution)/shard_map/ppermute | solution.py:84
  63.2 0.6 copy-start.9
  63.2 14.4 %collective-permute-start.24 = (f32[2,64,512]{2,1,0:T(8,128)S(1)}, f32[2,64,512]{2,1,0:T(8,128)S(1)}, u32[]{:S(2)}, u32[]{:S(2)}) collective-permute-start(f32[2,64,512]{2,1,0:T(8,128)S(1)} %get-tuple-element.19), channel_id=1, source_target_pairs={{0,16},{8,24},{16,0},{24,8},{1,17},{9,25},{17,1},{25,9},{2,18},{10... | collective-permute-start | bytes 786440 | tf_op jit(solution)/shard_map/ppermute | solution.py:84
  67.6 30.4 %all-to-all-start.1 = ((f32[8,8,2048]{2,1,0:T(8,128)}), f32[8,8,2048]{2,1,0:T(8,128)}, u32[]{:S(2)}, u32[]{:S(2)}) async-start(f32[8,8,2048]{2,1,0:T(8,128)} %broadcast_in_dim.2), calls=%async_computation.1 | async-start | bytes 1048576 | tf_op jit(solution)/shard_map/all_to_all | solution.py:139
  77.1 7.1 %copy-start.2 = (f32[2,64,512]{2,1,0:T(8,128)}, f32[2,64,512]{2,1,0:T(8,128)S(1)}, u32[]{:S(2)}) copy-start(f32[2,64,512]{2,1,0:T(8,128)S(1)} %collective-permute-done.25) | copy-start | bytes 786436
  77.1 7.1 %collective-permute-start.23 = (f32[2,64,512]{2,1,0:T(8,128)S(1)}, f32[2,64,512]{2,1,0:T(8,128)S(1)}, u32[]{:S(2)}, u32[]{:S(2)}) collective-permute-start(f32[2,64,512]{2,1,0:T(8,128)S(1)} %get-tuple-element.19), channel_id=1, source_target_pairs={{0,24},{8,0},{16,8},{24,16},{1,25},{9,1},{17,9},{25,17},{2,26},{10... | collective-permute-start | bytes 786440 | tf_op jit(solution)/shard_map/ppermute | solution.py:84
  77.6 6.7 %copy-start.3 = (f32[2,64,512]{2,1,0:T(8,128)}, f32[2,64,512]{2,1,0:T(8,128)S(1)}, u32[]{:S(2)}) copy-start(f32[2,64,512]{2,1,0:T(8,128)S(1)} %collective-permute-done.24) | copy-start | bytes 786436
  77.6 12.9 %collective-permute-start.12 = (f32[4,64,512]{2,1,0:T(8,128)S(1)}, f32[4,64,512]{2,1,0:T(8,128)}, u32[]{:S(2)}, u32[]{:S(2)}) collective-permute-start(f32[4,64,512]{2,1,0:T(8,128)S(1)} %pad_maximum_fusion.3), channel_id=1, source_target_pairs={{0,1},{1,0},{2,3},{3,2},{4,5},{5,4},{6,7},{7,6},{8,9},{9,8},{10,11... | collective-permute-start | bytes 1572872 | tf_op jit(solution)/shard_map/ppermute | solution.py:135
  78.8 17.2 %collective-permute-start.15 = (f32[4,64,512]{2,1,0:T(8,128)S(1)}, f32[4,64,512]{2,1,0:T(8,128)}, u32[]{:S(2)}, u32[]{:S(2)}) collective-permute-start(f32[4,64,512]{2,1,0:T(8,128)S(1)} %collective-permute-done.11), channel_id=1, source_target_pairs={{0,1},{1,0},{2,3},{3,2},{4,5},{5,4},{6,7},{7,6},{8,9},{9,8},{10,11... | collective-permute-start | bytes 1572872 | tf_op jit(solution)/shard_map/ppermute | solution.py:135
  79.1 16.9 %collective-permute-start.14 = (f32[4,64,512]{2,1,0:T(8,128)S(1)}, f32[4,64,512]{2,1,0:T(8,128)}, u32[]{:S(2)}, u32[]{:S(2)}) collective-permute-start(f32[4,64,512]{2,1,0:T(8,128)S(1)} %collective-permute-done.10), channel_id=1, source_target_pairs={{0,1},{1,0},{2,3},{3,2},{4,5},{5,4},{6,7},{7,6},{8,9},{9,8},{10,11... | collective-permute-start | bytes 1572872 | tf_op jit(solution)/shard_map/ppermute | solution.py:135
  79.3 16.7 %collective-permute-start.13 = (f32[4,64,512]{2,1,0:T(8,128)S(1)}, f32[4,64,512]{2,1,0:T(8,128)}, u32[]{:S(2)}, u32[]{:S(2)}) collective-permute-start(f32[4,64,512]{2,1,0:T(8,128)S(1)} %collective-permute-done.9), channel_id=1, source_target_pairs={{0,1},{1,0},{2,3},{3,2},{4,5},{5,4},{6,7},{7,6},{8,9},{9,8},{10,11... | collective-permute-start | bytes 1572872 | tf_op jit(solution)/shard_map/ppermute | solution.py:135
  84.3 0.7 copy-start.4
  86.2 42.2 %collective-permute-start.28 = (f32[2,4,64,512]{3,2,1,0:T(8,128)S(1)}, f32[2,4,64,512]{3,2,1,0:T(8,128)}, u32[]{:S(2)}, u32[]{:S(2)}) collective-permute-start(f32[2,4,64,512]{3,2,1,0:T(8,128)S(1)} %pad_maximum_fusion.2), channel_id=1, source_target_pairs={{0,64},{64,128},{128,192},{192,0},{1,65},{65,129},{129,193},{193,1... | collective-permute-start | bytes 3145736 | tf_op jit(solution)/shard_map/ppermute | solution.py:84
  90.5 48.2 %collective-permute-start.27 = (f32[2,4,64,512]{3,2,1,0:T(8,128)S(1)}, f32[2,4,64,512]{3,2,1,0:T(8,128)}, u32[]{:S(2)}, u32[]{:S(2)}) collective-permute-start(f32[2,4,64,512]{3,2,1,0:T(8,128)S(1)} %pad_maximum_fusion.2), channel_id=1, source_target_pairs={{0,128},{64,192},{128,0},{192,64},{1,129},{65,193},{129,1},{193,65... | collective-permute-start | bytes 3145736 | tf_op jit(solution)/shard_map/ppermute | solution.py:84
  101.1 26.9 %copy-start.1 = (f32[128,512]{1,0:T(8,128)S(1)}, f32[128,512]{1,0:T(8,128)}, u32[]{:S(2)}) copy-start(f32[128,512]{1,0:T(8,128)} %param.7) | copy-start | bytes 786436
  103.5 4.5 %collective-permute-start.18 = (f32[64,128]{1,0:T(8,128)S(1)}, f32[64,128]{1,0:T(8,128)S(1)}, u32[]{:S(2)}, u32[]{:S(2)}) collective-permute-start(f32[64,128]{1,0:T(8,128)S(1)} %get-tuple-element.25), channel_id=1, source_target_pairs={{0,8},{8,16},{16,24},{24,0},{1,9},{9,17},{17,25},{25,1},{2,10},{10... | collective-permute-start | bytes 98312 | tf_op jit(solution)/shard_map/ppermute | solution.py:84
  103.6 4.4 %collective-permute-start.17 = (f32[64,128]{1,0:T(8,128)S(1)}, f32[64,128]{1,0:T(8,128)S(1)}, u32[]{:S(2)}, u32[]{:S(2)}) collective-permute-start(f32[64,128]{1,0:T(8,128)S(1)} %get-tuple-element.26), channel_id=1, source_target_pairs={{0,16},{8,24},{16,0},{24,8},{1,17},{9,25},{17,1},{25,9},{2,18},{10... | collective-permute-start | bytes 98312 | tf_op jit(solution)/shard_map/ppermute | solution.py:84
  106.3 3.2 %collective-permute-start.16 = (f32[64,128]{1,0:T(8,128)S(1)}, f32[64,128]{1,0:T(8,128)S(1)}, u32[]{:S(2)}, u32[]{:S(2)}) collective-permute-start(f32[64,128]{1,0:T(8,128)S(1)} %get-tuple-element.27), channel_id=1, source_target_pairs={{0,24},{8,0},{16,8},{24,16},{1,25},{9,1},{17,9},{25,17},{2,26},{10... | collective-permute-start | bytes 98312 | tf_op jit(solution)/shard_map/ppermute | solution.py:84
  109.5 8.0 %collective-permute-start.22 = (f32[4,64,128]{2,1,0:T(8,128)S(1)}, f32[4,64,128]{2,1,0:T(8,128)S(1)}, u32[]{:S(2)}, u32[]{:S(2)}) collective-permute-start(f32[4,64,128]{2,1,0:T(8,128)S(1)} %get-tuple-element.23), channel_id=1, source_target_pairs={{0,2},{2,4},{4,6},{6,0},{1,3},{3,5},{5,7},{7,1},{8,10},{10,12},{12... | collective-permute-start | bytes 393224 | tf_op jit(solution)/shard_map/ppermute | solution.py:84
  109.6 9.7 %collective-permute-start.21 = (f32[4,64,128]{2,1,0:T(8,128)S(1)}, f32[4,64,128]{2,1,0:T(8,128)S(1)}, u32[]{:S(2)}, u32[]{:S(2)}) collective-permute-start(f32[4,64,128]{2,1,0:T(8,128)S(1)} %get-tuple-element.23), channel_id=1, source_target_pairs={{0,4},{2,6},{4,0},{6,2},{1,5},{3,7},{5,1},{7,3},{8,12},{10,14},{12... | collective-permute-start | bytes 393224 | tf_op jit(solution)/shard_map/ppermute | solution.py:84
  112.3 13.9 %collective-permute-start.20 = (f32[4,64,128]{2,1,0:T(8,128)S(1)}, f32[4,64,128]{2,1,0:T(8,128)S(1)}, u32[]{:S(2)}, u32[]{:S(2)}) collective-permute-start(f32[4,64,128]{2,1,0:T(8,128)S(1)} %get-tuple-element.23), channel_id=1, source_target_pairs={{0,6},{2,0},{4,2},{6,4},{1,7},{3,1},{5,3},{7,5},{8,14},{10,8},{12,... | collective-permute-start | bytes 393224 | tf_op jit(solution)/shard_map/ppermute | solution.py:84
  117.5 26.2 %collective-permute-start.26 = (f32[2,4,64,512]{3,2,1,0:T(8,128)S(1)}, f32[2,4,64,512]{3,2,1,0:T(8,128)S(1)}, u32[]{:S(2)}, u32[]{:S(2)}) collective-permute-start(f32[2,4,64,512]{3,2,1,0:T(8,128)S(1)} %pad_maximum_fusion.2), channel_id=1, source_target_pairs={{0,192},{64,0},{128,64},{192,128},{1,193},{65,1},{129,65},{193,129... | collective-permute-start | bytes 3145736 | tf_op jit(solution)/shard_map/ppermute | solution.py:84
  119.2 8.7 %collective-permute-start.19 = (f32[64,512]{1,0:T(8,128)S(1)}, f32[64,512]{1,0:T(8,128)}, u32[]{:S(2)}, u32[]{:S(2)}) collective-permute-start(f32[64,512]{1,0:T(8,128)S(1)} %fusion.13), channel_id=1, source_target_pairs={{0,0},{1,32},{2,64},{3,96},{4,128},{5,160},{6,192},{7,224},{8,8},{... | collective-permute-start | bytes 393224 | tf_op jit(solution)/shard_map/ppermute | solution.py:94
  126.2 14.0 %collective-permute-start.29 = (f32[4,4,64,128]{3,2,1,0:T(8,128)S(1)}, f32[4,4,64,128]{3,2,1,0:T(8,128)S(1)}, u32[]{:S(2)}, u32[]{:S(2)}) collective-permute-start(f32[4,4,64,128]{3,2,1,0:T(8,128)S(1)} %pad_maximum_fusion.4), channel_id=1, source_target_pairs={{0,1},{1,0},{2,3},{3,2},{4,5},{5,4},{6,7},{7,6},{8,9},{9,8},{10,11... | collective-permute-start | bytes 1572872 | tf_op jit(solution)/shard_map/ppermute | solution.py:146

commit v6 on v4

--- a/solution.py
+++ b/solution.py
@@ -13,7 +13,7 @@
 COLS = ("zh", "core")
 GROUP = ("x", "zl")
 SWAP = [(0, 1), (1, 0)]
-HI = lax.Precision.HIGHEST
+HI = lax.Precision.HIGH
 
 
 def class_kernel(structure, root, out):
@@ -147,7 +147,9 @@
     share = dot(near.reshape(256, 512), pairs[:, 0].reshape(256, 512), 0)
     share = share + dot(far.reshape(256, 512), pairs[:, 1].reshape(256, 512), 0)
     share, cross = lax.optimization_barrier((share, cross))
-    got = lax.all_to_all(share.reshape(4, 128, 512), "y", 0, 0)
+    y = lax.axis_index("y")
+    slabs = share.reshape(4, 128, 512)
+    got = [at(slabs, y)] + [shift(at(slabs, (y + k) % 4), "y", k) for k in (1, 2, 3)]
     child = child_diag - (got[0] + got[1] + got[2] + got[3])
     return turn(cross, 0), child
 

time: 131 us -> 125 us (0.954)
  waiting for transfers between devices: 38.5 us -> 35 us
  matrix products: 7.4 us -> 4.33 us
    all_to_all x1 -> x0, waiting for transfers between devices: 6.45 us -> none  [per_device(): got = lax.all_to_all(share.reshape(4, 128, 512), 'y', 0, 0)]
    all_to_all x1 -> x0, starting transfers between devices: 3.51 us -> none  [per_device(): got = lax.all_to_all(share.reshape(4, 128, 512), 'y', 0, 0)]
    dot_general x4, matrix products: 7.4 us -> 4.33 us  [dot(): lax.dot_general(first, second, (((axis,), (0,)), ((), ())), precision=HI,...]
    ppermute x12 -> x15, waiting for transfers between devices: 16.2 us -> 19.1 us  [shift(): return lax.ppermute(block, axis, [(i, (i + k) % 4) for i in range(4)])]
    ppermute x12 -> x15, starting transfers between devices: 24.2 us -> 27 us  [shift(): return lax.ppermute(block, axis, [(i, (i + k) % 4) for i in range(4)])]
  transfers between devices with their start and end apart: 27 -> 29, of which waited for: 12 -> 13; matrix products, arithmetic and copies ran while one was open for 10% -> 9% of each run, Pallas kernels for 3% -> 3%
where the time goes in v6:
time: 125 us; the launch traced here: 124 us
  starting transfers between devices  66.8 us (53%)
  waiting for transfers between devices  35 us (28%)
  Pallas kernels  6.16 us (5%)
  other arithmetic  5.75 us (5%)
  local copies, waits for them, and re-layouts  4.74 us (4%)
  matrix products  4.33 us (3%)
    ppermute x15, starting transfers between devices, shift(): return lax.ppermute(block, axis, [(i, (i + k) % 4) for i in range(4)])  27 us
    ppermute x5, starting transfers between devices, turn(): return lax.ppermute(block, AXES, pairs)  19.2 us
    ppermute x15, waiting for transfers between devices, shift(): return lax.ppermute(block, axis, [(i, (i + k) % 4) for i in range(4)])  19.1 us
    ppermute x5, waiting for transfers between devices, turn(): return lax.ppermute(block, AXES, pairs)  13.1 us
    all_to_all x1, starting transfers between devices, per_device(): pieces = lax.all_to_all(sends.reshape(32, 8, 768), CLASSED, 0, 0)  9.23 us
    pallas_call x3, Pallas kernels, call(): pl.pallas_call(kernel, out_shape=shapes, in_specs=[smem()] + [vmem()] * l...  6.16 us
    dot_general x4, matrix products, dot(): lax.dot_general(first, second, (((axis,), (0,)), ((), ())), precision=HI,...  4.33 us
    all_to_all x1, starting transfers between devices, per_device(): lax.all_to_all(jnp.broadcast_to(piece[None], (8, 8, 2048)), GROUP, 0, 0)  3.97 us
  transfers between devices with their start and end apart: 29, of which 13 were waited for; matrix products, arithmetic and copies ran while one was open for 9% of the time, Pallas kernels for 3%

profile of v6, /device:TPU:1, one launch (start us, length us, event | category | flops | bytes accessed | tf_op | source)
XLA Modules:
  0.0 123.7 jit_solution(7656209152819031396)
XLA Ops:
  0.6 2.2 %shard_map.59 = f32[4,64,768]{2,1,0:T(8,128)} custom-call(s32[16]{0:T(128)} %structure.5, f32[192,768]{1,0:T(8,128)} %root.1), custom_call_target="tpu_custom_call" | custom-call | tf_op jit(solution)/shard_map/pallas_call | solution.py:102
  2.8 9.2 %all-to-all-start = ((f32[32,8,768]{2,1,0:T(8,128)}), f32[32,8,768]{2,1,0:T(8,128)S(1)}, u32[]{:S(2)}, u32[]{:S(2)}) async-start(f32[32,8,768]{2,1,0:T(8,128)} %bitcast.67), calls=%async_computation | async-start | bytes 1572864 | tf_op jit(solution)/shard_map/all_to_all | solution.py:121
  12.1 4.3 %collective-permute-start = (f32[64,512]{1,0:T(8,128)S(1)}, f32[64,512]{1,0:T(8,128)S(1)}, u32[]{:S(2)}, u32[]{:S(2)}) collective-permute-start(f32[64,512]{1,0:T(8,128)S(1)} %copy-done.2), channel_id=1, source_target_pairs={{0,0},{1,32},{2,64},{3,96},{4,128},{5,160},{6,192},{7,224},{8,8},{... | collective-permute-start | bytes 393224 | tf_op jit(solution)/shard_map/ppermute | solution.py:94
  16.3 4.0 %collective-permute-start.1 = (f32[64,512]{1,0:T(8,128)S(1)}, f32[64,512]{1,0:T(8,128)S(1)}, u32[]{:S(2)}, u32[]{:S(2)}) collective-permute-start(f32[64,512]{1,0:T(8,128)S(1)} %copy-done.2), channel_id=1, source_target_pairs={{0,6},{1,38},{2,70},{3,102},{4,134},{5,166},{6,198},{7,230},{8,14}... | collective-permute-start | bytes 393224 | tf_op jit(solution)/shard_map/ppermute | solution.py:94
  20.4 5.6 %collective-permute-start.2 = (f32[64,512]{1,0:T(8,128)S(1)}, f32[64,512]{1,0:T(8,128)S(1)}, u32[]{:S(2)}, u32[]{:S(2)}) collective-permute-start(f32[64,512]{1,0:T(8,128)S(1)} %copy-done.2), channel_id=1, source_target_pairs={{0,4},{1,36},{2,68},{3,100},{4,132},{5,164},{6,196},{7,228},{8,12}... | collective-permute-start | bytes 393224 | tf_op jit(solution)/shard_map/ppermute | solution.py:94
  26.0 1.2 collective-permute-start.3
  27.2 1.7 %collective-permute-done = f32[64,512]{1,0:T(8,128)S(1)} collective-permute-done((f32[64,512]{1,0:T(8,128)S(1)}, f32[64,512]{1,0:T(8,128)S(1)}, u32[]{:S(2)}, u32[]{:S(2)}) %collective-permute-start) | collective-permute-done | bytes 131104 | tf_op jit(solution)/shard_map/ppermute | solution.py:94
  28.9 2.3 %collective-permute-done.2 = f32[64,512]{1,0:T(8,128)S(1)} collective-permute-done((f32[64,512]{1,0:T(8,128)S(1)}, f32[64,512]{1,0:T(8,128)S(1)}, u32[]{:S(2)}, u32[]{:S(2)}) %collective-permute-start.2) | collective-permute-done | bytes 131104 | tf_op jit(solution)/shard_map/ppermute | solution.py:94
  31.3 4.1 %collective-permute-done.3 = f32[64,512]{1,0:T(8,128)S(1)} collective-permute-done((f32[64,512]{1,0:T(8,128)S(1)}, f32[64,512]{1,0:T(8,128)S(1)}, u32[]{:S(2)}, u32[]{:S(2)}) %collective-permute-start.3) | collective-permute-done | bytes 131104 | tf_op jit(solution)/shard_map/ppermute | solution.py:94
  35.5 2.9 %collective-permute-start.9 = (f32[4,64,512]{2,1,0:T(8,128)S(1)}, f32[4,64,512]{2,1,0:T(8,128)S(1)}, u32[]{:S(2)}, u32[]{:S(2)}) collective-permute-start(f32[4,64,512]{2,1,0:T(8,128)S(1)} %get-tuple-element.38), channel_id=1, source_target_pairs={{0,16},{8,24},{16,0},{24,8},{1,17},{9,25},{17,1},{25,9},{2,18},{10... | collective-permute-start | bytes 1572872 | tf_op jit(solution)/shard_map/ppermute | solution.py:84
  38.7 2.3 %collective-permute-start.8 = (f32[4,64,512]{2,1,0:T(8,128)S(1)}, f32[4,64,512]{2,1,0:T(8,128)}, u32[]{:S(2)}, u32[]{:S(2)}) collective-permute-start(f32[4,64,512]{2,1,0:T(8,128)S(1)} %get-tuple-element.38), channel_id=1, source_target_pairs={{0,24},{8,0},{16,8},{24,16},{1,25},{9,1},{17,9},{25,17},{2,26},{10... | collective-permute-start | bytes 1572872 | tf_op jit(solution)/shard_map/ppermute | solution.py:84
  41.0 1.9 %shard_map.60 = (f32[2,8,768]{2,1,0:T(8,128)}, f32[2,8,768]{2,1,0:T(8,128)}, f32[2,8,768]{2,1,0:T(8,128)}, f32[2,8,768]{2,1,0:T(8,128)}) custom-call(s32[16]{0:T(128)} %structure.5, f32[32,8,768]{2,1,0:T(8,128)} %copy-done), custom_call_target="tpu_custom_call" | custom-call | tf_op jit(solution)/shard_map/pallas_call | solution.py:102
  43.0 3.2 %collective-permute-start.6 = (f32[2,8,768]{2,1,0:T(8,128)}, f32[2,8,768]{2,1,0:T(8,128)S(1)}, u32[]{:S(2)}, u32[]{:S(2)}) collective-permute-start(f32[2,8,768]{2,1,0:T(8,128)} %get-tuple-element.21), channel_id=1, source_target_pairs={{0,6},{2,0},{4,2},{6,4},{1,7},{3,1},{5,3},{7,5},{8,14},{10,8},{12,... | collective-permute-start | bytes 147464 | tf_op jit(solution)/shard_map/ppermute | solution.py:84
  46.1 5.6 %collective-permute-start.5 = (f32[2,8,768]{2,1,0:T(8,128)}, f32[2,8,768]{2,1,0:T(8,128)S(1)}, u32[]{:S(2)}, u32[]{:S(2)}) collective-permute-start(f32[2,8,768]{2,1,0:T(8,128)} %get-tuple-element.20), channel_id=1, source_target_pairs={{0,4},{2,6},{4,0},{6,2},{1,5},{3,7},{5,1},{7,3},{8,12},{10,14},{12... | collective-permute-start | bytes 147464 | tf_op jit(solution)/shard_map/ppermute | solution.py:84
  51.7 0.7 constant_dynamic-slice_fusion.3
  52.5 1.5 %collective-permute-start.4 = (f32[2,8,768]{2,1,0:T(8,128)}, f32[2,8,768]{2,1,0:T(8,128)S(1)}, u32[]{:S(2)}, u32[]{:S(2)}) collective-permute-start(f32[2,8,768]{2,1,0:T(8,128)} %get-tuple-element.19), channel_id=1, source_target_pairs={{0,2},{2,4},{4,6},{6,0},{1,3},{3,5},{5,7},{7,1},{8,10},{10,12},{12... | collective-permute-start | bytes 147464 | tf_op jit(solution)/shard_map/ppermute | solution.py:84
  54.0 4.3 %collective-permute-done.4.one = f32[2,8,768]{2,1,0:T(8,128)S(1)} collective-permute-done((f32[2,8,768]{2,1,0:T(8,128)}, f32[2,8,768]{2,1,0:T(8,128)S(1)}, u32[]{:S(2)}, u32[]{:S(2)}) %collective-permute-start.4) | collective-permute-done | bytes 49184 | tf_op jit(solution)/shard_map/ppermute | solution.py:84
  58.4 1.8 %collective-permute-start.7 = (f32[4,8,768]{2,1,0:T(8,128)S(1)}, f32[4,8,768]{2,1,0:T(8,128)S(1)}, u32[]{:S(2)}, u32[]{:S(2)}) collective-permute-start(f32[4,8,768]{2,1,0:T(8,128)S(1)} %pad_maximum_fusion.6), channel_id=1, source_target_pairs={{0,1},{1,0},{2,3},{3,2},{4,5},{5,4},{6,7},{7,6},{8,9},{9,8},{10,11... | collective-permute-start | bytes 294920 | tf_op jit(solution)/shard_map/ppermute | solution.py:127
  60.2 0.9 collective-permute-done.7.got
  61.2 0.6 copy-done.6
  61.8 2.1 %shard_map.61 = f32[8,2048]{1,0:T(8,128)} custom-call(s32[16]{0:T(128)} %structure.5, f32[2,8,768]{2,1,0:T(8,128)} %get-tuple-element.18.own, f32[2,8,768]{2,1,0:T(8,128)} %copy-done.5, f32[2,8,768]{2,1,0:T(8,128)} %copy-done.4, f32[2,8,768]{2,1,0:T(8,128)} %copy-done.3, f32[4,8,768]{2,1,0:T(8,128)} %copy-done.6), custom_call_target="tpu_custom_call" | custom-call | tf_op jit(solution)/shard_map/pallas_call | solution.py:102
  63.9 1.7 %broadcast_in_dim.16 = f32[8,8,2048]{2,1,0:T(8,128)} broadcast(f32[8,2048]{1,0:T(8,128)} %shard_map.61), dimensions={1,2} | broadcast | bytes 589824 | tf_op jit(solution)/shard_map/broadcast_in_dim | solution.py:131
  65.6 4.0 %all-to-all-start.1 = ((f32[8,8,2048]{2,1,0:T(8,128)}), f32[8,8,2048]{2,1,0:T(8,128)S(1)}, u32[]{:S(2)}, u32[]{:S(2)}) async-start(f32[8,8,2048]{2,1,0:T(8,128)} %broadcast_in_dim.16), calls=%async_computation.1 | async-start | bytes 1048576 | tf_op jit(solution)/shard_map/all_to_all | solution.py:131
  69.6 0.6 collective-permute-start.11
  70.8 2.0 %collective-permute-start.15 = (f32[64,512]{1,0:T(8,128)S(1)}, f32[64,512]{1,0:T(8,128)S(1)}, u32[]{:S(2)}, u32[]{:S(2)}) collective-permute-start(f32[64,512]{1,0:T(8,128)S(1)} %copy-done.2), channel_id=1, source_target_pairs={{0,32},{32,0},{1,33},{33,1},{2,34},{34,2},{3,35},{35,3},{4,36},{36... | collective-permute-start | bytes 393224 | tf_op jit(solution)/shard_map/ppermute | solution.py:129
  72.8 2.8 %pad_maximum_fusion = f32[4,4,64,512]{3,2,1,0:T(8,128)} fusion(f32[4,1,64,512]{3,2,1,0:T(8,128)} %bitcast.12, f32[4,1,64,512]{3,2,1,0:T(8,128)S(1)} %bitcast.75, f32[4,1,64,512]{3,2,1,0:T(8,128)} %bitcast.9, f32[4,1,64,512]{3,2,1,0:T(8,128)S(1)} %get-tuple-element.37), kind=kLoop, calls=%fused_computation.1 | loop fusion | flops 1572864 | bytes 4194304 | tf_op jit(solution)/shard_map/stack | solution.py:136
  75.7 1.6 %pad_maximum_fusion.1 = f32[4,4,64,512]{3,2,0,1:T(8,128)S(1)} fusion(f32[4,1,64,512]{3,2,0,1:T(8,128)} %bitcast.17, f32[4,1,64,512]{3,2,0,1:T(8,128)} %bitcast.16, f32[4,1,64,512]{3,2,0,1:T(8,128)} %bitcast.15, f32[4,1,64,512]{3,2,0,1:T(8,128)S(1)} %bitcast.76), kind=kLoop, calls=%fused_computation.2 | loop fusion | flops 1572864 | bytes 4194304 | tf_op jit(solution)/shard_map/stack | solution.py:137
  77.5 1.3 %all-to-all-done.1 = f32[8,8,2048]{2,1,0:T(8,128)S(1)} async-done(((f32[8,8,2048]{2,1,0:T(8,128)}), f32[8,8,2048]{2,1,0:T(8,128)S(1)}, u32[]{:S(2)}, u32[]{:S(2)}) %all-to-all-start.1) | async-done | bytes 524320 | tf_op jit(solution)/shard_map/all_to_all | solution.py:131
  78.8 2.3 %fusion.8 = f32[64,512]{1,0:T(8,128)S(1)} fusion(f32[1024,512]{1,0:T(8,128)} %bitcast.64, f32[64,2048]{1,0:T(8,128)S(1)} %bitcast.68), kind=kOutput, calls=%fused_computation.12 | convolution fusion | flops 201326592 | bytes 2490368 | tf_op jit(solution)/shard_map/dot_general | solution.py:66
  81.1 0.8 fusion.5
  81.9 2.5 %collective-permute-start.16 = (f32[64,512]{1,0:T(8,128)S(1)}, f32[64,512]{1,0:T(8,128)S(1)}, u32[]{:S(2)}, u32[]{:S(2)}) collective-permute-start(f32[64,512]{1,0:T(8,128)S(1)} %fusion.5), channel_id=1, source_target_pairs={{0,6},{2,0},{4,2},{6,4},{1,7},{3,1},{5,3},{7,5},{8,14},{10,8},{12,... | collective-permute-start | bytes 393224 | tf_op jit(solution)/shard_map/ppermute | solution.py:84
  84.5 0.9 collective-permute-start.19
  85.7 0.6 collective-permute-start.21
  86.3 3.6 %collective-permute-start.17 = (f32[64,512]{1,0:T(8,128)S(1)}, f32[64,512]{1,0:T(8,128)S(1)}, u32[]{:S(2)}, u32[]{:S(2)}) collective-permute-start(f32[64,512]{1,0:T(8,128)S(1)} %fusion.5), channel_id=1, source_target_pairs={{0,4},{2,6},{4,0},{6,2},{1,5},{3,7},{5,1},{7,3},{8,12},{10,14},{12... | collective-permute-start | bytes 393224 | tf_op jit(solution)/shard_map/ppermute | solution.py:84
  89.9 0.8 collective-permute-done.16
  91.3 4.4 %collective-permute-done.17 = f32[64,512]{1,0:T(8,128)S(1)} collective-permute-done((f32[64,512]{1,0:T(8,128)S(1)}, f32[64,512]{1,0:T(8,128)S(1)}, u32[]{:S(2)}, u32[]{:S(2)}) %collective-permute-start.17) | collective-permute-done | bytes 131104 | tf_op jit(solution)/shard_map/ppermute | solution.py:84
  95.6 6.6 %collective-permute-done.18 = f32[64,512]{1,0:T(8,128)S(1)} collective-permute-done((f32[64,512]{1,0:T(8,128)S(1)}, f32[64,512]{1,0:T(8,128)S(1)}, u32[]{:S(2)}, u32[]{:S(2)}) %collective-permute-start.18) | collective-permute-done | bytes 131104 | tf_op jit(solution)/shard_map/ppermute | solution.py:84
  102.2 2.4 %collective-permute-start.22 = (f32[4,64,512]{2,1,0:T(8,128)S(1)}, f32[4,64,512]{2,1,0:T(8,128)S(1)}, u32[]{:S(2)}, u32[]{:S(2)}) collective-permute-start(f32[4,64,512]{2,1,0:T(8,128)S(1)} %pad_maximum_fusion.4), channel_id=1, source_target_pairs={{0,1},{1,0},{2,3},{3,2},{4,5},{5,4},{6,7},{7,6},{8,9},{9,8},{10,11... | collective-permute-start | bytes 1572872 | tf_op jit(solution)/shard_map/ppermute | solution.py:143
  104.7 0.6 gather_fusion
  106.1 0.6 fusion.19
  106.8 0.6 convolution_add_fusion
  107.6 1.0 collective-permute-start.25
  108.5 1.7 %collective-permute-start.26 = (f32[128,512]{1,0:T(8,128)S(1)}, f32[128,512]{1,0:T(8,128)S(1)}, u32[]{:S(2)}, u32[]{:S(2)}) collective-permute-start(f32[128,512]{1,0:T(8,128)S(1)} %get-tuple-element.33), channel_id=1, source_target_pairs={{0,24},{8,0},{16,8},{24,16},{1,25},{9,1},{17,9},{25,17},{2,26},{10... | collective-permute-start | bytes 786440 | tf_op jit(solution)/shard_map/ppermute | solution.py:84
  110.2 4.0 %collective-permute-start.23 = (f32[64,512]{1,0:T(8,128)S(1)}, f32[64,512]{1,0:T(8,128)S(1)}, u32[]{:S(2)}, u32[]{:S(2)}) collective-permute-start(f32[64,512]{1,0:T(8,128)S(1)} %fusion.5), channel_id=1, source_target_pairs={{0,0},{1,32},{2,64},{3,96},{4,128},{5,160},{6,192},{7,224},{8,8},{... | collective-permute-start | bytes 393224 | tf_op jit(solution)/shard_map/ppermute | solution.py:94
  114.3 4.9 %collective-permute-done.23 = f32[64,512]{1,0:T(8,128)S(1)} collective-permute-done((f32[64,512]{1,0:T(8,128)S(1)}, f32[64,512]{1,0:T(8,128)S(1)}, u32[]{:S(2)}, u32[]{:S(2)}) %collective-permute-start.23) | collective-permute-done | bytes 131104 | tf_op jit(solution)/shard_map/ppermute | solution.py:94
  119.2 2.7 %collective-permute-done.24 = f32[128,512]{1,0:T(8,128)S(1)} collective-permute-done((f32[128,512]{1,0:T(8,128)S(1)}, f32[128,512]{1,0:T(8,128)S(1)}, u32[]{:S(2)}, u32[]{:S(2)}) %collective-permute-start.24) | collective-permute-done | bytes 262176 | tf_op jit(solution)/shard_map/ppermute | solution.py:84
  122.3 0.8 fusion.12
  123.1 0.7 copy.11
  (54 shorter events, 3.6 us)
Async XLA Ops:
  0.6 11.4 %copy-start.2 = (f32[64,512]{1,0:T(8,128)S(1)}, f32[64,512]{1,0:T(8,128)}, u32[]{:S(2)}) copy-start(f32[64,512]{1,0:T(8,128)} %param.6) | copy-start | bytes 393220
  2.8 32.6 %all-to-all-start = ((f32[32,8,768]{2,1,0:T(8,128)}), f32[32,8,768]{2,1,0:T(8,128)S(1)}, u32[]{:S(2)}, u32[]{:S(2)}) async-start(f32[32,8,768]{2,1,0:T(8,128)} %bitcast.67), calls=%async_computation | async-start | bytes 1572864 | tf_op jit(solution)/shard_map/all_to_all | solution.py:121
  12.1 16.9 %collective-permute-start = (f32[64,512]{1,0:T(8,128)S(1)}, f32[64,512]{1,0:T(8,128)S(1)}, u32[]{:S(2)}, u32[]{:S(2)}) collective-permute-start(f32[64,512]{1,0:T(8,128)S(1)} %copy-done.2), channel_id=1, source_target_pairs={{0,0},{1,32},{2,64},{3,96},{4,128},{5,160},{6,192},{7,224},{8,8},{... | collective-permute-start | bytes 393224 | tf_op jit(solution)/shard_map/ppermute | solution.py:94
  16.3 12.6 %collective-permute-start.1 = (f32[64,512]{1,0:T(8,128)S(1)}, f32[64,512]{1,0:T(8,128)S(1)}, u32[]{:S(2)}, u32[]{:S(2)}) collective-permute-start(f32[64,512]{1,0:T(8,128)S(1)} %copy-done.2), channel_id=1, source_target_pairs={{0,6},{1,38},{2,70},{3,102},{4,134},{5,166},{6,198},{7,230},{8,14}... | collective-permute-start | bytes 393224 | tf_op jit(solution)/shard_map/ppermute | solution.py:94
  20.4 10.9 %collective-permute-start.2 = (f32[64,512]{1,0:T(8,128)S(1)}, f32[64,512]{1,0:T(8,128)S(1)}, u32[]{:S(2)}, u32[]{:S(2)}) collective-permute-start(f32[64,512]{1,0:T(8,128)S(1)} %copy-done.2), channel_id=1, source_target_pairs={{0,4},{1,36},{2,68},{3,100},{4,132},{5,164},{6,196},{7,228},{8,12}... | collective-permute-start | bytes 393224 | tf_op jit(solution)/shard_map/ppermute | solution.py:94
  26.0 9.4 %collective-permute-start.3 = (f32[64,512]{1,0:T(8,128)S(1)}, f32[64,512]{1,0:T(8,128)S(1)}, u32[]{:S(2)}, u32[]{:S(2)}) collective-permute-start(f32[64,512]{1,0:T(8,128)S(1)} %copy-done.2), channel_id=1, source_target_pairs={{0,2},{1,34},{2,66},{3,98},{4,130},{5,162},{6,194},{7,226},{8,10},... | collective-permute-start | bytes 393224 | tf_op jit(solution)/shard_map/ppermute | solution.py:94
  35.4 5.7 %copy-start = (f32[32,8,768]{2,1,0:T(8,128)}, f32[32,8,768]{2,1,0:T(8,128)S(1)}, u32[]{:S(2)}) copy-start(f32[32,8,768]{2,1,0:T(8,128)S(1)} %all-to-all-done.pieces) | copy-start | bytes 2359300
  35.5 34.8 %collective-permute-start.9 = (f32[4,64,512]{2,1,0:T(8,128)S(1)}, f32[4,64,512]{2,1,0:T(8,128)S(1)}, u32[]{:S(2)}, u32[]{:S(2)}) collective-permute-start(f32[4,64,512]{2,1,0:T(8,128)S(1)} %get-tuple-element.38), channel_id=1, source_target_pairs={{0,16},{8,24},{16,0},{24,8},{1,17},{9,25},{17,1},{25,9},{2,18},{10... | collective-permute-start | bytes 1572872 | tf_op jit(solution)/shard_map/ppermute | solution.py:84
  38.4 32.4 %collective-permute-start.10 = (f32[4,64,512]{2,1,0:T(8,128)S(1)}, f32[4,64,512]{2,1,0:T(8,128)}, u32[]{:S(2)}, u32[]{:S(2)}) collective-permute-start(f32[4,64,512]{2,1,0:T(8,128)S(1)} %get-tuple-element.38), channel_id=1, source_target_pairs={{0,8},{8,16},{16,24},{24,0},{1,9},{9,17},{17,25},{25,1},{2,10},{10... | collective-permute-start | bytes 1572872 | tf_op jit(solution)/shard_map/ppermute | solution.py:84
  38.7 31.5 %collective-permute-start.8 = (f32[4,64,512]{2,1,0:T(8,128)S(1)}, f32[4,64,512]{2,1,0:T(8,128)}, u32[]{:S(2)}, u32[]{:S(2)}) collective-permute-start(f32[4,64,512]{2,1,0:T(8,128)S(1)} %get-tuple-element.38), channel_id=1, source_target_pairs={{0,24},{8,0},{16,8},{24,16},{1,25},{9,1},{17,9},{25,17},{2,26},{10... | collective-permute-start | bytes 1572872 | tf_op jit(solution)/shard_map/ppermute | solution.py:84
  43.0 9.5 %collective-permute-start.6 = (f32[2,8,768]{2,1,0:T(8,128)}, f32[2,8,768]{2,1,0:T(8,128)S(1)}, u32[]{:S(2)}, u32[]{:S(2)}) collective-permute-start(f32[2,8,768]{2,1,0:T(8,128)} %get-tuple-element.21), channel_id=1, source_target_pairs={{0,6},{2,0},{4,2},{6,4},{1,7},{3,1},{5,3},{7,5},{8,14},{10,8},{12,... | collective-permute-start | bytes 147464 | tf_op jit(solution)/shard_map/ppermute | solution.py:84
  46.1 7.9 %collective-permute-start.5 = (f32[2,8,768]{2,1,0:T(8,128)}, f32[2,8,768]{2,1,0:T(8,128)S(1)}, u32[]{:S(2)}, u32[]{:S(2)}) collective-permute-start(f32[2,8,768]{2,1,0:T(8,128)} %get-tuple-element.20), channel_id=1, source_target_pairs={{0,4},{2,6},{4,0},{6,2},{1,5},{3,7},{5,1},{7,3},{8,12},{10,14},{12... | collective-permute-start | bytes 147464 | tf_op jit(solution)/shard_map/ppermute | solution.py:84
  52.5 8.7 %copy-start.3 = (f32[2,8,768]{2,1,0:T(8,128)}, f32[2,8,768]{2,1,0:T(8,128)S(1)}, u32[]{:S(2)}) copy-start(f32[2,8,768]{2,1,0:T(8,128)S(1)} %collective-permute-done.6.three) | copy-start | bytes 147460
  52.5 5.9 %collective-permute-start.4 = (f32[2,8,768]{2,1,0:T(8,128)}, f32[2,8,768]{2,1,0:T(8,128)S(1)}, u32[]{:S(2)}, u32[]{:S(2)}) collective-permute-start(f32[2,8,768]{2,1,0:T(8,128)} %get-tuple-element.19), channel_id=1, source_target_pairs={{0,2},{2,4},{4,6},{6,0},{1,3},{3,5},{5,7},{7,1},{8,10},{10,12},{12... | collective-permute-start | bytes 147464 | tf_op jit(solution)/shard_map/ppermute | solution.py:84
  54.0 7.2 %copy-start.4 = (f32[2,8,768]{2,1,0:T(8,128)}, f32[2,8,768]{2,1,0:T(8,128)S(1)}, u32[]{:S(2)}) copy-start(f32[2,8,768]{2,1,0:T(8,128)S(1)} %collective-permute-done.5.two) | copy-start | bytes 147460
  58.4 2.8 %copy-start.5 = (f32[2,8,768]{2,1,0:T(8,128)}, f32[2,8,768]{2,1,0:T(8,128)S(1)}, u32[]{:S(2)}) copy-start(f32[2,8,768]{2,1,0:T(8,128)S(1)} %collective-permute-done.4.one) | copy-start | bytes 147460
  58.4 2.8 %collective-permute-start.7 = (f32[4,8,768]{2,1,0:T(8,128)S(1)}, f32[4,8,768]{2,1,0:T(8,128)S(1)}, u32[]{:S(2)}, u32[]{:S(2)}) collective-permute-start(f32[4,8,768]{2,1,0:T(8,128)S(1)} %pad_maximum_fusion.6), channel_id=1, source_target_pairs={{0,1},{1,0},{2,3},{3,2},{4,5},{5,4},{6,7},{7,6},{8,9},{9,8},{10,11... | collective-permute-start | bytes 294920 | tf_op jit(solution)/shard_map/ppermute | solution.py:127
  61.2 0.6 copy-start.6
  65.6 13.2 %all-to-all-start.1 = ((f32[8,8,2048]{2,1,0:T(8,128)}), f32[8,8,2048]{2,1,0:T(8,128)S(1)}, u32[]{:S(2)}, u32[]{:S(2)}) async-start(f32[8,8,2048]{2,1,0:T(8,128)} %broadcast_in_dim.16), calls=%async_computation.1 | async-start | bytes 1048576 | tf_op jit(solution)/shard_map/all_to_all | solution.py:131
  69.6 6.1 %collective-permute-start.11 = (f32[4,64,512]{2,1,0:T(8,128)S(1)}, f32[4,64,512]{2,1,0:T(8,128)S(1)}, u32[]{:S(2)}, u32[]{:S(2)}) collective-permute-start(f32[4,64,512]{2,1,0:T(8,128)S(1)} %get-tuple-element.38), channel_id=1, source_target_pairs={{0,1},{1,0},{2,3},{3,2},{4,5},{5,4},{6,7},{7,6},{8,9},{9,8},{10,11... | collective-permute-start | bytes 1572872 | tf_op jit(solution)/shard_map/ppermute | solution.py:135
  70.2 5.4 %collective-permute-start.12 = (f32[4,64,512]{2,1,0:T(8,128)}, f32[4,64,512]{2,1,0:T(8,128)}, u32[]{:S(2)}, u32[]{:S(2)}) collective-permute-start(f32[4,64,512]{2,1,0:T(8,128)} %collective-permute-done.8), channel_id=1, source_target_pairs={{0,1},{1,0},{2,3},{3,2},{4,5},{5,4},{6,7},{7,6},{8,9},{9,8},{10,11... | collective-permute-start | bytes 1572872 | tf_op jit(solution)/shard_map/ppermute | solution.py:135
  70.3 5.3 %collective-permute-start.13 = (f32[4,64,512]{2,1,0:T(8,128)S(1)}, f32[4,64,512]{2,1,0:T(8,128)}, u32[]{:S(2)}, u32[]{:S(2)}) collective-permute-start(f32[4,64,512]{2,1,0:T(8,128)S(1)} %collective-permute-done.9), channel_id=1, source_target_pairs={{0,1},{1,0},{2,3},{3,2},{4,5},{5,4},{6,7},{7,6},{8,9},{9,8},{10,11... | collective-permute-start | bytes 1572872 | tf_op jit(solution)/shard_map/ppermute | solution.py:135
  70.7 4.9 %collective-permute-start.14 = (f32[4,64,512]{2,1,0:T(8,128)}, f32[4,64,512]{2,1,0:T(8,128)}, u32[]{:S(2)}, u32[]{:S(2)}) collective-permute-start(f32[4,64,512]{2,1,0:T(8,128)} %collective-permute-done.10), channel_id=1, source_target_pairs={{0,1},{1,0},{2,3},{3,2},{4,5},{5,4},{6,7},{7,6},{8,9},{9,8},{10,11... | collective-permute-start | bytes 1572872 | tf_op jit(solution)/shard_map/ppermute | solution.py:135
  70.8 11.1 %collective-permute-start.15 = (f32[64,512]{1,0:T(8,128)S(1)}, f32[64,512]{1,0:T(8,128)S(1)}, u32[]{:S(2)}, u32[]{:S(2)}) collective-permute-start(f32[64,512]{1,0:T(8,128)S(1)} %copy-done.2), channel_id=1, source_target_pairs={{0,32},{32,0},{1,33},{33,1},{2,34},{34,2},{3,35},{35,3},{4,36},{36... | collective-permute-start | bytes 393224 | tf_op jit(solution)/shard_map/ppermute | solution.py:129
  81.9 8.8 %collective-permute-start.16 = (f32[64,512]{1,0:T(8,128)S(1)}, f32[64,512]{1,0:T(8,128)S(1)}, u32[]{:S(2)}, u32[]{:S(2)}) collective-permute-start(f32[64,512]{1,0:T(8,128)S(1)} %fusion.5), channel_id=1, source_target_pairs={{0,6},{2,0},{4,2},{6,4},{1,7},{3,1},{5,3},{7,5},{8,14},{10,8},{12,... | collective-permute-start | bytes 393224 | tf_op jit(solution)/shard_map/ppermute | solution.py:84
  84.5 20.1 %collective-permute-start.19 = (f32[2,64,512]{2,1,0:T(8,128)S(1)}, f32[2,64,512]{2,1,0:T(8,128)S(1)}, u32[]{:S(2)}, u32[]{:S(2)}) collective-permute-start(f32[2,64,512]{2,1,0:T(8,128)S(1)} %get-tuple-element.40), channel_id=1, source_target_pairs={{0,192},{64,0},{128,64},{192,128},{1,193},{65,1},{129,65},{193,129... | collective-permute-start | bytes 786440 | tf_op jit(solution)/shard_map/ppermute | solution.py:84
  85.4 19.2 %collective-permute-start.20 = (f32[2,64,512]{2,1,0:T(8,128)S(1)}, f32[2,64,512]{2,1,0:T(8,128)S(1)}, u32[]{:S(2)}, u32[]{:S(2)}) collective-permute-start(f32[2,64,512]{2,1,0:T(8,128)S(1)} %get-tuple-element.40), channel_id=1, source_target_pairs={{0,128},{64,192},{128,0},{192,64},{1,129},{65,193},{129,1},{193,65... | collective-permute-start | bytes 786440 | tf_op jit(solution)/shard_map/ppermute | solution.py:84
  85.7 18.9 %collective-permute-start.21 = (f32[2,64,512]{2,1,0:T(8,128)S(1)}, f32[2,64,512]{2,1,0:T(8,128)S(1)}, u32[]{:S(2)}, u32[]{:S(2)}) collective-permute-start(f32[2,64,512]{2,1,0:T(8,128)S(1)} %get-tuple-element.40), channel_id=1, source_target_pairs={{0,64},{64,128},{128,192},{192,0},{1,65},{65,129},{129,193},{193,1... | collective-permute-start | bytes 786440 | tf_op jit(solution)/shard_map/ppermute | solution.py:84
  86.3 9.4 %collective-permute-start.17 = (f32[64,512]{1,0:T(8,128)S(1)}, f32[64,512]{1,0:T(8,128)S(1)}, u32[]{:S(2)}, u32[]{:S(2)}) collective-permute-start(f32[64,512]{1,0:T(8,128)S(1)} %fusion.5), channel_id=1, source_target_pairs={{0,4},{2,6},{4,0},{6,2},{1,5},{3,7},{5,1},{7,3},{8,12},{10,14},{12... | collective-permute-start | bytes 393224 | tf_op jit(solution)/shard_map/ppermute | solution.py:84
  90.7 11.5 %collective-permute-start.18 = (f32[64,512]{1,0:T(8,128)S(1)}, f32[64,512]{1,0:T(8,128)S(1)}, u32[]{:S(2)}, u32[]{:S(2)}) collective-permute-start(f32[64,512]{1,0:T(8,128)S(1)} %fusion.5), channel_id=1, source_target_pairs={{0,2},{2,4},{4,6},{6,0},{1,3},{3,5},{5,7},{7,1},{8,10},{10,12},{12... | collective-permute-start | bytes 393224 | tf_op jit(solution)/shard_map/ppermute | solution.py:84
  102.2 3.9 %collective-permute-start.22 = (f32[4,64,512]{2,1,0:T(8,128)S(1)}, f32[4,64,512]{2,1,0:T(8,128)S(1)}, u32[]{:S(2)}, u32[]{:S(2)}) collective-permute-start(f32[4,64,512]{2,1,0:T(8,128)S(1)} %pad_maximum_fusion.4), channel_id=1, source_target_pairs={{0,1},{1,0},{2,3},{3,2},{4,5},{5,4},{6,7},{7,6},{8,9},{9,8},{10,11... | collective-permute-start | bytes 1572872 | tf_op jit(solution)/shard_map/ppermute | solution.py:143
  106.8 15.5 %copy-start.1 = (f32[128,512]{1,0:T(8,128)S(1)}, f32[128,512]{1,0:T(8,128)}, u32[]{:S(2)}) copy-start(f32[128,512]{1,0:T(8,128)} %param.7) | copy-start | bytes 786436
  107.5 14.4 %collective-permute-start.24 = (f32[128,512]{1,0:T(8,128)S(1)}, f32[128,512]{1,0:T(8,128)S(1)}, u32[]{:S(2)}, u32[]{:S(2)}) collective-permute-start(f32[128,512]{1,0:T(8,128)S(1)} %get-tuple-element.32), channel_id=1, source_target_pairs={{0,8},{8,16},{16,24},{24,0},{1,9},{9,17},{17,25},{25,1},{2,10},{10... | collective-permute-start | bytes 786440 | tf_op jit(solution)/shard_map/ppermute | solution.py:84
  107.6 14.3 %collective-permute-start.25 = (f32[128,512]{1,0:T(8,128)S(1)}, f32[128,512]{1,0:T(8,128)S(1)}, u32[]{:S(2)}, u32[]{:S(2)}) collective-permute-start(f32[128,512]{1,0:T(8,128)S(1)} %get-tuple-element.34), channel_id=1, source_target_pairs={{0,16},{8,24},{16,0},{24,8},{1,17},{9,25},{17,1},{25,9},{2,18},{10... | collective-permute-start | bytes 786440 | tf_op jit(solution)/shard_map/ppermute | solution.py:84
  108.5 13.7 %collective-permute-start.26 = (f32[128,512]{1,0:T(8,128)S(1)}, f32[128,512]{1,0:T(8,128)S(1)}, u32[]{:S(2)}, u32[]{:S(2)}) collective-permute-start(f32[128,512]{1,0:T(8,128)S(1)} %get-tuple-element.33), channel_id=1, source_target_pairs={{0,24},{8,0},{16,8},{24,16},{1,25},{9,1},{17,9},{25,17},{2,26},{10... | collective-permute-start | bytes 786440 | tf_op jit(solution)/shard_map/ppermute | solution.py:84
  110.2 9.0 %collective-permute-start.23 = (f32[64,512]{1,0:T(8,128)S(1)}, f32[64,512]{1,0:T(8,128)S(1)}, u32[]{:S(2)}, u32[]{:S(2)}) collective-permute-start(f32[64,512]{1,0:T(8,128)S(1)} %fusion.5), channel_id=1, source_target_pairs={{0,0},{1,32},{2,64},{3,96},{4,128},{5,160},{6,192},{7,224},{8,8},{... | collective-permute-start | bytes 393224 | tf_op jit(solution)/shard_map/ppermute | solution.py:94

commit v7 on v6

--- a/solution.py
+++ b/solution.py
@@ -59,7 +59,8 @@
                 tiles.append(jnp.where(holder % 2 == core, here, there))
             pair = jnp.concatenate(tiles, axis=1)
             pair = pltpu.roll(pair, (4 - y) % 4 * 64, 1)
-            out[:, (side * 4 + k) * 256:(side * 4 + k + 1) * 256] = pair
+            for copy in range(8):
+                out[copy, :, (side * 4 + k) * 256:(side * 4 + k + 1) * 256] = pair
 
 
 def dot(first, second, axis):
@@ -125,10 +126,10 @@
     landed = [cut[0]] + [shift(cut[k], "zh", k) for k in (1, 2, 3)]
     give = jnp.stack([at(part, 1 - core) for part in landed])
     got = lax.ppermute(give, "core", SWAP)
-    piece = call(columns_kernel, of(8, 2048), structure, *landed, got)
+    copies = call(columns_kernel, of(8, 8, 2048), structure, *landed, got)
     other = lax.ppermute(factor, "zl", SWAP)
 
-    rows = lax.all_to_all(jnp.broadcast_to(piece[None], (8, 8, 2048)), GROUP, 0, 0).reshape(64, 2048)
+    rows = lax.all_to_all(copies, GROUP, 0, 0).reshape(64, 2048)
 
     turned = jnp.stack(turned)
     near = [turned] + [shift(turned, "y", -k) for k in (1, 2, 3)]

time: 125 us -> 125 us (level)
  the two profiles are of different devices: /device:TPU:1 before, /device:TPU:68 now
where the time goes in v7:
time: 125 us; the launch traced here: 124 us
  starting transfers between devices  62.1 us (50%)
  waiting for transfers between devices  40.4 us (32%)
  Pallas kernels  6.34 us (5%)
  other arithmetic  5.64 us (5%)
  local copies, waits for them, and re-layouts  4.45 us (4%)
  matrix products  4.33 us (3%)
    ppermute x15, starting transfers between devices, shift(): return lax.ppermute(block, axis, [(i, (i + k) % 4) for i in range(4)])  30.1 us
    ppermute x5, waiting for transfers between devices, turn(): return lax.ppermute(block, AXES, pairs)  21.8 us
    ppermute x15, waiting for transfers between devices, shift(): return lax.ppermute(block, axis, [(i, (i + k) % 4) for i in range(4)])  15.4 us
    ppermute x5, starting transfers between devices, turn(): return lax.ppermute(block, AXES, pairs)  14.4 us
    all_to_all x1, starting transfers between devices, per_device(): pieces = lax.all_to_all(sends.reshape(32, 8, 768), CLASSED, 0, 0)  8.95 us
    pallas_call x3, Pallas kernels, call(): pl.pallas_call(kernel, out_shape=shapes, in_specs=[smem()] + [vmem()] * l...  6.34 us
    all_to_all x1, starting transfers between devices, per_device(): rows = lax.all_to_all(copies, GROUP, 0, 0).reshape(64, 2048)  5.72 us
    dot_general x4, matrix products, dot(): lax.dot_general(first, second, (((axis,), (0,)), ((), ())), precision=HI,...  4.33 us
  transfers between devices with their start and end apart: 29, of which 11 were waited for; matrix products, arithmetic and copies ran while one was open for 8% of the time, Pallas kernels for 3%

profile of v7, /device:TPU:68, one launch (start us, length us, event | category | flops | bytes accessed | tf_op | source)
XLA Modules:
  0.0 124.2 jit_solution(17453311172798826037)
XLA Ops:
  0.6 2.2 %shard_map.59 = f32[4,64,768]{2,1,0:T(8,128)} custom-call(s32[16]{0:T(128)} %structure.5, f32[192,768]{1,0:T(8,128)} %root.1), custom_call_target="tpu_custom_call" | custom-call | tf_op jit(solution)/shard_map/pallas_call | solution.py:103
  2.8 8.9 %all-to-all-start = ((f32[32,8,768]{2,1,0:T(8,128)}), f32[32,8,768]{2,1,0:T(8,128)S(1)}, u32[]{:S(2)}, u32[]{:S(2)}) async-start(f32[32,8,768]{2,1,0:T(8,128)} %bitcast.67), calls=%async_computation | async-start | bytes 1572864 | tf_op jit(solution)/shard_map/all_to_all | solution.py:122
  11.8 5.5 %collective-permute-start = (f32[64,512]{1,0:T(8,128)S(1)}, f32[64,512]{1,0:T(8,128)S(1)}, u32[]{:S(2)}, u32[]{:S(2)}) collective-permute-start(f32[64,512]{1,0:T(8,128)S(1)} %copy-done.2), channel_id=1, source_target_pairs={{0,0},{1,32},{2,64},{3,96},{4,128},{5,160},{6,192},{7,224},{8,8},{... | collective-permute-start | bytes 393224 | tf_op jit(solution)/shard_map/ppermute | solution.py:95
  17.5 6.1 %collective-permute-start.3 = (f32[64,512]{1,0:T(8,128)S(1)}, f32[64,512]{1,0:T(8,128)S(1)}, u32[]{:S(2)}, u32[]{:S(2)}) collective-permute-start(f32[64,512]{1,0:T(8,128)S(1)} %copy-done.2), channel_id=1, source_target_pairs={{0,2},{1,34},{2,66},{3,98},{4,130},{5,162},{6,194},{7,226},{8,10},... | collective-permute-start | bytes 393224 | tf_op jit(solution)/shard_map/ppermute | solution.py:95
  23.6 6.2 %collective-permute-done = f32[64,512]{1,0:T(8,128)S(1)} collective-permute-done((f32[64,512]{1,0:T(8,128)S(1)}, f32[64,512]{1,0:T(8,128)S(1)}, u32[]{:S(2)}, u32[]{:S(2)}) %collective-permute-start) | collective-permute-done | bytes 131104 | tf_op jit(solution)/shard_map/ppermute | solution.py:95
  29.8 1.4 %collective-permute-done.3 = f32[64,512]{1,0:T(8,128)S(1)} collective-permute-done((f32[64,512]{1,0:T(8,128)S(1)}, f32[64,512]{1,0:T(8,128)S(1)}, u32[]{:S(2)}, u32[]{:S(2)}) %collective-permute-start.3) | collective-permute-done | bytes 131104 | tf_op jit(solution)/shard_map/ppermute | solution.py:95
  31.2 1.1 fusion.17
  32.3 2.7 %collective-permute-start.8 = (f32[4,64,512]{2,1,0:T(8,128)}, f32[4,64,512]{2,1,0:T(8,128)}, u32[]{:S(2)}, u32[]{:S(2)}) collective-permute-start(f32[4,64,512]{2,1,0:T(8,128)} %get-tuple-element.38), channel_id=1, source_target_pairs={{0,24},{8,0},{16,8},{24,16},{1,25},{9,1},{17,9},{25,17},{2,26},{10... | collective-permute-start | bytes 1572872 | tf_op jit(solution)/shard_map/ppermute | solution.py:85
  35.0 0.8 collective-permute-start.9
  35.8 0.9 collective-permute-start.10
  36.7 1.9 %shard_map.60 = (f32[2,8,768]{2,1,0:T(8,128)}, f32[2,8,768]{2,1,0:T(8,128)}, f32[2,8,768]{2,1,0:T(8,128)}, f32[2,8,768]{2,1,0:T(8,128)}) custom-call(s32[16]{0:T(128)} %structure.5, f32[32,8,768]{2,1,0:T(8,128)} %copy-done), custom_call_target="tpu_custom_call" | custom-call | tf_op jit(solution)/shard_map/pallas_call | solution.py:103
  38.6 7.1 %collective-permute-start.6 = (f32[2,8,768]{2,1,0:T(8,128)}, f32[2,8,768]{2,1,0:T(8,128)S(1)}, u32[]{:S(2)}, u32[]{:S(2)}) collective-permute-start(f32[2,8,768]{2,1,0:T(8,128)} %get-tuple-element.21), channel_id=1, source_target_pairs={{0,6},{2,0},{4,2},{6,4},{1,7},{3,1},{5,3},{7,5},{8,14},{10,8},{12,... | collective-permute-start | bytes 147464 | tf_op jit(solution)/shard_map/ppermute | solution.py:85
  45.7 0.7 constant_dynamic-slice_fusion.3
  46.4 1.3 %collective-permute-done.6.three = f32[2,8,768]{2,1,0:T(8,128)S(1)} collective-permute-done((f32[2,8,768]{2,1,0:T(8,128)}, f32[2,8,768]{2,1,0:T(8,128)S(1)}, u32[]{:S(2)}, u32[]{:S(2)}) %collective-permute-start.6) | collective-permute-done | bytes 49184 | tf_op jit(solution)/shard_map/ppermute | solution.py:85
  47.7 2.3 %collective-permute-start.4 = (f32[2,8,768]{2,1,0:T(8,128)}, f32[2,8,768]{2,1,0:T(8,128)S(1)}, u32[]{:S(2)}, u32[]{:S(2)}) collective-permute-start(f32[2,8,768]{2,1,0:T(8,128)} %get-tuple-element.19), channel_id=1, source_target_pairs={{0,2},{2,4},{4,6},{6,0},{1,3},{3,5},{5,7},{7,1},{8,10},{10,12},{12... | collective-permute-start | bytes 147464 | tf_op jit(solution)/shard_map/ppermute | solution.py:85
  50.0 5.8 %collective-permute-done.5.two = f32[2,8,768]{2,1,0:T(8,128)S(1)} collective-permute-done((f32[2,8,768]{2,1,0:T(8,128)}, f32[2,8,768]{2,1,0:T(8,128)S(1)}, u32[]{:S(2)}, u32[]{:S(2)}) %collective-permute-start.5) | collective-permute-done | bytes 49184 | tf_op jit(solution)/shard_map/ppermute | solution.py:85
  56.0 1.3 %collective-permute-done.7.got = f32[4,8,768]{2,1,0:T(8,128)S(1)} collective-permute-done((f32[4,8,768]{2,1,0:T(8,128)S(1)}, f32[4,8,768]{2,1,0:T(8,128)S(1)}, u32[]{:S(2)}, u32[]{:S(2)}) %collective-permute-start.7) | collective-permute-done | bytes 98336 | tf_op jit(solution)/shard_map/ppermute | solution.py:128
  57.3 0.6 copy-done.6
  57.9 2.2 %shard_map.61 = f32[8,8,2048]{2,1,0:T(8,128)} custom-call(s32[16]{0:T(128)} %structure.5, f32[2,8,768]{2,1,0:T(8,128)} %get-tuple-element.18.own, f32[2,8,768]{2,1,0:T(8,128)} %copy-done.5, f32[2,8,768]{2,1,0:T(8,128)} %copy-done.4, f32[2,8,768]{2,1,0:T(8,128)} %copy-done.3, f32[4,8,768]{2,1,0:T(8,128)} %copy-done.6), custom_call_target="tpu_custom_call" | custom-call | tf_op jit(solution)/shard_map/pallas_call | solution.py:103
  60.1 5.7 %all-to-all-start.1 = ((f32[8,8,2048]{2,1,0:T(8,128)}), f32[8,8,2048]{2,1,0:T(8,128)S(1)}, u32[]{:S(2)}, u32[]{:S(2)}) async-start(f32[8,8,2048]{2,1,0:T(8,128)} %shard_map.61), calls=%async_computation.1 | async-start | bytes 1048576 | tf_op jit(solution)/shard_map/all_to_all | solution.py:132
  65.9 0.5 collective-permute-start.12
  66.5 0.4 collective-permute-start.14
  66.9 1.7 %collective-permute-start.15 = (f32[64,512]{1,0:T(8,128)S(1)}, f32[64,512]{1,0:T(8,128)S(1)}, u32[]{:S(2)}, u32[]{:S(2)}) collective-permute-start(f32[64,512]{1,0:T(8,128)S(1)} %copy-done.2), channel_id=1, source_target_pairs={{0,32},{32,0},{1,33},{33,1},{2,34},{34,2},{3,35},{35,3},{4,36},{36... | collective-permute-start | bytes 393224 | tf_op jit(solution)/shard_map/ppermute | solution.py:130
  68.6 1.6 %pad_maximum_fusion = f32[4,4,64,512]{3,2,1,0:T(8,128)S(1)} fusion(f32[4,1,64,512]{3,2,1,0:T(8,128)} %bitcast.12, f32[4,1,64,512]{3,2,1,0:T(8,128)} %bitcast.11, f32[4,1,64,512]{3,2,1,0:T(8,128)} %bitcast.9, f32[4,1,64,512]{3,2,1,0:T(8,128)S(1)} %get-tuple-element.37), kind=kLoop, calls=%fused_computation.1 | loop fusion | flops 1572864 | bytes 4194304 | tf_op jit(solution)/shard_map/stack | solution.py:137
  70.4 1.7 %pad_maximum_fusion.1 = f32[4,4,64,512]{3,2,0,1:T(8,128)S(1)} fusion(f32[4,1,64,512]{3,2,0,1:T(8,128)} %bitcast.17, f32[4,1,64,512]{3,2,0,1:T(8,128)} %bitcast.16, f32[4,1,64,512]{3,2,0,1:T(8,128)} %bitcast.15, f32[4,1,64,512]{3,2,0,1:T(8,128)} %bitcast.14), kind=kLoop, calls=%fused_computation.2 | loop fusion | flops 1572864 | bytes 4194304 | tf_op jit(solution)/shard_map/stack | solution.py:138
  72.1 1.6 %copy.9 = f32[4,4,64,512]{3,2,1,0:T(8,128)} copy(f32[4,4,64,512]{3,2,0,1:T(8,128)S(1)} %pad_maximum_fusion.1) | data formatting | bytes 4194304 | tf_op jit(solution)/shard_map/stack | solution.py:138
  73.7 1.0 all-to-all-done.1
  74.7 2.3 %fusion = f32[64,512]{1,0:T(8,128)S(1)} fusion(f32[1024,512]{1,0:T(8,128)} %bitcast.64, f32[64,2048]{1,0:T(8,128)S(1)} %bitcast.68), kind=kOutput, calls=%fused_computation.8 | convolution fusion | flops 201326592 | bytes 2490368 | tf_op jit(solution)/shard_map/dot_general | solution.py:67
  77.0 0.8 fusion.7
  77.8 0.6 collective-permute-start.16
  78.5 0.6 collective-permute-start.19
  79.1 3.0 %collective-permute-start.20 = (f32[2,64,512]{2,1,0:T(8,128)S(1)}, f32[2,64,512]{2,1,0:T(8,128)S(1)}, u32[]{:S(2)}, u32[]{:S(2)}) collective-permute-start(f32[2,64,512]{2,1,0:T(8,128)S(1)} %get-tuple-element.40), channel_id=1, source_target_pairs={{0,128},{64,192},{128,0},{192,64},{1,129},{65,193},{129,1},{193,65... | collective-permute-start | bytes 786440 | tf_op jit(solution)/shard_map/ppermute | solution.py:85
  82.1 1.8 %collective-permute-start.21 = (f32[2,64,512]{2,1,0:T(8,128)S(1)}, f32[2,64,512]{2,1,0:T(8,128)S(1)}, u32[]{:S(2)}, u32[]{:S(2)}) collective-permute-start(f32[2,64,512]{2,1,0:T(8,128)S(1)} %get-tuple-element.40), channel_id=1, source_target_pairs={{0,64},{64,128},{128,192},{192,0},{1,65},{65,129},{129,193},{193,1... | collective-permute-start | bytes 786440 | tf_op jit(solution)/shard_map/ppermute | solution.py:85
  83.9 2.7 %collective-permute-start.17 = (f32[64,512]{1,0:T(8,128)S(1)}, f32[64,512]{1,0:T(8,128)S(1)}, u32[]{:S(2)}, u32[]{:S(2)}) collective-permute-start(f32[64,512]{1,0:T(8,128)S(1)} %fusion.7), channel_id=1, source_target_pairs={{0,4},{2,6},{4,0},{6,2},{1,5},{3,7},{5,1},{7,3},{8,12},{10,14},{12... | collective-permute-start | bytes 393224 | tf_op jit(solution)/shard_map/ppermute | solution.py:85
  86.6 0.7 collective-permute-done.16
  87.3 2.2 %collective-permute-start.18 = (f32[64,512]{1,0:T(8,128)S(1)}, f32[64,512]{1,0:T(8,128)S(1)}, u32[]{:S(2)}, u32[]{:S(2)}) collective-permute-start(f32[64,512]{1,0:T(8,128)S(1)} %fusion.7), channel_id=1, source_target_pairs={{0,2},{2,4},{4,6},{6,0},{1,3},{3,5},{5,7},{7,1},{8,10},{10,12},{12... | collective-permute-start | bytes 393224 | tf_op jit(solution)/shard_map/ppermute | solution.py:85
  89.6 7.5 %collective-permute-done.17 = f32[64,512]{1,0:T(8,128)S(1)} collective-permute-done((f32[64,512]{1,0:T(8,128)S(1)}, f32[64,512]{1,0:T(8,128)S(1)}, u32[]{:S(2)}, u32[]{:S(2)}) %collective-permute-start.17) | collective-permute-done | bytes 131104 | tf_op jit(solution)/shard_map/ppermute | solution.py:85
  97.3 0.6 gather_fusion
  98.3 0.8 collective-permute-done.22
  99.1 0.6 fusion.19
  99.7 0.6 convolution_add_fusion
  100.5 2.5 %collective-permute-start.24 = (f32[128,512]{1,0:T(8,128)S(1)}, f32[128,512]{1,0:T(8,128)S(1)}, u32[]{:S(2)}, u32[]{:S(2)}) collective-permute-start(f32[128,512]{1,0:T(8,128)S(1)} %get-tuple-element.32), channel_id=1, source_target_pairs={{0,8},{8,16},{16,24},{24,0},{1,9},{9,17},{17,25},{25,1},{2,10},{10... | collective-permute-start | bytes 786440 | tf_op jit(solution)/shard_map/ppermute | solution.py:85
  103.0 2.3 %collective-permute-start.25 = (f32[128,512]{1,0:T(8,128)S(1)}, f32[128,512]{1,0:T(8,128)S(1)}, u32[]{:S(2)}, u32[]{:S(2)}) collective-permute-start(f32[128,512]{1,0:T(8,128)S(1)} %get-tuple-element.34), channel_id=1, source_target_pairs={{0,16},{8,24},{16,0},{24,8},{1,17},{9,25},{17,1},{25,9},{2,18},{10... | collective-permute-start | bytes 786440 | tf_op jit(solution)/shard_map/ppermute | solution.py:85
  105.2 0.7 collective-permute-start.26
  105.9 2.6 %collective-permute-start.23 = (f32[64,512]{1,0:T(8,128)S(1)}, f32[64,512]{1,0:T(8,128)S(1)}, u32[]{:S(2)}, u32[]{:S(2)}) collective-permute-start(f32[64,512]{1,0:T(8,128)S(1)} %fusion.7), channel_id=1, source_target_pairs={{0,0},{1,32},{2,64},{3,96},{4,128},{5,160},{6,192},{7,224},{8,8},{... | collective-permute-start | bytes 393224 | tf_op jit(solution)/shard_map/ppermute | solution.py:95
  108.5 14.2 %collective-permute-done.23 = f32[64,512]{1,0:T(8,128)S(1)} collective-permute-done((f32[64,512]{1,0:T(8,128)S(1)}, f32[64,512]{1,0:T(8,128)S(1)}, u32[]{:S(2)}, u32[]{:S(2)}) %collective-permute-start.23) | collective-permute-done | bytes 131104 | tf_op jit(solution)/shard_map/ppermute | solution.py:95
  122.7 0.8 fusion.12
  123.5 0.7 copy.11
  (53 shorter events, 1.3 us)
Async XLA Ops:
  0.6 11.1 %copy-start.2 = (f32[64,512]{1,0:T(8,128)S(1)}, f32[64,512]{1,0:T(8,128)}, u32[]{:S(2)}) copy-start(f32[64,512]{1,0:T(8,128)} %param.6) | copy-start | bytes 393220
  2.8 28.4 %all-to-all-start = ((f32[32,8,768]{2,1,0:T(8,128)}), f32[32,8,768]{2,1,0:T(8,128)S(1)}, u32[]{:S(2)}, u32[]{:S(2)}) async-start(f32[32,8,768]{2,1,0:T(8,128)} %bitcast.67), calls=%async_computation | async-start | bytes 1572864 | tf_op jit(solution)/shard_map/all_to_all | solution.py:122
  11.8 18.0 %collective-permute-start = (f32[64,512]{1,0:T(8,128)S(1)}, f32[64,512]{1,0:T(8,128)S(1)}, u32[]{:S(2)}, u32[]{:S(2)}) collective-permute-start(f32[64,512]{1,0:T(8,128)S(1)} %copy-done.2), channel_id=1, source_target_pairs={{0,0},{1,32},{2,64},{3,96},{4,128},{5,160},{6,192},{7,224},{8,8},{... | collective-permute-start | bytes 393224 | tf_op jit(solution)/shard_map/ppermute | solution.py:95
  17.3 12.5 %collective-permute-start.1 = (f32[64,512]{1,0:T(8,128)S(1)}, f32[64,512]{1,0:T(8,128)S(1)}, u32[]{:S(2)}, u32[]{:S(2)}) collective-permute-start(f32[64,512]{1,0:T(8,128)S(1)} %copy-done.2), channel_id=1, source_target_pairs={{0,6},{1,38},{2,70},{3,102},{4,134},{5,166},{6,198},{7,230},{8,14}... | collective-permute-start | bytes 393224 | tf_op jit(solution)/shard_map/ppermute | solution.py:95
  17.4 12.4 %collective-permute-start.2 = (f32[64,512]{1,0:T(8,128)S(1)}, f32[64,512]{1,0:T(8,128)S(1)}, u32[]{:S(2)}, u32[]{:S(2)}) collective-permute-start(f32[64,512]{1,0:T(8,128)S(1)} %copy-done.2), channel_id=1, source_target_pairs={{0,4},{1,36},{2,68},{3,100},{4,132},{5,164},{6,196},{7,228},{8,12}... | collective-permute-start | bytes 393224 | tf_op jit(solution)/shard_map/ppermute | solution.py:95
  17.5 13.7 %collective-permute-start.3 = (f32[64,512]{1,0:T(8,128)S(1)}, f32[64,512]{1,0:T(8,128)S(1)}, u32[]{:S(2)}, u32[]{:S(2)}) collective-permute-start(f32[64,512]{1,0:T(8,128)S(1)} %copy-done.2), channel_id=1, source_target_pairs={{0,2},{1,34},{2,66},{3,98},{4,130},{5,162},{6,194},{7,226},{8,10},... | collective-permute-start | bytes 393224 | tf_op jit(solution)/shard_map/ppermute | solution.py:95
  31.2 5.5 %copy-start = (f32[32,8,768]{2,1,0:T(8,128)}, f32[32,8,768]{2,1,0:T(8,128)S(1)}, u32[]{:S(2)}) copy-start(f32[32,8,768]{2,1,0:T(8,128)S(1)} %all-to-all-done.pieces) | copy-start | bytes 2359300
  32.3 33.6 %collective-permute-start.8 = (f32[4,64,512]{2,1,0:T(8,128)}, f32[4,64,512]{2,1,0:T(8,128)}, u32[]{:S(2)}, u32[]{:S(2)}) collective-permute-start(f32[4,64,512]{2,1,0:T(8,128)} %get-tuple-element.38), channel_id=1, source_target_pairs={{0,24},{8,0},{16,8},{24,16},{1,25},{9,1},{17,9},{25,17},{2,26},{10... | collective-permute-start | bytes 1572872 | tf_op jit(solution)/shard_map/ppermute | solution.py:85
  35.0 31.4 %collective-permute-start.9 = (f32[4,64,512]{2,1,0:T(8,128)}, f32[4,64,512]{2,1,0:T(8,128)}, u32[]{:S(2)}, u32[]{:S(2)}) collective-permute-start(f32[4,64,512]{2,1,0:T(8,128)} %get-tuple-element.38), channel_id=1, source_target_pairs={{0,16},{8,24},{16,0},{24,8},{1,17},{9,25},{17,1},{25,9},{2,18},{10... | collective-permute-start | bytes 1572872 | tf_op jit(solution)/shard_map/ppermute | solution.py:85
  35.8 30.7 %collective-permute-start.10 = (f32[4,64,512]{2,1,0:T(8,128)}, f32[4,64,512]{2,1,0:T(8,128)}, u32[]{:S(2)}, u32[]{:S(2)}) collective-permute-start(f32[4,64,512]{2,1,0:T(8,128)} %get-tuple-element.38), channel_id=1, source_target_pairs={{0,8},{8,16},{16,24},{24,0},{1,9},{9,17},{17,25},{25,1},{2,10},{10... | collective-permute-start | bytes 1572872 | tf_op jit(solution)/shard_map/ppermute | solution.py:85
  38.6 9.1 %collective-permute-start.6 = (f32[2,8,768]{2,1,0:T(8,128)}, f32[2,8,768]{2,1,0:T(8,128)S(1)}, u32[]{:S(2)}, u32[]{:S(2)}) collective-permute-start(f32[2,8,768]{2,1,0:T(8,128)} %get-tuple-element.21), channel_id=1, source_target_pairs={{0,6},{2,0},{4,2},{6,4},{1,7},{3,1},{5,3},{7,5},{8,14},{10,8},{12,... | collective-permute-start | bytes 147464 | tf_op jit(solution)/shard_map/ppermute | solution.py:85
  45.7 10.1 %collective-permute-start.5 = (f32[2,8,768]{2,1,0:T(8,128)}, f32[2,8,768]{2,1,0:T(8,128)S(1)}, u32[]{:S(2)}, u32[]{:S(2)}) collective-permute-start(f32[2,8,768]{2,1,0:T(8,128)} %get-tuple-element.20), channel_id=1, source_target_pairs={{0,4},{2,6},{4,0},{6,2},{1,5},{3,7},{5,1},{7,3},{8,12},{10,14},{12... | collective-permute-start | bytes 147464 | tf_op jit(solution)/shard_map/ppermute | solution.py:85
  47.7 9.5 %copy-start.3 = (f32[2,8,768]{2,1,0:T(8,128)}, f32[2,8,768]{2,1,0:T(8,128)S(1)}, u32[]{:S(2)}) copy-start(f32[2,8,768]{2,1,0:T(8,128)S(1)} %collective-permute-done.6.three) | copy-start | bytes 147460
  47.7 8.1 %collective-permute-start.4 = (f32[2,8,768]{2,1,0:T(8,128)}, f32[2,8,768]{2,1,0:T(8,128)S(1)}, u32[]{:S(2)}, u32[]{:S(2)}) collective-permute-start(f32[2,8,768]{2,1,0:T(8,128)} %get-tuple-element.19), channel_id=1, source_target_pairs={{0,2},{2,4},{4,6},{6,0},{1,3},{3,5},{5,7},{7,1},{8,10},{10,12},{12... | collective-permute-start | bytes 147464 | tf_op jit(solution)/shard_map/ppermute | solution.py:85
  55.8 1.5 %copy-start.4 = (f32[2,8,768]{2,1,0:T(8,128)}, f32[2,8,768]{2,1,0:T(8,128)S(1)}, u32[]{:S(2)}) copy-start(f32[2,8,768]{2,1,0:T(8,128)S(1)} %collective-permute-done.5.two) | copy-start | bytes 147460
  55.8 1.4 %copy-start.5 = (f32[2,8,768]{2,1,0:T(8,128)}, f32[2,8,768]{2,1,0:T(8,128)S(1)}, u32[]{:S(2)}) copy-start(f32[2,8,768]{2,1,0:T(8,128)S(1)} %collective-permute-done.4.one) | copy-start | bytes 147460
  55.8 1.4 %collective-permute-start.7 = (f32[4,8,768]{2,1,0:T(8,128)S(1)}, f32[4,8,768]{2,1,0:T(8,128)S(1)}, u32[]{:S(2)}, u32[]{:S(2)}) collective-permute-start(f32[4,8,768]{2,1,0:T(8,128)S(1)} %pad_maximum_fusion.6), channel_id=1, source_target_pairs={{0,1},{1,0},{2,3},{3,2},{4,5},{5,4},{6,7},{7,6},{8,9},{9,8},{10,11... | collective-permute-start | bytes 294920 | tf_op jit(solution)/shard_map/ppermute | solution.py:128
  57.2 0.6 copy-start.6
  60.1 14.5 %all-to-all-start.1 = ((f32[8,8,2048]{2,1,0:T(8,128)}), f32[8,8,2048]{2,1,0:T(8,128)S(1)}, u32[]{:S(2)}, u32[]{:S(2)}) async-start(f32[8,8,2048]{2,1,0:T(8,128)} %shard_map.61), calls=%async_computation.1 | async-start | bytes 1048576 | tf_op jit(solution)/shard_map/all_to_all | solution.py:132
  65.9 4.4 %collective-permute-start.11 = (f32[4,64,512]{2,1,0:T(8,128)}, f32[4,64,512]{2,1,0:T(8,128)}, u32[]{:S(2)}, u32[]{:S(2)}) collective-permute-start(f32[4,64,512]{2,1,0:T(8,128)} %get-tuple-element.38), channel_id=1, source_target_pairs={{0,1},{1,0},{2,3},{3,2},{4,5},{5,4},{6,7},{7,6},{8,9},{9,8},{10,11... | collective-permute-start | bytes 1572872 | tf_op jit(solution)/shard_map/ppermute | solution.py:136
  65.9 4.4 %collective-permute-start.12 = (f32[4,64,512]{2,1,0:T(8,128)}, f32[4,64,512]{2,1,0:T(8,128)}, u32[]{:S(2)}, u32[]{:S(2)}) collective-permute-start(f32[4,64,512]{2,1,0:T(8,128)} %collective-permute-done.8), channel_id=1, source_target_pairs={{0,1},{1,0},{2,3},{3,2},{4,5},{5,4},{6,7},{7,6},{8,9},{9,8},{10,11... | collective-permute-start | bytes 1572872 | tf_op jit(solution)/shard_map/ppermute | solution.py:136
  66.4 3.9 %collective-permute-start.13 = (f32[4,64,512]{2,1,0:T(8,128)}, f32[4,64,512]{2,1,0:T(8,128)}, u32[]{:S(2)}, u32[]{:S(2)}) collective-permute-start(f32[4,64,512]{2,1,0:T(8,128)} %collective-permute-done.9), channel_id=1, source_target_pairs={{0,1},{1,0},{2,3},{3,2},{4,5},{5,4},{6,7},{7,6},{8,9},{9,8},{10,11... | collective-permute-start | bytes 1572872 | tf_op jit(solution)/shard_map/ppermute | solution.py:136
  66.5 3.9 %collective-permute-start.14 = (f32[4,64,512]{2,1,0:T(8,128)}, f32[4,64,512]{2,1,0:T(8,128)}, u32[]{:S(2)}, u32[]{:S(2)}) collective-permute-start(f32[4,64,512]{2,1,0:T(8,128)} %collective-permute-done.10), channel_id=1, source_target_pairs={{0,1},{1,0},{2,3},{3,2},{4,5},{5,4},{6,7},{7,6},{8,9},{9,8},{10,11... | collective-permute-start | bytes 1572872 | tf_op jit(solution)/shard_map/ppermute | solution.py:136
  66.9 10.8 %collective-permute-start.15 = (f32[64,512]{1,0:T(8,128)S(1)}, f32[64,512]{1,0:T(8,128)S(1)}, u32[]{:S(2)}, u32[]{:S(2)}) collective-permute-start(f32[64,512]{1,0:T(8,128)S(1)} %copy-done.2), channel_id=1, source_target_pairs={{0,32},{32,0},{1,33},{33,1},{2,34},{34,2},{3,35},{35,3},{4,36},{36... | collective-permute-start | bytes 393224 | tf_op jit(solution)/shard_map/ppermute | solution.py:130
  77.8 9.6 %collective-permute-start.16 = (f32[64,512]{1,0:T(8,128)S(1)}, f32[64,512]{1,0:T(8,128)S(1)}, u32[]{:S(2)}, u32[]{:S(2)}) collective-permute-start(f32[64,512]{1,0:T(8,128)S(1)} %fusion.7), channel_id=1, source_target_pairs={{0,6},{2,0},{4,2},{6,4},{1,7},{3,1},{5,3},{7,5},{8,14},{10,8},{12,... | collective-permute-start | bytes 393224 | tf_op jit(solution)/shard_map/ppermute | solution.py:85
  78.5 18.7 %collective-permute-start.19 = (f32[2,64,512]{2,1,0:T(8,128)S(1)}, f32[2,64,512]{2,1,0:T(8,128)S(1)}, u32[]{:S(2)}, u32[]{:S(2)}) collective-permute-start(f32[2,64,512]{2,1,0:T(8,128)S(1)} %get-tuple-element.40), channel_id=1, source_target_pairs={{0,192},{64,0},{128,64},{192,128},{1,193},{65,1},{129,65},{193,129... | collective-permute-start | bytes 786440 | tf_op jit(solution)/shard_map/ppermute | solution.py:85
  79.1 18.1 %collective-permute-start.20 = (f32[2,64,512]{2,1,0:T(8,128)S(1)}, f32[2,64,512]{2,1,0:T(8,128)S(1)}, u32[]{:S(2)}, u32[]{:S(2)}) collective-permute-start(f32[2,64,512]{2,1,0:T(8,128)S(1)} %get-tuple-element.40), channel_id=1, source_target_pairs={{0,128},{64,192},{128,0},{192,64},{1,129},{65,193},{129,1},{193,65... | collective-permute-start | bytes 786440 | tf_op jit(solution)/shard_map/ppermute | solution.py:85
  82.1 15.1 %collective-permute-start.21 = (f32[2,64,512]{2,1,0:T(8,128)S(1)}, f32[2,64,512]{2,1,0:T(8,128)S(1)}, u32[]{:S(2)}, u32[]{:S(2)}) collective-permute-start(f32[2,64,512]{2,1,0:T(8,128)S(1)} %get-tuple-element.40), channel_id=1, source_target_pairs={{0,64},{64,128},{128,192},{192,0},{1,65},{65,129},{129,193},{193,1... | collective-permute-start | bytes 786440 | tf_op jit(solution)/shard_map/ppermute | solution.py:85
  83.9 13.2 %collective-permute-start.17 = (f32[64,512]{1,0:T(8,128)S(1)}, f32[64,512]{1,0:T(8,128)S(1)}, u32[]{:S(2)}, u32[]{:S(2)}) collective-permute-start(f32[64,512]{1,0:T(8,128)S(1)} %fusion.7), channel_id=1, source_target_pairs={{0,4},{2,6},{4,0},{6,2},{1,5},{3,7},{5,1},{7,3},{8,12},{10,14},{12... | collective-permute-start | bytes 393224 | tf_op jit(solution)/shard_map/ppermute | solution.py:85
  87.3 9.7 %collective-permute-start.18 = (f32[64,512]{1,0:T(8,128)S(1)}, f32[64,512]{1,0:T(8,128)S(1)}, u32[]{:S(2)}, u32[]{:S(2)}) collective-permute-start(f32[64,512]{1,0:T(8,128)S(1)} %fusion.7), channel_id=1, source_target_pairs={{0,2},{2,4},{4,6},{6,0},{1,3},{3,5},{5,7},{7,1},{8,10},{10,12},{12... | collective-permute-start | bytes 393224 | tf_op jit(solution)/shard_map/ppermute | solution.py:85
  97.1 2.0 %collective-permute-start.22 = (f32[4,64,512]{2,1,0:T(8,128)S(1)}, f32[4,64,512]{2,1,0:T(8,128)S(1)}, u32[]{:S(2)}, u32[]{:S(2)}) collective-permute-start(f32[4,64,512]{2,1,0:T(8,128)S(1)} %pad_maximum_fusion.4), channel_id=1, source_target_pairs={{0,1},{1,0},{2,3},{3,2},{4,5},{5,4},{6,7},{7,6},{8,9},{9,8},{10,11... | collective-permute-start | bytes 1572872 | tf_op jit(solution)/shard_map/ppermute | solution.py:144
  99.7 23.0 %copy-start.1 = (f32[128,512]{1,0:T(8,128)S(1)}, f32[128,512]{1,0:T(8,128)}, u32[]{:S(2)}) copy-start(f32[128,512]{1,0:T(8,128)} %param.7) | copy-start | bytes 786436
  100.5 22.3 %collective-permute-start.24 = (f32[128,512]{1,0:T(8,128)S(1)}, f32[128,512]{1,0:T(8,128)S(1)}, u32[]{:S(2)}, u32[]{:S(2)}) collective-permute-start(f32[128,512]{1,0:T(8,128)S(1)} %get-tuple-element.32), channel_id=1, source_target_pairs={{0,8},{8,16},{16,24},{24,0},{1,9},{9,17},{17,25},{25,1},{2,10},{10... | collective-permute-start | bytes 786440 | tf_op jit(solution)/shard_map/ppermute | solution.py:85
  103.0 19.8 %collective-permute-start.25 = (f32[128,512]{1,0:T(8,128)S(1)}, f32[128,512]{1,0:T(8,128)S(1)}, u32[]{:S(2)}, u32[]{:S(2)}) collective-permute-start(f32[128,512]{1,0:T(8,128)S(1)} %get-tuple-element.34), channel_id=1, source_target_pairs={{0,16},{8,24},{16,0},{24,8},{1,17},{9,25},{17,1},{25,9},{2,18},{10... | collective-permute-start | bytes 786440 | tf_op jit(solution)/shard_map/ppermute | solution.py:85
  105.2 17.5 %collective-permute-start.26 = (f32[128,512]{1,0:T(8,128)S(1)}, f32[128,512]{1,0:T(8,128)S(1)}, u32[]{:S(2)}, u32[]{:S(2)}) collective-permute-start(f32[128,512]{1,0:T(8,128)S(1)} %get-tuple-element.33), channel_id=1, source_target_pairs={{0,24},{8,0},{16,8},{24,16},{1,25},{9,1},{17,9},{25,17},{2,26},{10... | collective-permute-start | bytes 786440 | tf_op jit(solution)/shard_map/ppermute | solution.py:85
  105.9 16.8 %collective-permute-start.23 = (f32[64,512]{1,0:T(8,128)S(1)}, f32[64,512]{1,0:T(8,128)S(1)}, u32[]{:S(2)}, u32[]{:S(2)}) collective-permute-start(f32[64,512]{1,0:T(8,128)S(1)} %fusion.7), channel_id=1, source_target_pairs={{0,0},{1,32},{2,64},{3,96},{4,128},{5,160},{6,192},{7,224},{8,8},{... | collective-permute-start | bytes 393224 | tf_op jit(solution)/shard_map/ppermute | solution.py:95
